TPU v7x, 32 devices: a whole 2x2x4 slice. The times are simulated.
32 devices in a mesh: row: 8 (over y, x, core), col: 4 (over z).
Axes of the slice: x: 2, y: 2, z: 4, core: 2. Of those that a mesh axis runs over, the one named last changes fastest.
Arguments:
- tokens: bfloat16 [256, 2880], P('row', 'col'), may hold values from -6 to 6
- route_ids: int32 [256, 4], P('row'), may hold values from 0 to 15, all different within a row; in each aligned block of 32 rows (0 to 31, 32 to 63, ...) at most 8 rows name the same one
- route_weights: float32 [256, 4], P('row'), may hold values from 0.1 to 1
- expert_gate_up: bfloat16 [16, 2880, 2, 2880], P('row', None, None, 'col'), may hold values from -0.109375 to 0.109375
- expert_down: bfloat16 [16, 2880, 2880], P('row', 'col'), may hold values from -0.15625 to 0.15625
Outputs:
- moe_out: bfloat16 [256, 2880], P('row', 'col')
Inputs may be any that keep to these rules, and one draw needn't show every extreme that they name: `route_ids`: each token names 4 different experts. Among the 32 tokens of one index of row, no expert is named more than 8 times, a bound that some block reaches.
All inputs are finite; a program needn't handle non-finite values.
Results may differ from a plain program's by a relative error of at most 0.0049.
Values may be sent and summed in bfloat16 or wider, within the bound.
No kernel may reach another device: no remote copies, remote signals or barrier semaphores. Data moves between devices by JAX's collectives and lax.ppermute only.
A program may use at most 256 MiB of HBM per device.

v0:
```python
import jax
import jax.numpy as jnp
from jax import lax
from jax.sharding import PartitionSpec as P

TOP = 4
CAP = 8


def activate(act, width):
    gate = act[..., :width]
    up = act[..., width:]
    return ((up + 1.0) * gate * jax.nn.sigmoid(1.702 * gate)).astype(jnp.bfloat16)


def on_device(tokens, route_ids, route_weights, expert_gate_up, expert_down):
    nrow = lax.axis_size("row")
    tok_count = tokens.shape[0]
    exp_dev = expert_gate_up.shape[0]
    model_width = expert_gate_up.shape[1]
    hid_width = expert_gate_up.shape[3]
    experts = exp_dev * nrow
    chosen = route_ids.reshape(-1)
    onehot = (chosen[:, None] == jnp.arange(experts, dtype=jnp.int32)[None, :]).astype(jnp.int32)
    before = jnp.cumsum(onehot, axis=0) - onehot
    slot = jnp.sum(before * onehot, axis=1)
    target = chosen * CAP + slot
    place = (target[:, None] == jnp.arange(experts * CAP, dtype=jnp.int32)[None, :]).astype(
        jnp.float32
    )
    place = place.reshape(tok_count, TOP, experts * CAP)
    place_tok = jnp.sum(place, axis=1).astype(jnp.bfloat16)
    combine = jnp.sum(place * route_weights[:, :, None], axis=1)
    weights_gu = expert_gate_up.reshape(exp_dev, model_width, 2 * hid_width)
    whole = lax.all_gather(tokens, "col", axis=1, tiled=True)
    sending = jnp.dot(place_tok.T, whole, preferred_element_type=jnp.float32).astype(jnp.bfloat16)
    sending = sending.reshape(nrow, exp_dev, CAP, model_width)
    arrived = lax.all_to_all(sending, "row", split_axis=0, concat_axis=0, tiled=True)
    act = jnp.einsum("secd,edf->secf", arrived, weights_gu, preferred_element_type=jnp.float32)
    hidden = activate(act, hid_width)
    partial_out = jnp.einsum(
        "secf,efd->secd", hidden, expert_down, preferred_element_type=jnp.float32
    )
    returned = lax.all_to_all(partial_out, "row", split_axis=0, concat_axis=0, tiled=True)
    flat = returned.reshape(experts * CAP, model_width)
    weighted = jnp.dot(
        combine, flat, precision=lax.Precision.HIGHEST, preferred_element_type=jnp.float32
    )
    mixed = lax.psum_scatter(weighted, "col", scatter_dimension=1, tiled=True)
    return mixed.astype(jnp.bfloat16)


def solution(mesh):
    return jax.shard_map(
        on_device,
        mesh=mesh,
        in_specs=(
            P("row", "col"),
            P("row", None),
            P("row", None),
            P("row", None, None, "col"),
            P("row", "col", None),
        ),
        out_specs=P("row", "col"),
        check_vma=False,
    )
```

profile of v0, /device:TPU:0, one launch (start us, length us, event | category | flops | bytes accessed | tf_op | source)
XLA Modules:
  0.0 124.1 jit_solution(13134663760587441074)
XLA Ops:
  6.5 0.0 reduce-scatter.4.cloned.1.call-start
  6.5 0.8 copy.35
  7.3 0.1 eq.29
  7.4 0.1 fusion.12
  7.5 0.2 reduce_window_sum.11
  7.7 0.2 select_reduce_fusion.1
  7.8 0.1 reduce_sum.30
  8.0 0.1 copy.36
  8.0 0.7 multiply_add_fusion
  8.7 15.7 %all-gather = bf16[4,720,32]{1,2,0:T(8,128)(2,1)S(1)} all-gather(bf16[1,720,32]{1,2,0:T(8,128)(2,1)} %bitcast.35), channel_id=1, replica_groups=mesh['row'=8,'col'=4] {'col'}, dimensions={0}, use_global_device_ids=true | all-gather | bytes 230400 | tf_op jit(solution)/shard_map/all_gather | solution.py:35
  24.4 0.2 copy.37
  24.6 0.2 reshape.33
  24.8 0.8 convert_reduce_fusion
  25.5 0.4 convolution_convert_fusion
  26.0 0.3 copy.38
  26.3 15.7 %all_to_all.10 = bf16[8,2,8,2880]{3,2,1,0:T(8,128)(2,1)S(1)} all-to-all(bf16[8,2,8,2880]{3,2,1,0:T(8,128)(2,1)S(1)} %bitcast.33), channel_id=1, replica_groups=mesh['row'=8,'col'=4] {'row'}, dimensions={0} | all-to-all | bytes 1474560 | tf_op jit(solution)/shard_map/all_to_all | solution.py:38
  42.0 8.6 %convolution_bitcast_fusion.1 = f32[8,2,8,1440]{3,2,0,1:T(8,128)S(1)} fusion(bf16[2,2880,1440,1]{1,2,3,0:T(8,128)(2,1)} %bitcast.31, bf16[8,2,8,2880]{3,2,1,0:T(8,128)(2,1)S(1)} %all_to_all.10), kind=kOutput, calls=%fused_computation.5 | convolution fusion | flops 1061683200 | bytes 18063360 | tf_op jit(solution)/shard_map/secd,edf->secf/dot_general | solution.py:39
  50.6 5.0 %fusion.2 = f32[8,2,8,2880]{3,2,0,1:T(8,128)S(1)} fusion(bf16[2,720,2880]{2,1,0:T(8,128)(2,1)} %param.9, f32[8,2,8,1440]{3,2,0,1:T(8,128)S(1)} %convolution_bitcast_fusion.1), kind=kOutput, calls=%fused_computation.2 | convolution fusion | flops 531578880 | bytes 10506240 | tf_op jit(solution)/shard_map/secf,efd->secd/dot_general | solution.py:41
  55.6 0.1 copy.40
  55.7 22.7 %all_to_all.11 = f32[8,2,8,2880]{3,2,1,0:T(8,128)S(1)} all-to-all(f32[8,2,8,2880]{3,2,1,0:T(8,128)S(1)} %copy.40), channel_id=1, replica_groups=mesh['row'=8,'col'=4] {'row'}, dimensions={0} | all-to-all | bytes 2949120 | tf_op jit(solution)/shard_map/all_to_all | solution.py:44
  78.4 3.6 %convolution_bitcast_fusion = f32[2880,32]{1,0:T(8,128)} fusion(f32[32,128]{1,0:T(8,128)S(1)} %get-tuple-element.6, f32[128,2880]{1,0:T(8,128)S(1)} %bitcast.32), kind=kOutput, calls=%fused_computation.3 | convolution fusion | flops 141557760 | bytes 1859584
  82.0 0.0 reduce-scatter.4.cloned.1.call-update
  82.1 33.5 %reduce-scatter.4.cloned.1.call-done = f32[720,32]{1,0:T(8,128)} async-done(((f32[2880,32]{1,0:T(8,128)}), f32[720,32]{1,0:T(8,128)}) %reduce-scatter.4.cloned.1.call-update) | async-done | bytes 92176
  115.5 1.7 %copy.44 = bf16[32,720]{1,0:T(8,128)(2,1)} copy(f32[32,720]{0,1:T(8,128)} %bitcast.34) | data formatting | bytes 138240
Async XLA Ops:
  6.5 109.0 %reduce-scatter.4.cloned.1.call-start = ((), (), s32[]{:S(2)}) async-start(), calls=%async_computation.3 | async-start | bytes 1843200
Sparse Core Ops, SparseCore 0:
  82.2 33.2 reduce-scatter.3
where the time goes:
time: 124 us
  blocking collectives  54 us (44%)
  waiting for transfers between devices  33.5 us (27%)
  matrix products  17.7 us (14%)
  between operations  13.5 us (11%)
  local copies, waits for them, and re-layouts  3.55 us (3%)
  other arithmetic  1.91 us (2%)
    unnamed x2, waiting for transfers between devices  33.5 us
    all_to_all x1, blocking collectives, on_device(): lax.all_to_all(partial_out, 'row', split_axis=0, concat_axis=0, tiled=True)  22.7 us
    all_to_all x1, blocking collectives, on_device(): lax.all_to_all(sending, 'row', split_axis=0, concat_axis=0, tiled=True)  15.7 us
    all_gather x1, blocking collectives, on_device(): whole = lax.all_gather(tokens, 'col', axis=1, tiled=True)  15.7 us
    dot_general x1, matrix products, on_device(): jnp.einsum('secd,edf->secf', arrived, weights_gu, preferred_element_type=...  8.58 us
    dot_general x1, matrix products, on_device(): jnp.einsum('secf,efd->secd', hidden, expert_down, preferred_element_type=...  5.04 us
    unnamed x1, matrix products  3.64 us
    unnamed x3, local copies, waits for them, and re-layouts  2.66 us
  transfers between devices with their start and end apart: 1, of which 1 were waited for; matrix products, arithmetic and copies ran while one was open for 0% of the time, Pallas kernels for 0%

commit v1 on v0

v1 whole, which is shorter than its diff:
```python
import functools

import jax
import jax.numpy as jnp
from jax import lax
from jax.experimental import pallas as pl
from jax.experimental.pallas import tpu as pltpu
from jax.sharding import PartitionSpec as P

CAP = 8
NT = (((1,), (1,)), ((), ()))
TN = (((0,), (0,)), ((), ()))
VMEM = pl.BlockSpec(memory_space=pltpu.VMEM)
HBM = pl.BlockSpec(memory_space=pltpu.HBM)


def dest(i, j, n):
    return i ^ j if n & (n - 1) == 0 else (i + j) % n


def source(i, j, n):
    return i ^ j if n & (n - 1) == 0 else (i + n - j) % n


def chunks_of(total, size):
    return [(at, min(size, total - at)) for at in range(0, total, size)]


def route_kernel(rows, exp_dev, ids_ref, w_ref, place_ref, high_ref, low_ref):
    pair = 2 if rows % 2 == 0 else 1
    chips = rows // pair
    me = lax.axis_index("row")
    top, toks = ids_ref.shape
    experts = rows * exp_dev
    at = lax.broadcasted_iota(jnp.int32, (experts, 1), 0)
    e, q, j = at // rows, (at // chips) % pair, at % chips
    chip = dest(jnp.full_like(at, me // pair), j, chips)
    core = jnp.full_like(at, me % pair) ^ q
    expert = (chip * pair + core) * exp_dev + e
    hit = jnp.zeros((experts, toks), jnp.float32)
    weight = jnp.zeros((experts, toks), jnp.float32)
    for k in range(top):
        same = (ids_ref[k : k + 1, :] == expert).astype(jnp.float32)
        hit += same
        weight += same * w_ref[k : k + 1, :]
    earlier = lax.broadcasted_iota(jnp.int32, (toks, toks), 0)
    later = lax.broadcasted_iota(jnp.int32, (toks, toks), 1)
    before = jnp.dot(
        hit.astype(jnp.bfloat16),
        (earlier < later).astype(jnp.bfloat16),
        preferred_element_type=jnp.float32,
    )
    slot = jnp.where(hit > 0.0, before, -1.0)
    spread = lambda a: jnp.broadcast_to(a[:, None, :], (experts, CAP, toks)).reshape(
        experts * CAP, toks
    )
    want = lax.broadcasted_iota(jnp.int32, (experts * CAP, toks), 0) % CAP
    place = (spread(slot) == want.astype(jnp.float32)).astype(jnp.float32)
    value = place * spread(weight)
    high = value.astype(jnp.bfloat16)
    place_ref[...] = place.astype(jnp.bfloat16)
    high_ref[...] = high
    low_ref[...] = (value - high.astype(jnp.float32)).astype(jnp.bfloat16)


def dispatch_kernel(cols, outs, place_ref, *refs):
    part_refs, out_refs, whole = refs[:cols], refs[cols : cols + outs], refs[-1]
    col = lax.axis_index("col")
    width = part_refs[0].shape[1]
    parts = [r[...] for r in part_refs]
    for p in range(cols):
        j = source(col, p, cols) if cols & (cols - 1) == 0 else (col + cols - p) % cols
        part = parts[0]
        for other in range(1, cols):
            part = jnp.where(j == other, parts[other], part)
        whole[:, p * width : (p + 1) * width] = part.astype(jnp.float32)
    full = whole[...].astype(jnp.bfloat16)
    sent = jnp.dot(place_ref[...], full, preferred_element_type=jnp.float32)
    sent = sent.astype(jnp.bfloat16)
    each = sent.shape[0] // outs
    for i in range(outs):
        out_refs[i][...] = sent[i * each : (i + 1) * each]


def expert_kernel(e, blocks, gu_hbm, dn_hbm, *refs):
    x_refs, y_refs = refs[:blocks], refs[blocks : 2 * blocks]
    gu, dn, x, hidden, sems = refs[2 * blocks :]
    hid, width = dn.shape
    steps = chunks_of(hid, 256)
    copies = []
    for i, (at, size) in enumerate(steps):
        for g in range(2):
            copies.append(
                pltpu.make_async_copy(
                    gu_hbm.at[e, g, pl.ds(at, size)],
                    gu.at[g, pl.ds(at, size)],
                    sems.at[2 * i + g],
                )
            )
    last = pltpu.make_async_copy(dn_hbm.at[e], dn, sems.at[2 * len(steps)])
    for c in copies:
        c.start()
    last.start()
    rows = x_refs[0].shape[0]
    for b in range(blocks):
        x[b * rows : (b + 1) * rows] = x_refs[b][...]
    for i, (at, size) in enumerate(steps):
        copies[2 * i].wait()
        gate = lax.dot_general(
            x[...], gu[0, at : at + size], NT, preferred_element_type=jnp.float32
        )
        copies[2 * i + 1].wait()
        up = lax.dot_general(
            x[...], gu[1, at : at + size], NT, preferred_element_type=jnp.float32
        )
        act = (up + 1.0) * gate * jax.nn.sigmoid(1.702 * gate)
        hidden[:, at : at + size] = act.astype(jnp.bfloat16)
    last.wait()
    for at, size in chunks_of(width, 768):
        part = jnp.dot(
            hidden[...], dn[:, at : at + size], preferred_element_type=jnp.float32
        ).astype(jnp.bfloat16)
        for b in range(blocks):
            y_refs[b][:, at : at + size] = part[b * rows : (b + 1) * rows]


def combine_kernel(exp_dev, chips, pair, cols, high_ref, low_ref, *refs):
    per = chips + (pair - 1)
    ins, refs = refs[: exp_dev * per], refs[exp_dev * per :]
    own_ref, out_refs, flat, mixed = refs[0], refs[1:cols], refs[-2], refs[-1]
    col = lax.axis_index("col")
    at = 0
    for e in range(exp_dev):
        for j in range(chips):
            flat[at : at + CAP] = ins[e * per + j][:CAP]
            at += CAP
        if pair == 2:
            flat[at : at + CAP * chips] = ins[e * per + chips][...]
            at += CAP * chips
    y = flat[...]
    total = lax.dot_general(high_ref[...], y, TN, preferred_element_type=jnp.float32)
    total += lax.dot_general(low_ref[...], y, TN, preferred_element_type=jnp.float32)
    width = own_ref.shape[1]
    for p in range(cols):
        mixed[p] = total[:, p * width : (p + 1) * width]
    own_ref[...] = mixed[col]
    for j in range(1, cols):
        out_refs[j - 1][...] = mixed[dest(col, j, cols)].astype(jnp.bfloat16)


def params(mib):
    return pltpu.CompilerParams(vmem_limit_bytes=mib << 20)


def on_device(tokens, route_ids, route_weights, expert_gate_up, expert_down):
    rows, cols = lax.axis_size("row"), lax.axis_size("col")
    pair = 2 if rows % 2 == 0 else 1
    chips = rows // pair
    toks, part_width = tokens.shape
    exp_dev, width, _, hid = expert_gate_up.shape
    slots = exp_dev * rows * CAP
    bf16, f32 = jnp.bfloat16, jnp.float32
    shape = jax.ShapeDtypeStruct

    def over_col(x, j):
        return lax.ppermute(x, "col", [(i, dest(i, j, cols)) for i in range(cols)])

    def over_chips(x, j, back=False):
        to = source if back else dest
        perm = [
            (c * pair + k, to(c, j, chips) * pair + k)
            for c in range(chips)
            for k in range(pair)
        ]
        return lax.ppermute(x, "row", perm)

    def over_cores(x):
        return lax.ppermute(x, "row", [(i, i ^ 1) for i in range(rows)])

    far = list(range(cols - 1, 0, -1))
    arrived = {j: over_col(tokens, j) for j in far}
    parts = [tokens] + [arrived[j] for j in range(1, cols)]

    place, high, low = pl.pallas_call(
        functools.partial(route_kernel, rows, exp_dev),
        out_shape=[shape((slots, toks), bf16)] * 3,
        in_specs=[VMEM] * 2,
        out_specs=[VMEM] * 3,
        compiler_params=params(4),
        name="route",
    )(route_ids.T, route_weights.T)

    outs = exp_dev * pair
    sent = pl.pallas_call(
        functools.partial(dispatch_kernel, cols, outs),
        out_shape=[shape((chips * CAP, width), bf16)] * outs,
        in_specs=[VMEM] * (1 + cols),
        out_specs=[VMEM] * outs,
        scratch_shapes=[pltpu.VMEM((toks, width), f32)],
        compiler_params=params(8),
        name="dispatch",
    )(place, *parts)

    gate_up = jnp.transpose(expert_gate_up, (0, 2, 3, 1))
    block = pair * CAP
    n_copies = 2 * len(chunks_of(hid, 256)) + 1
    inputs = []
    for e in range(exp_dev):
        halves = [sent[e * pair].reshape(chips, CAP, width)]
        if pair == 2:
            halves.append(over_cores(sent[e * pair + 1]).reshape(chips, CAP, width))
        blocks = [
            jnp.concatenate([h[j] for h in halves], axis=0) for j in range(chips)
        ]
        inputs.append(
            {0: blocks[0]}
            | {j: over_chips(blocks[j], j) for j in range(chips - 1, 0, -1)}
        )
    terms = []
    for e in range(exp_dev):
        ys = pl.pallas_call(
            functools.partial(expert_kernel, e, chips),
            out_shape=[shape((block, width), bf16)] * chips,
            in_specs=[HBM] * 2 + [VMEM] * chips,
            out_specs=[VMEM] * chips,
            scratch_shapes=[
                pltpu.VMEM((2, hid, width), bf16),
                pltpu.VMEM((hid, width), bf16),
                pltpu.VMEM((chips * block, width), bf16),
                pltpu.VMEM((chips * block, hid), bf16),
                pltpu.SemaphoreType.DMA((n_copies,)),
            ],
            compiler_params=params(24),
            cost_estimate=pl.CostEstimate(
                flops=6 * chips * block * width * hid,
                bytes_accessed=6 * width * hid,
                transcendentals=chips * block * hid,
            ),
            name=f"expert{e}",
        )(gate_up, expert_down, *[inputs[e][j] for j in range(chips)])
        back = {0: ys[0]} | {
            j: over_chips(ys[j], j, True) for j in range(chips - 1, 0, -1)
        }
        got = [back[j] for j in range(chips)]
        terms += got
        if pair == 2:
            give = jnp.concatenate([g[CAP:] for g in got], axis=0)
            terms.append(over_cores(give))

    own, *leaving = pl.pallas_call(
        functools.partial(combine_kernel, exp_dev, chips, pair, cols),
        out_shape=[shape((toks, part_width), f32)]
        + [shape((toks, part_width), bf16)] * (cols - 1),
        in_specs=[VMEM] * (2 + len(terms)),
        out_specs=[VMEM] * cols,
        scratch_shapes=[
            pltpu.VMEM((slots, width), bf16),
            pltpu.VMEM((cols, toks, part_width), f32),
        ],
        compiler_params=params(16),
        name="combine",
    )(high, low, *terms)
    total = own
    for j in far:
        total = total + over_col(leaving[j - 1], j).astype(f32)
    return total.astype(bf16)


def solution(mesh):
    return jax.shard_map(
        on_device,
        mesh=mesh,
        in_specs=(
            P("row", "col"),
            P("row", None),
            P("row", None),
            P("row", None, None, "col"),
            P("row", "col", None),
        ),
        out_specs=P("row", "col"),
        check_vma=False,
    )
```

time: 124 us -> 70.8 us (0.57)
  blocking collectives: 54 us -> 0 us
  starting transfers between devices: 0.01 us -> 25.5 us
  waiting for transfers between devices: 33.5 us -> 14.5 us
  Pallas kernels: 0 us -> 18 us
  matrix products: 17.7 us -> 0 us
  between operations: 13.5 us -> 0.21 us
  local copies, waits for them, and re-layouts: 3.55 us -> 11.5 us
    all_to_all x2 -> x0, blocking collectives: 38.4 us -> none  [the longest x1 22.7 us: on_device(): lax.all_to_all(partial_out, 'row', split_axis=0, concat_axis=0, tiled=True)]
    unnamed x2 -> x0, waiting for transfers between devices: 33.5 us -> none
    ppermute x0 -> x22, starting transfers between devices: none -> 25.5 us  [the longest x12 14.7 us: over_chips(): return lax.ppermute(x, 'row', perm)]
    pallas_call x0 -> x5, Pallas kernels: none -> 18 us  [the longest x2 16.9 us: on_device(): pl.pallas_call(functools.partial(expert_kernel, e, chips), out_shape=[sha...]
    all_gather x1 -> x0, blocking collectives: 15.7 us -> none  [on_device(): whole = lax.all_gather(tokens, 'col', axis=1, tiled=True)]
    ppermute x0 -> x22, waiting for transfers between devices: none -> 14.5 us  [the longest x6 7.33 us: over_col(): return lax.ppermute(x, 'col', [(i, dest(i, j, cols)) for i in range(cols)])]
    dot_general x3 -> x0, matrix products: 14 us -> none  [the longest x1 8.58 us: on_device(): jnp.einsum('secd,edf->secf', arrived, weights_gu, preferred_element_type=...]
    unnamed x3 -> x10, local copies, waits for them, and re-layouts: 2.66 us -> 11.4 us
  transfers between devices with their start and end apart: 1 -> 22, of which waited for: 1 -> 11; matrix products, arithmetic and copies ran while one was open for 0% -> 0% of each run, Pallas kernels for 0% -> 24%
where the time goes in v1:
time: 70.8 us; the launch traced here: 70.5 us
  starting transfers between devices  25.5 us (36%)
  Pallas kernels  18 us (25%)
  waiting for transfers between devices  14.5 us (20%)
  local copies, waits for them, and re-layouts  11.5 us (16%)
  other arithmetic  0.78 us (1%)
    pallas_call x2, Pallas kernels, on_device(): pl.pallas_call(functools.partial(expert_kernel, e, chips), out_shape=[sha...  16.9 us
    ppermute x12, starting transfers between devices, over_chips(): return lax.ppermute(x, 'row', perm)  14.7 us
    unnamed x10, local copies, waits for them, and re-layouts  11.4 us
    ppermute x6, starting transfers between devices, over_col(): return lax.ppermute(x, 'col', [(i, dest(i, j, cols)) for i in range(cols)])  10.1 us
    ppermute x6, waiting for transfers between devices, over_col(): return lax.ppermute(x, 'col', [(i, dest(i, j, cols)) for i in range(cols)])  7.33 us
    ppermute x12, waiting for transfers between devices, over_chips(): return lax.ppermute(x, 'row', perm)  4.92 us
    ppermute x4, waiting for transfers between devices, over_cores(): return lax.ppermute(x, 'row', [(i, i ^ 1) for i in range(rows)])  2.3 us
  transfers between devices with their start and end apart: 22, of which 11 were waited for; matrix products, arithmetic and copies ran while one was open for 0% of the time, Pallas kernels for 24%

profile of v1, /device:TPU:0, one launch (start us, length us, event | category | flops | bytes accessed | tf_op | source)
XLA Modules:
  0.0 70.5 jit_solution(13286245490725862777)
XLA Ops:
  0.0 4.1 %collective-permute-start.1 = (bf16[32,720]{1,0:T(8,128)(2,1)}, bf16[32,720]{1,0:T(8,128)(2,1)S(1)}, u32[]{:S(2)}, u32[]{:S(2)}) collective-permute-start(bf16[32,720]{1,0:T(8,128)(2,1)} %refs_0_.1), channel_id=1, source_target_pairs={{0,2},{1,3},{2,0},{3,1},{4,6},{5,7},{6,4},{7,5},{8,10},{9,11},{10,... | collective-permute-start | bytes 138248 | tf_op jit(solution)/shard_map/ppermute | solution.py:166
  4.1 1.6 %collective-permute-start = (bf16[32,720]{1,0:T(8,128)(2,1)}, bf16[32,720]{1,0:T(8,128)(2,1)S(1)}, u32[]{:S(2)}, u32[]{:S(2)}) collective-permute-start(bf16[32,720]{1,0:T(8,128)(2,1)} %refs_0_.1), channel_id=1, source_target_pairs={{0,1},{1,0},{2,3},{3,2},{4,5},{5,4},{6,7},{7,6},{8,9},{9,8},{10,11... | collective-permute-start | bytes 138248 | tf_op jit(solution)/shard_map/ppermute | solution.py:166
  7.2 1.2 %collective-permute-done.refs_1_ = bf16[32,720]{1,0:T(8,128)(2,1)S(1)} collective-permute-done((bf16[32,720]{1,0:T(8,128)(2,1)}, bf16[32,720]{1,0:T(8,128)(2,1)S(1)}, u32[]{:S(2)}, u32[]{:S(2)}) %collective-permute-start) | collective-permute-done | bytes 46112 | tf_op jit(solution)/shard_map/ppermute | solution.py:166
  8.4 3.4 %collective-permute-done.2.refs_3_ = bf16[32,720]{1,0:T(8,128)(2,1)S(1)} collective-permute-done((bf16[32,720]{1,0:T(8,128)(2,1)}, bf16[32,720]{1,0:T(8,128)(2,1)S(1)}, u32[]{:S(2)}, u32[]{:S(2)}) %collective-permute-start.2) | collective-permute-done | bytes 46112 | tf_op jit(solution)/shard_map/ppermute | solution.py:166
  13.5 0.9 %collective-permute-done.3 = bf16[32,2880]{1,0:T(8,128)(2,1)S(1)} collective-permute-done((bf16[32,2880]{1,0:T(8,128)(2,1)S(1)}, bf16[32,2880]{1,0:T(8,128)(2,1)S(1)}, u32[]{:S(2)}, u32[]{:S(2)}) %collective-permute-start.3) | collective-permute-done | bytes 184352 | tf_op jit(solution)/shard_map/ppermute | solution.py:178
  14.5 1.6 %collective-permute-start.4 = (bf16[16,2880]{1,0:T(8,128)(2,1)S(1)}, bf16[16,2880]{1,0:T(8,128)(2,1)S(1)}, u32[]{:S(2)}, u32[]{:S(2)}) collective-permute-start(bf16[16,2880]{1,0:T(8,128)(2,1)S(1)} %pad_maximum_fusion.3), channel_id=1, source_target_pairs={{0,8},{4,12},{8,0},{12,4},{16,24},{20,28},{24,16},{28,20},{1,9},{5... | collective-permute-start | bytes 276488 | tf_op jit(solution)/shard_map/ppermute | solution.py:175
  16.0 1.6 %collective-permute-start.5 = (bf16[16,2880]{1,0:T(8,128)(2,1)S(1)}, bf16[16,2880]{1,0:T(8,128)(2,1)S(1)}, u32[]{:S(2)}, u32[]{:S(2)}) collective-permute-start(bf16[16,2880]{1,0:T(8,128)(2,1)S(1)} %pad_maximum_fusion.4), channel_id=1, source_target_pairs={{0,16},{4,20},{8,24},{12,28},{16,0},{20,4},{24,8},{28,12},{1,17},{... | collective-permute-start | bytes 276488 | tf_op jit(solution)/shard_map/ppermute | solution.py:175
  18.2 1.6 %collective-permute-start.12 = (bf16[16,2880]{1,0:T(8,128)(2,1)S(1)}, bf16[16,2880]{1,0:T(8,128)(2,1)S(1)}, u32[]{:S(2)}, u32[]{:S(2)}) collective-permute-start(bf16[16,2880]{1,0:T(8,128)(2,1)S(1)} %pad_maximum_fusion.7), channel_id=1, source_target_pairs={{0,8},{4,12},{8,0},{12,4},{16,24},{20,28},{24,16},{28,20},{1,9},{5... | collective-permute-start | bytes 276488 | tf_op jit(solution)/shard_map/ppermute | solution.py:175
  19.8 1.6 %collective-permute-start.13 = (bf16[16,2880]{1,0:T(8,128)(2,1)S(1)}, bf16[16,2880]{1,0:T(8,128)(2,1)S(1)}, u32[]{:S(2)}, u32[]{:S(2)}) collective-permute-start(bf16[16,2880]{1,0:T(8,128)(2,1)S(1)} %pad_maximum_fusion.8), channel_id=1, source_target_pairs={{0,16},{4,20},{8,24},{12,28},{16,0},{20,4},{24,8},{28,12},{1,17},{... | collective-permute-start | bytes 276488 | tf_op jit(solution)/shard_map/ppermute | solution.py:175
  22.1 1.7 %collective-permute-done.6.refs_3_ = bf16[16,2880]{1,0:T(8,128)(2,1)S(1)} collective-permute-done((bf16[16,2880]{1,0:T(8,128)(2,1)S(1)}, bf16[16,2880]{1,0:T(8,128)(2,1)S(1)}, u32[]{:S(2)}, u32[]{:S(2)}) %collective-permute-start.6) | collective-permute-done | bytes 92192 | tf_op jit(solution)/shard_map/ppermute | solution.py:175
  23.9 5.8 %copy-done = bf16[2,2880,2,720]{1,3,2,0:T(8,128)(2,1)S(1)} copy-done((bf16[2,2880,2,720]{1,3,2,0:T(8,128)(2,1)S(1)}, bf16[2,2880,2,720]{1,3,2,0:T(8,128)(2,1)}, u32[]{:S(2)}) %copy-start) | copy-done | bytes 16588824
  29.7 3.4 %copy-done.1 = bf16[2,720,2880]{2,1,0:T(8,128)(2,1)S(1)} copy-done((bf16[2,720,2880]{2,1,0:T(8,128)(2,1)S(1)}, bf16[2,720,2880]{2,1,0:T(8,128)(2,1)}, u32[]{:S(2)}) %copy-start.1) | copy-done | bytes 8294424
  33.1 8.5 %expert0.1 = (bf16[16,2880]{1,0:T(8,128)(2,1)S(1)}, bf16[16,2880]{1,0:T(8,128)(2,1)S(1)}, bf16[16,2880]{1,0:T(8,128)(2,1)S(1)}, bf16[16,2880]{1,0:T(8,128)(2,1)S(1)}) custom-call(bf16[2,2,720,2880]{3,2,1,0:T(8,128)(2,1)S(1)} %bitcast.3, bf16[2,720,2880]{2,1,0:T(8,128)(2,1)S(1)} %copy-done.1, bf16[16,2880]{1,0:T(8,128)(2,1)S(1)} %pad_maximum_fusion.2.refs_0_, ...), custom_call_target="tpu_custom_call" | custom-call | flops 796262400 | bytes 12441600 | tf_op jit(solution)/shard_map/expert0/pallas_call | solution.py:221
  41.6 0.9 %collective-permute-start.7 = (bf16[16,2880]{1,0:T(8,128)(2,1)S(1)}, bf16[16,2880]{1,0:T(8,128)(2,1)S(1)}, u32[]{:S(2)}, u32[]{:S(2)}) collective-permute-start(bf16[16,2880]{1,0:T(8,128)(2,1)S(1)} %get-tuple-element.30), channel_id=1, source_target_pairs={{0,8},{4,12},{8,0},{12,4},{16,24},{20,28},{24,16},{28,20},{1,9},{5... | collective-permute-start | bytes 276488 | tf_op jit(solution)/shard_map/ppermute | solution.py:175
  43.0 2.1 %collective-permute-start.9 = (bf16[16,2880]{1,0:T(8,128)(2,1)S(1)}, bf16[16,2880]{1,0:T(8,128)(2,1)S(1)}, u32[]{:S(2)}, u32[]{:S(2)}) collective-permute-start(bf16[16,2880]{1,0:T(8,128)(2,1)S(1)} %get-tuple-element.32), channel_id=1, source_target_pairs={{0,24},{4,28},{8,16},{12,20},{16,8},{20,12},{24,0},{28,4},{1,25},{... | collective-permute-start | bytes 276488 | tf_op jit(solution)/shard_map/ppermute | solution.py:175
  45.2 8.5 %expert1.1 = (bf16[16,2880]{1,0:T(8,128)(2,1)S(1)}, bf16[16,2880]{1,0:T(8,128)(2,1)S(1)}, bf16[16,2880]{1,0:T(8,128)(2,1)S(1)}, bf16[16,2880]{1,0:T(8,128)(2,1)S(1)}) custom-call(bf16[2,2,720,2880]{3,2,1,0:T(8,128)(2,1)S(1)} %bitcast.4, bf16[2,720,2880]{2,1,0:T(8,128)(2,1)S(1)} %copy-done.1, bf16[16,2880]{1,0:T(8,128)(2,1)S(1)} %pad_maximum_fusion.6.refs_0_, ...), custom_call_target="tpu_custom_call" | custom-call | flops 796262400 | bytes 12441600 | tf_op jit(solution)/shard_map/expert1/pallas_call | solution.py:221
  53.7 0.9 %collective-permute-start.15 = (bf16[16,2880]{1,0:T(8,128)(2,1)S(1)}, bf16[16,2880]{1,0:T(8,128)(2,1)S(1)}, u32[]{:S(2)}, u32[]{:S(2)}) collective-permute-start(bf16[16,2880]{1,0:T(8,128)(2,1)S(1)} %get-tuple-element.36), channel_id=1, source_target_pairs={{0,8},{4,12},{8,0},{12,4},{16,24},{20,28},{24,16},{28,20},{1,9},{5... | collective-permute-start | bytes 276488 | tf_op jit(solution)/shard_map/ppermute | solution.py:175
  55.1 2.1 %collective-permute-start.17 = (bf16[16,2880]{1,0:T(8,128)(2,1)S(1)}, bf16[16,2880]{1,0:T(8,128)(2,1)S(1)}, u32[]{:S(2)}, u32[]{:S(2)}) collective-permute-start(bf16[16,2880]{1,0:T(8,128)(2,1)S(1)} %get-tuple-element.38), channel_id=1, source_target_pairs={{0,24},{4,28},{8,16},{12,20},{16,8},{20,12},{24,0},{28,4},{1,25},{... | collective-permute-start | bytes 276488 | tf_op jit(solution)/shard_map/ppermute | solution.py:175
  57.4 0.9 %collective-permute-done.15.refs_6_ = bf16[16,2880]{1,0:T(8,128)(2,1)S(1)} collective-permute-done((bf16[16,2880]{1,0:T(8,128)(2,1)S(1)}, bf16[16,2880]{1,0:T(8,128)(2,1)S(1)}, u32[]{:S(2)}, u32[]{:S(2)}) %collective-permute-start.15) | collective-permute-done | bytes 92192 | tf_op jit(solution)/shard_map/ppermute | solution.py:175
  58.3 0.8 %collective-permute-done.16.refs_7_ = bf16[16,2880]{1,0:T(8,128)(2,1)S(1)} collective-permute-done((bf16[16,2880]{1,0:T(8,128)(2,1)S(1)}, bf16[16,2880]{1,0:T(8,128)(2,1)S(1)}, u32[]{:S(2)}, u32[]{:S(2)}) %collective-permute-start.16) | collective-permute-done | bytes 92192 | tf_op jit(solution)/shard_map/ppermute | solution.py:175
  59.2 1.4 %collective-permute-done.17.refs_8_ = bf16[16,2880]{1,0:T(8,128)(2,1)S(1)} collective-permute-done((bf16[16,2880]{1,0:T(8,128)(2,1)S(1)}, bf16[16,2880]{1,0:T(8,128)(2,1)S(1)}, u32[]{:S(2)}, u32[]{:S(2)}) %collective-permute-start.17) | collective-permute-done | bytes 92192 | tf_op jit(solution)/shard_map/ppermute | solution.py:175
  60.7 1.4 %collective-permute-done.18.refs_9_ = bf16[32,2880]{1,0:T(8,128)(2,1)S(1)} collective-permute-done((bf16[32,2880]{1,0:T(8,128)(2,1)S(1)}, bf16[32,2880]{1,0:T(8,128)(2,1)S(1)}, u32[]{:S(2)}, u32[]{:S(2)}) %collective-permute-start.18) | collective-permute-done | bytes 184352 | tf_op jit(solution)/shard_map/ppermute | solution.py:178
  63.3 3.7 %collective-permute-start.21 = (bf16[32,720]{1,0:T(8,128)(2,1)S(1)}, bf16[32,720]{1,0:T(8,128)(2,1)S(1)}, u32[]{:S(2)}, u32[]{:S(2)}) collective-permute-start(bf16[32,720]{1,0:T(8,128)(2,1)S(1)} %get-tuple-element.42), channel_id=1, source_target_pairs={{0,1},{1,0},{2,3},{3,2},{4,5},{5,4},{6,7},{7,6},{8,9},{9,8},{10,11... | collective-permute-start | bytes 138248 | tf_op jit(solution)/shard_map/ppermute | solution.py:166
  67.1 2.0 %collective-permute-done.19 = bf16[32,720]{1,0:T(8,128)(2,1)S(1)} collective-permute-done((bf16[32,720]{1,0:T(8,128)(2,1)S(1)}, bf16[32,720]{1,0:T(8,128)(2,1)S(1)}, u32[]{:S(2)}, u32[]{:S(2)}) %collective-permute-start.19) | collective-permute-done | bytes 46112 | tf_op jit(solution)/shard_map/ppermute | solution.py:166
  (57 shorter events, 8.6 us)
Async XLA Ops:
  0.0 7.2 %collective-permute-start.1 = (bf16[32,720]{1,0:T(8,128)(2,1)}, bf16[32,720]{1,0:T(8,128)(2,1)S(1)}, u32[]{:S(2)}, u32[]{:S(2)}) collective-permute-start(bf16[32,720]{1,0:T(8,128)(2,1)} %refs_0_.1), channel_id=1, source_target_pairs={{0,2},{1,3},{2,0},{3,1},{4,6},{5,7},{6,4},{7,5},{8,10},{9,11},{10,... | collective-permute-start | bytes 138248 | tf_op jit(solution)/shard_map/ppermute | solution.py:166
  4.1 4.3 %collective-permute-start = (bf16[32,720]{1,0:T(8,128)(2,1)}, bf16[32,720]{1,0:T(8,128)(2,1)S(1)}, u32[]{:S(2)}, u32[]{:S(2)}) collective-permute-start(bf16[32,720]{1,0:T(8,128)(2,1)} %refs_0_.1), channel_id=1, source_target_pairs={{0,1},{1,0},{2,3},{3,2},{4,5},{5,4},{6,7},{7,6},{8,9},{9,8},{10,11... | collective-permute-start | bytes 138248 | tf_op jit(solution)/shard_map/ppermute | solution.py:166
  5.6 6.1 %collective-permute-start.2 = (bf16[32,720]{1,0:T(8,128)(2,1)}, bf16[32,720]{1,0:T(8,128)(2,1)S(1)}, u32[]{:S(2)}, u32[]{:S(2)}) collective-permute-start(bf16[32,720]{1,0:T(8,128)(2,1)} %refs_0_.1), channel_id=1, source_target_pairs={{0,3},{1,2},{2,1},{3,0},{4,7},{5,6},{6,5},{7,4},{8,11},{9,10},{10,... | collective-permute-start | bytes 138248 | tf_op jit(solution)/shard_map/ppermute | solution.py:166
  12.9 1.5 %collective-permute-start.3 = (bf16[32,2880]{1,0:T(8,128)(2,1)S(1)}, bf16[32,2880]{1,0:T(8,128)(2,1)S(1)}, u32[]{:S(2)}, u32[]{:S(2)}) collective-permute-start(bf16[32,2880]{1,0:T(8,128)(2,1)S(1)} %get-tuple-element.28), channel_id=1, source_target_pairs={{0,4},{4,0},{8,12},{12,8},{16,20},{20,16},{24,28},{28,24},{1,5},{5... | collective-permute-start | bytes 552968 | tf_op jit(solution)/shard_map/ppermute | solution.py:178
  13.0 5.2 %collective-permute-start.11 = (bf16[32,2880]{1,0:T(8,128)(2,1)S(1)}, bf16[32,2880]{1,0:T(8,128)(2,1)S(1)}, u32[]{:S(2)}, u32[]{:S(2)}) collective-permute-start(bf16[32,2880]{1,0:T(8,128)(2,1)S(1)} %get-tuple-element.34), channel_id=1, source_target_pairs={{0,4},{4,0},{8,12},{12,8},{16,20},{20,16},{24,28},{28,24},{1,5},{5... | collective-permute-start | bytes 552968 | tf_op jit(solution)/shard_map/ppermute | solution.py:178
  14.5 6.9 %collective-permute-start.4 = (bf16[16,2880]{1,0:T(8,128)(2,1)S(1)}, bf16[16,2880]{1,0:T(8,128)(2,1)S(1)}, u32[]{:S(2)}, u32[]{:S(2)}) collective-permute-start(bf16[16,2880]{1,0:T(8,128)(2,1)S(1)} %pad_maximum_fusion.3), channel_id=1, source_target_pairs={{0,8},{4,12},{8,0},{12,4},{16,24},{20,28},{24,16},{28,20},{1,9},{5... | collective-permute-start | bytes 276488 | tf_op jit(solution)/shard_map/ppermute | solution.py:175
  16.0 6.1 %collective-permute-start.5 = (bf16[16,2880]{1,0:T(8,128)(2,1)S(1)}, bf16[16,2880]{1,0:T(8,128)(2,1)S(1)}, u32[]{:S(2)}, u32[]{:S(2)}) collective-permute-start(bf16[16,2880]{1,0:T(8,128)(2,1)S(1)} %pad_maximum_fusion.4), channel_id=1, source_target_pairs={{0,16},{4,20},{8,24},{12,28},{16,0},{20,4},{24,8},{28,12},{1,17},{... | collective-permute-start | bytes 276488 | tf_op jit(solution)/shard_map/ppermute | solution.py:175
  17.6 6.2 %collective-permute-start.6 = (bf16[16,2880]{1,0:T(8,128)(2,1)S(1)}, bf16[16,2880]{1,0:T(8,128)(2,1)S(1)}, u32[]{:S(2)}, u32[]{:S(2)}) collective-permute-start(bf16[16,2880]{1,0:T(8,128)(2,1)S(1)} %pad_maximum_fusion.5), channel_id=1, source_target_pairs={{0,24},{4,28},{8,16},{12,20},{16,8},{20,12},{24,0},{28,4},{1,25},{... | collective-permute-start | bytes 276488 | tf_op jit(solution)/shard_map/ppermute | solution.py:175
  18.2 24.8 %collective-permute-start.12 = (bf16[16,2880]{1,0:T(8,128)(2,1)S(1)}, bf16[16,2880]{1,0:T(8,128)(2,1)S(1)}, u32[]{:S(2)}, u32[]{:S(2)}) collective-permute-start(bf16[16,2880]{1,0:T(8,128)(2,1)S(1)} %pad_maximum_fusion.7), channel_id=1, source_target_pairs={{0,8},{4,12},{8,0},{12,4},{16,24},{20,28},{24,16},{28,20},{1,9},{5... | collective-permute-start | bytes 276488 | tf_op jit(solution)/shard_map/ppermute | solution.py:175
  19.8 25.4 %collective-permute-start.13 = (bf16[16,2880]{1,0:T(8,128)(2,1)S(1)}, bf16[16,2880]{1,0:T(8,128)(2,1)S(1)}, u32[]{:S(2)}, u32[]{:S(2)}) collective-permute-start(bf16[16,2880]{1,0:T(8,128)(2,1)S(1)} %pad_maximum_fusion.8), channel_id=1, source_target_pairs={{0,16},{4,20},{8,24},{12,28},{16,0},{20,4},{24,8},{28,12},{1,17},{... | collective-permute-start | bytes 276488 | tf_op jit(solution)/shard_map/ppermute | solution.py:175
  21.4 23.8 %collective-permute-start.14 = (bf16[16,2880]{1,0:T(8,128)(2,1)S(1)}, bf16[16,2880]{1,0:T(8,128)(2,1)S(1)}, u32[]{:S(2)}, u32[]{:S(2)}) collective-permute-start(bf16[16,2880]{1,0:T(8,128)(2,1)S(1)} %pad_maximum_fusion.9), channel_id=1, source_target_pairs={{0,24},{4,28},{8,16},{12,20},{16,8},{20,12},{24,0},{28,4},{1,25},{... | collective-permute-start | bytes 276488 | tf_op jit(solution)/shard_map/ppermute | solution.py:175
  23.9 5.8 %copy-start = (bf16[2,2880,2,720]{1,3,2,0:T(8,128)(2,1)S(1)}, bf16[2,2880,2,720]{1,3,2,0:T(8,128)(2,1)}, u32[]{:S(2)}) copy-start(bf16[2,2880,2,720]{1,3,2,0:T(8,128)(2,1)} %param.8) | copy-start | bytes 49766404
  29.7 3.4 %copy-start.1 = (bf16[2,720,2880]{2,1,0:T(8,128)(2,1)S(1)}, bf16[2,720,2880]{2,1,0:T(8,128)(2,1)}, u32[]{:S(2)}) copy-start(bf16[2,720,2880]{2,1,0:T(8,128)(2,1)} %dn_hbm.3) | copy-start | bytes 24883204
  41.6 13.5 %collective-permute-start.7 = (bf16[16,2880]{1,0:T(8,128)(2,1)S(1)}, bf16[16,2880]{1,0:T(8,128)(2,1)S(1)}, u32[]{:S(2)}, u32[]{:S(2)}) collective-permute-start(bf16[16,2880]{1,0:T(8,128)(2,1)S(1)} %get-tuple-element.30), channel_id=1, source_target_pairs={{0,8},{4,12},{8,0},{12,4},{16,24},{20,28},{24,16},{28,20},{1,9},{5... | collective-permute-start | bytes 276488 | tf_op jit(solution)/shard_map/ppermute | solution.py:175
  42.5 14.8 %collective-permute-start.8 = (bf16[16,2880]{1,0:T(8,128)(2,1)S(1)}, bf16[16,2880]{1,0:T(8,128)(2,1)S(1)}, u32[]{:S(2)}, u32[]{:S(2)}) collective-permute-start(bf16[16,2880]{1,0:T(8,128)(2,1)S(1)} %get-tuple-element.31), channel_id=1, source_target_pairs={{0,16},{4,20},{8,24},{12,28},{16,0},{20,4},{24,8},{28,12},{1,17},{... | collective-permute-start | bytes 276488 | tf_op jit(solution)/shard_map/ppermute | solution.py:175
  43.0 14.3 %collective-permute-start.9 = (bf16[16,2880]{1,0:T(8,128)(2,1)S(1)}, bf16[16,2880]{1,0:T(8,128)(2,1)S(1)}, u32[]{:S(2)}, u32[]{:S(2)}) collective-permute-start(bf16[16,2880]{1,0:T(8,128)(2,1)S(1)} %get-tuple-element.32), channel_id=1, source_target_pairs={{0,24},{4,28},{8,16},{12,20},{16,8},{20,12},{24,0},{28,4},{1,25},{... | collective-permute-start | bytes 276488 | tf_op jit(solution)/shard_map/ppermute | solution.py:175
  53.7 4.6 %collective-permute-start.15 = (bf16[16,2880]{1,0:T(8,128)(2,1)S(1)}, bf16[16,2880]{1,0:T(8,128)(2,1)S(1)}, u32[]{:S(2)}, u32[]{:S(2)}) collective-permute-start(bf16[16,2880]{1,0:T(8,128)(2,1)S(1)} %get-tuple-element.36), channel_id=1, source_target_pairs={{0,8},{4,12},{8,0},{12,4},{16,24},{20,28},{24,16},{28,20},{1,9},{5... | collective-permute-start | bytes 276488 | tf_op jit(solution)/shard_map/ppermute | solution.py:175
  54.6 4.6 %collective-permute-start.16 = (bf16[16,2880]{1,0:T(8,128)(2,1)S(1)}, bf16[16,2880]{1,0:T(8,128)(2,1)S(1)}, u32[]{:S(2)}, u32[]{:S(2)}) collective-permute-start(bf16[16,2880]{1,0:T(8,128)(2,1)S(1)} %get-tuple-element.37), channel_id=1, source_target_pairs={{0,16},{4,20},{8,24},{12,28},{16,0},{20,4},{24,8},{28,12},{1,17},{... | collective-permute-start | bytes 276488 | tf_op jit(solution)/shard_map/ppermute | solution.py:175
  55.1 5.5 %collective-permute-start.17 = (bf16[16,2880]{1,0:T(8,128)(2,1)S(1)}, bf16[16,2880]{1,0:T(8,128)(2,1)S(1)}, u32[]{:S(2)}, u32[]{:S(2)}) collective-permute-start(bf16[16,2880]{1,0:T(8,128)(2,1)S(1)} %get-tuple-element.38), channel_id=1, source_target_pairs={{0,24},{4,28},{8,16},{12,20},{16,8},{20,12},{24,0},{28,4},{1,25},{... | collective-permute-start | bytes 276488 | tf_op jit(solution)/shard_map/ppermute | solution.py:175
  57.3 3.4 %collective-permute-start.10 = (bf16[32,2880]{1,0:T(8,128)(2,1)S(1)}, bf16[32,2880]{1,0:T(8,128)(2,1)S(1)}, u32[]{:S(2)}, u32[]{:S(2)}) collective-permute-start(bf16[32,2880]{1,0:T(8,128)(2,1)S(1)} %pad_maximum_fusion), channel_id=1, source_target_pairs={{0,4},{4,0},{8,12},{12,8},{16,20},{20,16},{24,28},{28,24},{1,5},{5... | collective-permute-start | bytes 552968 | tf_op jit(solution)/shard_map/ppermute | solution.py:178
  60.6 1.5 %collective-permute-start.18 = (bf16[32,2880]{1,0:T(8,128)(2,1)S(1)}, bf16[32,2880]{1,0:T(8,128)(2,1)S(1)}, u32[]{:S(2)}, u32[]{:S(2)}) collective-permute-start(bf16[32,2880]{1,0:T(8,128)(2,1)S(1)} %pad_maximum_fusion.1), channel_id=1, source_target_pairs={{0,4},{4,0},{8,12},{12,8},{16,20},{20,16},{24,28},{28,24},{1,5},{5... | collective-permute-start | bytes 552968 | tf_op jit(solution)/shard_map/ppermute | solution.py:178
  62.6 6.5 %collective-permute-start.19 = (bf16[32,720]{1,0:T(8,128)(2,1)S(1)}, bf16[32,720]{1,0:T(8,128)(2,1)S(1)}, u32[]{:S(2)}, u32[]{:S(2)}) collective-permute-start(bf16[32,720]{1,0:T(8,128)(2,1)S(1)} %get-tuple-element.40), channel_id=1, source_target_pairs={{0,3},{1,2},{2,1},{3,0},{4,7},{5,6},{6,5},{7,4},{8,11},{9,10},{10,... | collective-permute-start | bytes 138248 | tf_op jit(solution)/shard_map/ppermute | solution.py:166
  63.3 6.2 %collective-permute-start.20 = (bf16[32,720]{1,0:T(8,128)(2,1)S(1)}, bf16[32,720]{1,0:T(8,128)(2,1)S(1)}, u32[]{:S(2)}, u32[]{:S(2)}) collective-permute-start(bf16[32,720]{1,0:T(8,128)(2,1)S(1)} %get-tuple-element.41), channel_id=1, source_target_pairs={{0,2},{1,3},{2,0},{3,1},{4,6},{5,7},{6,4},{7,5},{8,10},{9,11},{10,... | collective-permute-start | bytes 138248 | tf_op jit(solution)/shard_map/ppermute | solution.py:166
  63.3 6.5 %collective-permute-start.21 = (bf16[32,720]{1,0:T(8,128)(2,1)S(1)}, bf16[32,720]{1,0:T(8,128)(2,1)S(1)}, u32[]{:S(2)}, u32[]{:S(2)}) collective-permute-start(bf16[32,720]{1,0:T(8,128)(2,1)S(1)} %get-tuple-element.42), channel_id=1, source_target_pairs={{0,1},{1,0},{2,3},{3,2},{4,5},{5,4},{6,7},{7,6},{8,9},{9,8},{10,11... | collective-permute-start | bytes 138248 | tf_op jit(solution)/shard_map/ppermute | solution.py:166
  (3 other events, 2.2 us)

commit v2 on v1

--- a/solution.py
+++ b/solution.py
@@ -26,7 +26,18 @@
     return [(at, min(size, total - at)) for at in range(0, total, size)]
 
 
-def route_kernel(rows, exp_dev, ids_ref, w_ref, place_ref, high_ref, low_ref):
+def fetches(e, gu_hbm, dn_hbm, gu, dn, sems):
+    return [
+        pltpu.make_async_copy(gu_hbm.at[e], gu, sems.at[0]),
+        pltpu.make_async_copy(dn_hbm.at[e], dn, sems.at[1]),
+    ]
+
+
+def route_kernel(rows, exp_dev, ids_ref, w_ref, gu_hbm, dn_hbm, *refs):
+    place_ref, high_ref, low_ref, gu, dn, *_, sems = refs
+    copies = fetches(0, gu_hbm, dn_hbm, gu, dn, sems)
+    for c in copies:
+        c.start()
     pair = 2 if rows % 2 == 0 else 1
     chips = rows // pair
     me = lax.axis_index("row")
@@ -61,6 +72,8 @@
     place_ref[...] = place.astype(jnp.bfloat16)
     high_ref[...] = high
     low_ref[...] = (value - high.astype(jnp.float32)).astype(jnp.bfloat16)
+    for c in copies:
+        c.wait()
 
 
 def dispatch_kernel(cols, outs, place_ref, *refs):
@@ -82,46 +95,38 @@
         out_refs[i][...] = sent[i * each : (i + 1) * each]
 
 
-def expert_kernel(e, blocks, gu_hbm, dn_hbm, *refs):
-    x_refs, y_refs = refs[:blocks], refs[blocks : 2 * blocks]
-    gu, dn, x, hidden, sems = refs[2 * blocks :]
-    hid, width = dn.shape
-    steps = chunks_of(hid, 256)
+def expert_kernel(e, blocks, more, *refs):
+    gu, dn = refs[:2]
+    refs = refs[2:]
     copies = []
-    for i, (at, size) in enumerate(steps):
-        for g in range(2):
-            copies.append(
-                pltpu.make_async_copy(
-                    gu_hbm.at[e, g, pl.ds(at, size)],
-                    gu.at[g, pl.ds(at, size)],
-                    sems.at[2 * i + g],
-                )
-            )
-    last = pltpu.make_async_copy(dn_hbm.at[e], dn, sems.at[2 * len(steps)])
+    if more:
+        copies = fetches(e + 1, *refs[:2], *refs[-5:-3], refs[-1])
+        refs = refs[4:-1]
     for c in copies:
         c.start()
-    last.start()
+    x_refs, y_refs = refs[:blocks], refs[blocks : 2 * blocks]
+    x, hidden = refs[-2:]
+    hid, width = dn.shape
     rows = x_refs[0].shape[0]
     for b in range(blocks):
         x[b * rows : (b + 1) * rows] = x_refs[b][...]
-    for i, (at, size) in enumerate(steps):
-        copies[2 * i].wait()
-        gate = lax.dot_general(
-            x[...], gu[0, at : at + size], NT, preferred_element_type=jnp.float32
-        )
-        copies[2 * i + 1].wait()
-        up = lax.dot_general(
-            x[...], gu[1, at : at + size], NT, preferred_element_type=jnp.float32
-        )
+    for at, size in chunks_of(hid, 256):
+        gate, up = [
+            lax.dot_general(
+                x[...], gu[g, at : at + size], NT, preferred_element_type=jnp.float32
+            )
+            for g in range(2)
+        ]
         act = (up + 1.0) * gate * jax.nn.sigmoid(1.702 * gate)
         hidden[:, at : at + size] = act.astype(jnp.bfloat16)
-    last.wait()
     for at, size in chunks_of(width, 768):
         part = jnp.dot(
             hidden[...], dn[:, at : at + size], preferred_element_type=jnp.float32
         ).astype(jnp.bfloat16)
         for b in range(blocks):
             y_refs[b][:, at : at + size] = part[b * rows : (b + 1) * rows]
+    for c in copies:
+        c.wait()
 
 
 def combine_kernel(exp_dev, chips, pair, cols, high_ref, low_ref, *refs):
@@ -148,6 +153,10 @@
         out_refs[j - 1][...] = mixed[dest(col, j, cols)].astype(jnp.bfloat16)
 
 
+def room(held_bytes):
+    return pltpu.CompilerParams(vmem_limit_bytes=(58 << 20) - held_bytes)
+
+
 def params(mib):
     return pltpu.CompilerParams(vmem_limit_bytes=mib << 20)
 
@@ -181,14 +190,21 @@
     arrived = {j: over_col(tokens, j) for j in far}
     parts = [tokens] + [arrived[j] for j in range(1, cols)]
 
-    place, high, low = pl.pallas_call(
+    gate_up = pltpu.with_memory_space_constraint(
+        jnp.transpose(expert_gate_up, (0, 2, 3, 1)), pltpu.HBM
+    )
+    expert_down = pltpu.with_memory_space_constraint(expert_down, pltpu.HBM)
+    held = [pltpu.VMEM((2, hid, width), bf16), pltpu.VMEM((hid, width), bf16)]
+    held_bytes = 6 * hid * width
+    place, high, low, *weights = pl.pallas_call(
         functools.partial(route_kernel, rows, exp_dev),
-        out_shape=[shape((slots, toks), bf16)] * 3,
-        in_specs=[VMEM] * 2,
-        out_specs=[VMEM] * 3,
-        compiler_params=params(4),
+        out_shape=[shape((slots, toks), bf16)] * 3 + held * exp_dev,
+        in_specs=[VMEM] * 2 + [HBM] * 2,
+        out_specs=[VMEM] * (3 + 2 * exp_dev),
+        scratch_shapes=[pltpu.SemaphoreType.DMA((2,))],
+        compiler_params=params(16),
         name="route",
-    )(route_ids.T, route_weights.T)
+    )(route_ids.T, route_weights.T, gate_up, expert_down)
 
     outs = exp_dev * pair
     sent = pl.pallas_call(
@@ -201,9 +217,7 @@
         name="dispatch",
     )(place, *parts)
 
-    gate_up = jnp.transpose(expert_gate_up, (0, 2, 3, 1))
     block = pair * CAP
-    n_copies = 2 * len(chunks_of(hid, 256)) + 1
     inputs = []
     for e in range(exp_dev):
         halves = [sent[e * pair].reshape(chips, CAP, width)]
@@ -218,26 +232,31 @@
         )
     terms = []
     for e in range(exp_dev):
+        more = e + 1 < exp_dev
         ys = pl.pallas_call(
-            functools.partial(expert_kernel, e, chips),
-            out_shape=[shape((block, width), bf16)] * chips,
-            in_specs=[HBM] * 2 + [VMEM] * chips,
-            out_specs=[VMEM] * chips,
+            functools.partial(expert_kernel, e, chips, more),
+            out_shape=[shape((block, width), bf16)] * chips + held * more,
+            in_specs=[VMEM] * 2 + [HBM, HBM, VMEM, VMEM] * more + [VMEM] * chips,
+            out_specs=[VMEM] * (chips + 2 * more),
             scratch_shapes=[
-                pltpu.VMEM((2, hid, width), bf16),
-                pltpu.VMEM((hid, width), bf16),
                 pltpu.VMEM((chips * block, width), bf16),
                 pltpu.VMEM((chips * block, hid), bf16),
-                pltpu.SemaphoreType.DMA((n_copies,)),
-            ],
-            compiler_params=params(24),
+            ]
+            + [pltpu.SemaphoreType.DMA((2,))] * more,
+            compiler_params=params(16),
             cost_estimate=pl.CostEstimate(
                 flops=6 * chips * block * width * hid,
                 bytes_accessed=6 * width * hid,
                 transcendentals=chips * block * hid,
             ),
+            input_output_aliases={4: chips, 5: chips + 1} if more else {},
             name=f"expert{e}",
-        )(gate_up, expert_down, *[inputs[e][j] for j in range(chips)])
+        )(
+            *weights[:2],
+            *[gate_up, expert_down, *weights[2:4]] * more,
+            *[inputs[e][j] for j in range(chips)],
+        )
+        weights = [*ys[chips:], *weights[4:]]
         back = {0: ys[0]} | {
             j: over_chips(ys[j], j, True) for j in range(chips - 1, 0, -1)
         }

time: 70.8 us -> 53.7 us (0.76)
  local copies, waits for them, and re-layouts: 11.5 us -> 1.46 us
  Pallas kernels: 18 us -> 13.9 us
  waiting for transfers between devices: 14.5 us -> 11.4 us
    unnamed x10 -> x6, local copies, waits for them, and re-layouts: 11.4 us -> 1.37 us
    pallas_call x2, Pallas kernels: 16.9 us -> 8.21 us  [on_device(): pl.pallas_call(functools.partial(expert_kernel, e, chips, more), out_shap...]
    pallas_call x1, Pallas kernels: 0.17 us -> 4.76 us  [on_device(): pl.pallas_call(functools.partial(route_kernel, rows, exp_dev), out_shape=...]
    ppermute x6, waiting for transfers between devices: 7.33 us -> 4.36 us  [over_col(): return lax.ppermute(x, 'col', [(i, dest(i, j, cols)) for i in range(cols)])]
  transfers between devices with their start and end apart: 22 -> 22, of which waited for: 11 -> 8; matrix products, arithmetic and copies ran while one was open for 0% -> 0% of each run, Pallas kernels for 24% -> 24%
where the time goes in v2:
time: 53.7 us; the launch traced here: 53.5 us
  starting transfers between devices  25.7 us (48%)
  Pallas kernels  13.9 us (26%)
  waiting for transfers between devices  11.4 us (21%)
  local copies, waits for them, and re-layouts  1.46 us (3%)
  other arithmetic  0.77 us (1%)
    ppermute x12, starting transfers between devices, over_chips(): return lax.ppermute(x, 'row', perm)  14.9 us
    ppermute x6, starting transfers between devices, over_col(): return lax.ppermute(x, 'col', [(i, dest(i, j, cols)) for i in range(cols)])  10.1 us
    pallas_call x2, Pallas kernels, on_device(): pl.pallas_call(functools.partial(expert_kernel, e, chips, more), out_shap...  8.21 us
    pallas_call x1, Pallas kernels, on_device(): pl.pallas_call(functools.partial(route_kernel, rows, exp_dev), out_shape=...  4.76 us
    ppermute x12, waiting for transfers between devices, over_chips(): return lax.ppermute(x, 'row', perm)  4.74 us
    ppermute x6, waiting for transfers between devices, over_col(): return lax.ppermute(x, 'col', [(i, dest(i, j, cols)) for i in range(cols)])  4.36 us
    ppermute x4, waiting for transfers between devices, over_cores(): return lax.ppermute(x, 'row', [(i, i ^ 1) for i in range(rows)])  2.3 us
    unnamed x6, local copies, waits for them, and re-layouts  1.37 us
  transfers between devices with their start and end apart: 22, of which 8 were waited for; matrix products, arithmetic and copies ran while one was open for 0% of the time, Pallas kernels for 24%

profile of v2, /device:TPU:0, one launch (start us, length us, event | category | flops | bytes accessed | tf_op | source)
XLA Modules:
  0.0 53.5 jit_solution(10059523236007596850)
XLA Ops:
  0.0 4.1 %collective-permute-start.1 = (bf16[32,720]{1,0:T(8,128)(2,1)}, bf16[32,720]{1,0:T(8,128)(2,1)S(1)}, u32[]{:S(2)}, u32[]{:S(2)}) collective-permute-start(bf16[32,720]{1,0:T(8,128)(2,1)} %refs_0_.1), channel_id=1, source_target_pairs={{0,2},{1,3},{2,0},{3,1},{4,6},{5,7},{6,4},{7,5},{8,10},{9,11},{10,... | collective-permute-start | bytes 138248 | tf_op jit(solution)/shard_map/ppermute | solution.py:175
  4.1 1.6 %collective-permute-start = (bf16[32,720]{1,0:T(8,128)(2,1)}, bf16[32,720]{1,0:T(8,128)(2,1)S(1)}, u32[]{:S(2)}, u32[]{:S(2)}) collective-permute-start(bf16[32,720]{1,0:T(8,128)(2,1)} %refs_0_.1), channel_id=1, source_target_pairs={{0,1},{1,0},{2,3},{3,2},{4,5},{5,4},{6,7},{7,6},{8,9},{9,8},{10,11... | collective-permute-start | bytes 138248 | tf_op jit(solution)/shard_map/ppermute | solution.py:175
  5.6 0.7 %copy-done.1 = s32[32,4]{0,1:T(4,128)S(1)} copy-done((s32[32,4]{0,1:T(4,128)S(1)}, s32[32,4]{0,1:T(4,128)}, u32[]{:S(2)}) %copy-start.1) | copy-done | bytes 536
  7.0 4.8 %route.1 = (bf16[128,32]{1,0:T(8,128)(2,1)S(1)}, bf16[128,32]{1,0:T(8,128)(2,1)S(1)}, bf16[128,32]{1,0:T(8,128)(2,1)S(1)}, bf16[2,720,2880]{2,1,0:T(8,128)(2,1)S...) custom-call(s32[4,32]{1,0:T(4,128)S(1)} %bitcast.3, ...), custom_call_target="tpu_custom_call" | custom-call | tf_op jit(solution)/shard_map/route/pallas_call | solution.py:199
  12.8 0.9 %collective-permute-done.3 = bf16[32,2880]{1,0:T(8,128)(2,1)S(1)} collective-permute-done((bf16[32,2880]{1,0:T(8,128)(2,1)S(1)}, bf16[32,2880]{1,0:T(8,128)(2,1)S(1)}, u32[]{:S(2)}, u32[]{:S(2)}) %collective-permute-start.3) | collective-permute-done | bytes 184352 | tf_op jit(solution)/shard_map/ppermute | solution.py:187
  13.7 1.8 %collective-permute-start.4 = (bf16[16,2880]{1,0:T(8,128)(2,1)S(1)}, bf16[16,2880]{1,0:T(8,128)(2,1)S(1)}, u32[]{:S(2)}, u32[]{:S(2)}) collective-permute-start(bf16[16,2880]{1,0:T(8,128)(2,1)S(1)} %pad_maximum_fusion.3), channel_id=1, source_target_pairs={{0,8},{4,12},{8,0},{12,4},{16,24},{20,28},{24,16},{28,20},{1,9},{5... | collective-permute-start | bytes 276488 | tf_op jit(solution)/shard_map/ppermute | solution.py:184
  15.5 1.6 %collective-permute-start.5 = (bf16[16,2880]{1,0:T(8,128)(2,1)S(1)}, bf16[16,2880]{1,0:T(8,128)(2,1)S(1)}, u32[]{:S(2)}, u32[]{:S(2)}) collective-permute-start(bf16[16,2880]{1,0:T(8,128)(2,1)S(1)} %pad_maximum_fusion.4), channel_id=1, source_target_pairs={{0,16},{4,20},{8,24},{12,28},{16,0},{20,4},{24,8},{28,12},{1,17},{... | collective-permute-start | bytes 276488 | tf_op jit(solution)/shard_map/ppermute | solution.py:184
  17.5 1.8 %collective-permute-start.12 = (bf16[16,2880]{1,0:T(8,128)(2,1)S(1)}, bf16[16,2880]{1,0:T(8,128)(2,1)S(1)}, u32[]{:S(2)}, u32[]{:S(2)}) collective-permute-start(bf16[16,2880]{1,0:T(8,128)(2,1)S(1)} %pad_maximum_fusion.7), channel_id=1, source_target_pairs={{0,8},{4,12},{8,0},{12,4},{16,24},{20,28},{24,16},{28,20},{1,9},{5... | collective-permute-start | bytes 276488 | tf_op jit(solution)/shard_map/ppermute | solution.py:184
  19.3 1.6 %collective-permute-start.13 = (bf16[16,2880]{1,0:T(8,128)(2,1)S(1)}, bf16[16,2880]{1,0:T(8,128)(2,1)S(1)}, u32[]{:S(2)}, u32[]{:S(2)}) collective-permute-start(bf16[16,2880]{1,0:T(8,128)(2,1)S(1)} %pad_maximum_fusion.8), channel_id=1, source_target_pairs={{0,16},{4,20},{8,24},{12,28},{16,0},{20,4},{24,8},{28,12},{1,17},{... | collective-permute-start | bytes 276488 | tf_op jit(solution)/shard_map/ppermute | solution.py:184
  20.9 0.7 %collective-permute-start.14 = (bf16[16,2880]{1,0:T(8,128)(2,1)S(1)}, bf16[16,2880]{1,0:T(8,128)(2,1)S(1)}, u32[]{:S(2)}, u32[]{:S(2)}) collective-permute-start(bf16[16,2880]{1,0:T(8,128)(2,1)S(1)} %pad_maximum_fusion.9), channel_id=1, source_target_pairs={{0,24},{4,28},{8,16},{12,20},{16,8},{20,12},{24,0},{28,4},{1,25},{... | collective-permute-start | bytes 276488 | tf_op jit(solution)/shard_map/ppermute | solution.py:184
  21.7 1.7 %collective-permute-done.6.refs_9_ = bf16[16,2880]{1,0:T(8,128)(2,1)S(1)} collective-permute-done((bf16[16,2880]{1,0:T(8,128)(2,1)S(1)}, bf16[16,2880]{1,0:T(8,128)(2,1)S(1)}, u32[]{:S(2)}, u32[]{:S(2)}) %collective-permute-start.6) | collective-permute-done | bytes 92192 | tf_op jit(solution)/shard_map/ppermute | solution.py:184
  23.4 4.6 %expert0.1 = (bf16[16,2880]{1,0:T(8,128)(2,1)S(1)}, bf16[16,2880]{1,0:T(8,128)(2,1)S(1)}, bf16[16,2880]{1,0:T(8,128)(2,1)S(1)}, bf16[16,2880]{1,0:T(8,128)(2,1)S...) custom-call(bf16[2,720,2880]{2,1,0:T(8,128)(2,1)S(1)} %get-tuple-ele, ...), custom_call_target="tpu_custom_call", output_to_operand_aliasing={{4}: (4, {}), {5}: (5, {})} | custom-call | flops 796262400 | bytes 12441600 | tf_op jit(solution)/shard_map/expert0/pallas_call | solution.py:236
  28.0 0.9 %collective-permute-start.7 = (bf16[16,2880]{1,0:T(8,128)(2,1)S(1)}, bf16[16,2880]{1,0:T(8,128)(2,1)S(1)}, u32[]{:S(2)}, u32[]{:S(2)}) collective-permute-start(bf16[16,2880]{1,0:T(8,128)(2,1)S(1)} %get-tuple-element.40), channel_id=1, source_target_pairs={{0,8},{4,12},{8,0},{12,4},{16,24},{20,28},{24,16},{28,20},{1,9},{5... | collective-permute-start | bytes 276488 | tf_op jit(solution)/shard_map/ppermute | solution.py:184
  29.3 2.3 %collective-permute-start.9 = (bf16[16,2880]{1,0:T(8,128)(2,1)S(1)}, bf16[16,2880]{1,0:T(8,128)(2,1)S(1)}, u32[]{:S(2)}, u32[]{:S(2)}) collective-permute-start(bf16[16,2880]{1,0:T(8,128)(2,1)S(1)} %get-tuple-element.42), channel_id=1, source_target_pairs={{0,24},{4,28},{8,16},{12,20},{16,8},{20,12},{24,0},{28,4},{1,25},{... | collective-permute-start | bytes 276488 | tf_op jit(solution)/shard_map/ppermute | solution.py:184
  31.6 3.6 %expert1.1 = (bf16[16,2880]{1,0:T(8,128)(2,1)S(1)}, bf16[16,2880]{1,0:T(8,128)(2,1)S(1)}, bf16[16,2880]{1,0:T(8,128)(2,1)S(1)}, bf16[16,2880]{1,0:T(8,128)(2,1)S(1)}) custom-call(bf16[2,720,2880]{2,1,0:T(8,128)(2,1)S(1)} %get-tuple-element.43.refs_0_, bf16[720,2880]{1,0:T(8,128)(2,1)S(1)} %get-tuple-element.44.refs_1_, ...), custom_call_target="tpu_custom_call" | custom-call | flops 796262400 | bytes 12441600 | tf_op jit(solution)/shard_map/expert1/pallas_call | solution.py:236
  35.2 0.9 %collective-permute-start.15 = (bf16[16,2880]{1,0:T(8,128)(2,1)S(1)}, bf16[16,2880]{1,0:T(8,128)(2,1)S(1)}, u32[]{:S(2)}, u32[]{:S(2)}) collective-permute-start(bf16[16,2880]{1,0:T(8,128)(2,1)S(1)} %get-tuple-element.48), channel_id=1, source_target_pairs={{0,8},{4,12},{8,0},{12,4},{16,24},{20,28},{24,16},{28,20},{1,9},{5... | collective-permute-start | bytes 276488 | tf_op jit(solution)/shard_map/ppermute | solution.py:184
  36.5 2.3 %collective-permute-start.17 = (bf16[16,2880]{1,0:T(8,128)(2,1)S(1)}, bf16[16,2880]{1,0:T(8,128)(2,1)S(1)}, u32[]{:S(2)}, u32[]{:S(2)}) collective-permute-start(bf16[16,2880]{1,0:T(8,128)(2,1)S(1)} %get-tuple-element.50), channel_id=1, source_target_pairs={{0,24},{4,28},{8,16},{12,20},{16,8},{20,12},{24,0},{28,4},{1,25},{... | collective-permute-start | bytes 276488 | tf_op jit(solution)/shard_map/ppermute | solution.py:184
  38.9 0.9 %collective-permute-done.15.refs_6_ = bf16[16,2880]{1,0:T(8,128)(2,1)S(1)} collective-permute-done((bf16[16,2880]{1,0:T(8,128)(2,1)S(1)}, bf16[16,2880]{1,0:T(8,128)(2,1)S(1)}, u32[]{:S(2)}, u32[]{:S(2)}) %collective-permute-start.15) | collective-permute-done | bytes 92192 | tf_op jit(solution)/shard_map/ppermute | solution.py:184
  39.9 0.8 %collective-permute-done.16.refs_7_ = bf16[16,2880]{1,0:T(8,128)(2,1)S(1)} collective-permute-done((bf16[16,2880]{1,0:T(8,128)(2,1)S(1)}, bf16[16,2880]{1,0:T(8,128)(2,1)S(1)}, u32[]{:S(2)}, u32[]{:S(2)}) %collective-permute-start.16) | collective-permute-done | bytes 92192 | tf_op jit(solution)/shard_map/ppermute | solution.py:184
  40.7 1.2 %collective-permute-done.17.refs_8_ = bf16[16,2880]{1,0:T(8,128)(2,1)S(1)} collective-permute-done((bf16[16,2880]{1,0:T(8,128)(2,1)S(1)}, bf16[16,2880]{1,0:T(8,128)(2,1)S(1)}, u32[]{:S(2)}, u32[]{:S(2)}) %collective-permute-start.17) | collective-permute-done | bytes 92192 | tf_op jit(solution)/shard_map/ppermute | solution.py:184
  42.1 1.4 %collective-permute-done.18.refs_9_ = bf16[32,2880]{1,0:T(8,128)(2,1)S(1)} collective-permute-done((bf16[32,2880]{1,0:T(8,128)(2,1)S(1)}, bf16[32,2880]{1,0:T(8,128)(2,1)S(1)}, u32[]{:S(2)}, u32[]{:S(2)}) %collective-permute-start.18) | collective-permute-done | bytes 184352 | tf_op jit(solution)/shard_map/ppermute | solution.py:187
  44.0 3.9 %collective-permute-start.19 = (bf16[32,720]{1,0:T(8,128)(2,1)S(1)}, bf16[32,720]{1,0:T(8,128)(2,1)S(1)}, u32[]{:S(2)}, u32[]{:S(2)}) collective-permute-start(bf16[32,720]{1,0:T(8,128)(2,1)S(1)} %get-tuple-element.52), channel_id=1, source_target_pairs={{0,3},{1,2},{2,1},{3,0},{4,7},{5,6},{6,5},{7,4},{8,11},{9,10},{10,... | collective-permute-start | bytes 138248 | tf_op jit(solution)/shard_map/ppermute | solution.py:175
  48.5 2.0 %collective-permute-done.19 = bf16[32,720]{1,0:T(8,128)(2,1)S(1)} collective-permute-done((bf16[32,720]{1,0:T(8,128)(2,1)S(1)}, bf16[32,720]{1,0:T(8,128)(2,1)S(1)}, u32[]{:S(2)}, u32[]{:S(2)}) %collective-permute-start.19) | collective-permute-done | bytes 46112 | tf_op jit(solution)/shard_map/ppermute | solution.py:175
  50.5 2.3 %collective-permute-done.20 = bf16[32,720]{1,0:T(8,128)(2,1)S(1)} collective-permute-done((bf16[32,720]{1,0:T(8,128)(2,1)S(1)}, bf16[32,720]{1,0:T(8,128)(2,1)S(1)}, u32[]{:S(2)}, u32[]{:S(2)}) %collective-permute-start.20) | collective-permute-done | bytes 46112 | tf_op jit(solution)/shard_map/ppermute | solution.py:175
  (53 shorter events, 4.8 us)
Async XLA Ops:
  0.0 11.8 %collective-permute-start.1 = (bf16[32,720]{1,0:T(8,128)(2,1)}, bf16[32,720]{1,0:T(8,128)(2,1)S(1)}, u32[]{:S(2)}, u32[]{:S(2)}) collective-permute-start(bf16[32,720]{1,0:T(8,128)(2,1)} %refs_0_.1), channel_id=1, source_target_pairs={{0,2},{1,3},{2,0},{3,1},{4,6},{5,7},{6,4},{7,5},{8,10},{9,11},{10,... | collective-permute-start | bytes 138248 | tf_op jit(solution)/shard_map/ppermute | solution.py:175
  4.1 7.7 %collective-permute-start = (bf16[32,720]{1,0:T(8,128)(2,1)}, bf16[32,720]{1,0:T(8,128)(2,1)S(1)}, u32[]{:S(2)}, u32[]{:S(2)}) collective-permute-start(bf16[32,720]{1,0:T(8,128)(2,1)} %refs_0_.1), channel_id=1, source_target_pairs={{0,1},{1,0},{2,3},{3,2},{4,5},{5,4},{6,7},{7,6},{8,9},{9,8},{10,11... | collective-permute-start | bytes 138248 | tf_op jit(solution)/shard_map/ppermute | solution.py:175
  5.6 6.2 %collective-permute-start.2 = (bf16[32,720]{1,0:T(8,128)(2,1)}, bf16[32,720]{1,0:T(8,128)(2,1)S(1)}, u32[]{:S(2)}, u32[]{:S(2)}) collective-permute-start(bf16[32,720]{1,0:T(8,128)(2,1)} %refs_0_.1), channel_id=1, source_target_pairs={{0,3},{1,2},{2,1},{3,0},{4,7},{5,6},{6,5},{7,4},{8,11},{9,10},{10,... | collective-permute-start | bytes 138248 | tf_op jit(solution)/shard_map/ppermute | solution.py:175
  5.6 0.7 %copy-start.1 = (s32[32,4]{0,1:T(4,128)S(1)}, s32[32,4]{0,1:T(4,128)}, u32[]{:S(2)}) copy-start(s32[32,4]{0,1:T(4,128)} %param.6) | copy-start | bytes 1540
  7.0 4.8 %copy-start = (bf16[32,720]{1,0:T(8,128)(2,1)S(1)}, bf16[32,720]{1,0:T(8,128)(2,1)}, u32[]{:S(2)}) copy-start(bf16[32,720]{1,0:T(8,128)(2,1)} %refs_0_.1) | copy-start | bytes 138244
  12.2 1.5 %collective-permute-start.3 = (bf16[32,2880]{1,0:T(8,128)(2,1)S(1)}, bf16[32,2880]{1,0:T(8,128)(2,1)S(1)}, u32[]{:S(2)}, u32[]{:S(2)}) collective-permute-start(bf16[32,2880]{1,0:T(8,128)(2,1)S(1)} %get-tuple-element.38), channel_id=1, source_target_pairs={{0,4},{4,0},{8,12},{12,8},{16,20},{20,16},{24,28},{28,24},{1,5},{5... | collective-permute-start | bytes 552968 | tf_op jit(solution)/shard_map/ppermute | solution.py:187
  12.3 5.2 %collective-permute-start.11 = (bf16[32,2880]{1,0:T(8,128)(2,1)S(1)}, bf16[32,2880]{1,0:T(8,128)(2,1)S(1)}, u32[]{:S(2)}, u32[]{:S(2)}) collective-permute-start(bf16[32,2880]{1,0:T(8,128)(2,1)S(1)} %get-tuple-element.46), channel_id=1, source_target_pairs={{0,4},{4,0},{8,12},{12,8},{16,20},{20,16},{24,28},{28,24},{1,5},{5... | collective-permute-start | bytes 552968 | tf_op jit(solution)/shard_map/ppermute | solution.py:187
  13.7 7.2 %collective-permute-start.4 = (bf16[16,2880]{1,0:T(8,128)(2,1)S(1)}, bf16[16,2880]{1,0:T(8,128)(2,1)S(1)}, u32[]{:S(2)}, u32[]{:S(2)}) collective-permute-start(bf16[16,2880]{1,0:T(8,128)(2,1)S(1)} %pad_maximum_fusion.3), channel_id=1, source_target_pairs={{0,8},{4,12},{8,0},{12,4},{16,24},{20,28},{24,16},{28,20},{1,9},{5... | collective-permute-start | bytes 276488 | tf_op jit(solution)/shard_map/ppermute | solution.py:184
  15.5 6.1 %collective-permute-start.5 = (bf16[16,2880]{1,0:T(8,128)(2,1)S(1)}, bf16[16,2880]{1,0:T(8,128)(2,1)S(1)}, u32[]{:S(2)}, u32[]{:S(2)}) collective-permute-start(bf16[16,2880]{1,0:T(8,128)(2,1)S(1)} %pad_maximum_fusion.4), channel_id=1, source_target_pairs={{0,16},{4,20},{8,24},{12,28},{16,0},{20,4},{24,8},{28,12},{1,17},{... | collective-permute-start | bytes 276488 | tf_op jit(solution)/shard_map/ppermute | solution.py:184
  17.1 6.2 %collective-permute-start.6 = (bf16[16,2880]{1,0:T(8,128)(2,1)S(1)}, bf16[16,2880]{1,0:T(8,128)(2,1)S(1)}, u32[]{:S(2)}, u32[]{:S(2)}) collective-permute-start(bf16[16,2880]{1,0:T(8,128)(2,1)S(1)} %pad_maximum_fusion.5), channel_id=1, source_target_pairs={{0,24},{4,28},{8,16},{12,20},{16,8},{20,12},{24,0},{28,4},{1,25},{... | collective-permute-start | bytes 276488 | tf_op jit(solution)/shard_map/ppermute | solution.py:184
  17.5 11.8 %collective-permute-start.12 = (bf16[16,2880]{1,0:T(8,128)(2,1)S(1)}, bf16[16,2880]{1,0:T(8,128)(2,1)S(1)}, u32[]{:S(2)}, u32[]{:S(2)}) collective-permute-start(bf16[16,2880]{1,0:T(8,128)(2,1)S(1)} %pad_maximum_fusion.7), channel_id=1, source_target_pairs={{0,8},{4,12},{8,0},{12,4},{16,24},{20,28},{24,16},{28,20},{1,9},{5... | collective-permute-start | bytes 276488 | tf_op jit(solution)/shard_map/ppermute | solution.py:184
  19.3 12.3 %collective-permute-start.13 = (bf16[16,2880]{1,0:T(8,128)(2,1)S(1)}, bf16[16,2880]{1,0:T(8,128)(2,1)S(1)}, u32[]{:S(2)}, u32[]{:S(2)}) collective-permute-start(bf16[16,2880]{1,0:T(8,128)(2,1)S(1)} %pad_maximum_fusion.8), channel_id=1, source_target_pairs={{0,16},{4,20},{8,24},{12,28},{16,0},{20,4},{24,8},{28,12},{1,17},{... | collective-permute-start | bytes 276488 | tf_op jit(solution)/shard_map/ppermute | solution.py:184
  20.9 10.7 %collective-permute-start.14 = (bf16[16,2880]{1,0:T(8,128)(2,1)S(1)}, bf16[16,2880]{1,0:T(8,128)(2,1)S(1)}, u32[]{:S(2)}, u32[]{:S(2)}) collective-permute-start(bf16[16,2880]{1,0:T(8,128)(2,1)S(1)} %pad_maximum_fusion.9), channel_id=1, source_target_pairs={{0,24},{4,28},{8,16},{12,20},{16,8},{20,12},{24,0},{28,4},{1,25},{... | collective-permute-start | bytes 276488 | tf_op jit(solution)/shard_map/ppermute | solution.py:184
  28.0 8.4 %collective-permute-start.7 = (bf16[16,2880]{1,0:T(8,128)(2,1)S(1)}, bf16[16,2880]{1,0:T(8,128)(2,1)S(1)}, u32[]{:S(2)}, u32[]{:S(2)}) collective-permute-start(bf16[16,2880]{1,0:T(8,128)(2,1)S(1)} %get-tuple-element.40), channel_id=1, source_target_pairs={{0,8},{4,12},{8,0},{12,4},{16,24},{20,28},{24,16},{28,20},{1,9},{5... | collective-permute-start | bytes 276488 | tf_op jit(solution)/shard_map/ppermute | solution.py:184
  28.9 9.9 %collective-permute-start.8 = (bf16[16,2880]{1,0:T(8,128)(2,1)S(1)}, bf16[16,2880]{1,0:T(8,128)(2,1)S(1)}, u32[]{:S(2)}, u32[]{:S(2)}) collective-permute-start(bf16[16,2880]{1,0:T(8,128)(2,1)S(1)} %get-tuple-element.41), channel_id=1, source_target_pairs={{0,16},{4,20},{8,24},{12,28},{16,0},{20,4},{24,8},{28,12},{1,17},{... | collective-permute-start | bytes 276488 | tf_op jit(solution)/shard_map/ppermute | solution.py:184
  29.3 9.5 %collective-permute-start.9 = (bf16[16,2880]{1,0:T(8,128)(2,1)S(1)}, bf16[16,2880]{1,0:T(8,128)(2,1)S(1)}, u32[]{:S(2)}, u32[]{:S(2)}) collective-permute-start(bf16[16,2880]{1,0:T(8,128)(2,1)S(1)} %get-tuple-element.42), channel_id=1, source_target_pairs={{0,24},{4,28},{8,16},{12,20},{16,8},{20,12},{24,0},{28,4},{1,25},{... | collective-permute-start | bytes 276488 | tf_op jit(solution)/shard_map/ppermute | solution.py:184
  35.2 4.6 %collective-permute-start.15 = (bf16[16,2880]{1,0:T(8,128)(2,1)S(1)}, bf16[16,2880]{1,0:T(8,128)(2,1)S(1)}, u32[]{:S(2)}, u32[]{:S(2)}) collective-permute-start(bf16[16,2880]{1,0:T(8,128)(2,1)S(1)} %get-tuple-element.48), channel_id=1, source_target_pairs={{0,8},{4,12},{8,0},{12,4},{16,24},{20,28},{24,16},{28,20},{1,9},{5... | collective-permute-start | bytes 276488 | tf_op jit(solution)/shard_map/ppermute | solution.py:184
  36.1 4.6 %collective-permute-start.16 = (bf16[16,2880]{1,0:T(8,128)(2,1)S(1)}, bf16[16,2880]{1,0:T(8,128)(2,1)S(1)}, u32[]{:S(2)}, u32[]{:S(2)}) collective-permute-start(bf16[16,2880]{1,0:T(8,128)(2,1)S(1)} %get-tuple-element.49), channel_id=1, source_target_pairs={{0,16},{4,20},{8,24},{12,28},{16,0},{20,4},{24,8},{28,12},{1,17},{... | collective-permute-start | bytes 276488 | tf_op jit(solution)/shard_map/ppermute | solution.py:184
  36.5 5.5 %collective-permute-start.17 = (bf16[16,2880]{1,0:T(8,128)(2,1)S(1)}, bf16[16,2880]{1,0:T(8,128)(2,1)S(1)}, u32[]{:S(2)}, u32[]{:S(2)}) collective-permute-start(bf16[16,2880]{1,0:T(8,128)(2,1)S(1)} %get-tuple-element.50), channel_id=1, source_target_pairs={{0,24},{4,28},{8,16},{12,20},{16,8},{20,12},{24,0},{28,4},{1,25},{... | collective-permute-start | bytes 276488 | tf_op jit(solution)/shard_map/ppermute | solution.py:184
  38.9 3.2 %collective-permute-start.10 = (bf16[32,2880]{1,0:T(8,128)(2,1)S(1)}, bf16[32,2880]{1,0:T(8,128)(2,1)S(1)}, u32[]{:S(2)}, u32[]{:S(2)}) collective-permute-start(bf16[32,2880]{1,0:T(8,128)(2,1)S(1)} %pad_maximum_fusion), channel_id=1, source_target_pairs={{0,4},{4,0},{8,12},{12,8},{16,20},{20,16},{24,28},{28,24},{1,5},{5... | collective-permute-start | bytes 552968 | tf_op jit(solution)/shard_map/ppermute | solution.py:187
  42.0 1.5 %collective-permute-start.18 = (bf16[32,2880]{1,0:T(8,128)(2,1)S(1)}, bf16[32,2880]{1,0:T(8,128)(2,1)S(1)}, u32[]{:S(2)}, u32[]{:S(2)}) collective-permute-start(bf16[32,2880]{1,0:T(8,128)(2,1)S(1)} %pad_maximum_fusion.1), channel_id=1, source_target_pairs={{0,4},{4,0},{8,12},{12,8},{16,20},{20,16},{24,28},{28,24},{1,5},{5... | collective-permute-start | bytes 552968 | tf_op jit(solution)/shard_map/ppermute | solution.py:187
  44.0 6.5 %collective-permute-start.19 = (bf16[32,720]{1,0:T(8,128)(2,1)S(1)}, bf16[32,720]{1,0:T(8,128)(2,1)S(1)}, u32[]{:S(2)}, u32[]{:S(2)}) collective-permute-start(bf16[32,720]{1,0:T(8,128)(2,1)S(1)} %get-tuple-element.52), channel_id=1, source_target_pairs={{0,3},{1,2},{2,1},{3,0},{4,7},{5,6},{6,5},{7,4},{8,11},{9,10},{10,... | collective-permute-start | bytes 138248 | tf_op jit(solution)/shard_map/ppermute | solution.py:175
  47.8 5.0 %collective-permute-start.20 = (bf16[32,720]{1,0:T(8,128)(2,1)S(1)}, bf16[32,720]{1,0:T(8,128)(2,1)S(1)}, u32[]{:S(2)}, u32[]{:S(2)}) collective-permute-start(bf16[32,720]{1,0:T(8,128)(2,1)S(1)} %get-tuple-element.53), channel_id=1, source_target_pairs={{0,2},{1,3},{2,0},{3,1},{4,6},{5,7},{6,4},{7,5},{8,10},{9,11},{10,... | collective-permute-start | bytes 138248 | tf_op jit(solution)/shard_map/ppermute | solution.py:175
  47.8 5.0 %collective-permute-start.21 = (bf16[32,720]{1,0:T(8,128)(2,1)S(1)}, bf16[32,720]{1,0:T(8,128)(2,1)S(1)}, u32[]{:S(2)}, u32[]{:S(2)}) collective-permute-start(bf16[32,720]{1,0:T(8,128)(2,1)S(1)} %get-tuple-element.54), channel_id=1, source_target_pairs={{0,1},{1,0},{2,3},{3,2},{4,5},{5,4},{6,7},{7,6},{8,9},{9,8},{10,11... | collective-permute-start | bytes 138248 | tf_op jit(solution)/shard_map/ppermute | solution.py:175
  (1 other events, 0.7 us)

commit v3 on v2

v3 whole, which is shorter than its diff:
```python
import functools

import jax
import jax.numpy as jnp
from jax import lax
from jax.experimental import pallas as pl
from jax.experimental.pallas import tpu as pltpu
from jax.sharding import PartitionSpec as P


CAP = 8
NT = (((1,), (1,)), ((), ()))
TN = (((0,), (0,)), ((), ()))
VMEM = pl.BlockSpec(memory_space=pltpu.VMEM)
HBM = pl.BlockSpec(memory_space=pltpu.HBM)


def dest(i, j, n):
    return i ^ j if n & (n - 1) == 0 else (i + j) % n


def source(i, j, n):
    return i ^ j if n & (n - 1) == 0 else (i + n - j) % n


def chunks_of(total, size):
    return [(at, min(size, total - at)) for at in range(0, total, size)]


def fetches(e, gu_hbm, dn_hbm, gu, dn, sems):
    return [
        pltpu.make_async_copy(gu_hbm.at[e], gu, sems.at[0]),
        pltpu.make_async_copy(dn_hbm.at[e], dn, sems.at[1]),
    ]


def route_kernel(rows, exp_dev, ids_hbm, w_hbm, gu_hbm, dn_hbm, *refs):
    place_ref, high_ref, low_ref, gu, dn, ids_ref, w_ref, sems = refs
    small = [
        pltpu.make_async_copy(ids_hbm, ids_ref, sems.at[2]),
        pltpu.make_async_copy(w_hbm, w_ref, sems.at[3]),
    ]
    copies = fetches(0, gu_hbm, dn_hbm, gu, dn, sems)
    for c in small + copies:
        c.start()
    pair = 2 if rows % 2 == 0 else 1
    chips = rows // pair
    me = lax.axis_index("row")
    top, toks = ids_ref.shape
    experts = rows * exp_dev
    at = lax.broadcasted_iota(jnp.int32, (experts, 1), 0)
    q, j, e = at // (chips * exp_dev), (at // exp_dev) % chips, at % exp_dev
    chip = dest(jnp.full_like(at, me // pair), j, chips)
    core = jnp.full_like(at, me % pair) ^ q
    expert = (chip * pair + core) * exp_dev + e
    hit = jnp.zeros((experts, toks), jnp.float32)
    weight = jnp.zeros((experts, toks), jnp.float32)
    for c in small:
        c.wait()
    for k in range(top):
        same = (ids_ref[k : k + 1, :] == expert).astype(jnp.float32)
        hit += same
        weight += same * w_ref[k : k + 1, :]
    earlier = lax.broadcasted_iota(jnp.int32, (toks, toks), 0)
    later = lax.broadcasted_iota(jnp.int32, (toks, toks), 1)
    before = jnp.dot(
        hit.astype(jnp.bfloat16),
        (earlier < later).astype(jnp.bfloat16),
        preferred_element_type=jnp.float32,
    )
    slot = jnp.where(hit > 0.0, before, -1.0)
    spread = lambda a: jnp.broadcast_to(a[:, None, :], (experts, CAP, toks)).reshape(
        experts * CAP, toks
    )
    want = lax.broadcasted_iota(jnp.int32, (experts * CAP, toks), 0) % CAP
    place = (spread(slot) == want.astype(jnp.float32)).astype(jnp.float32)
    value = place * spread(weight)
    high = value.astype(jnp.bfloat16)
    place_ref[...] = place.astype(jnp.bfloat16)
    high_ref[...] = high
    low_ref[...] = (value - high.astype(jnp.float32)).astype(jnp.bfloat16)
    for c in copies:
        c.wait()


def dispatch_kernel(cols, outs, place_ref, *refs):
    part_refs, out_refs, whole = refs[:cols], refs[cols : cols + outs], refs[-1]
    col = lax.axis_index("col")
    width = part_refs[0].shape[1]
    parts = [r[...] for r in part_refs]
    for p in range(cols):
        j = source(col, p, cols) if cols & (cols - 1) == 0 else (col + cols - p) % cols
        part = parts[0]
        for other in range(1, cols):
            part = jnp.where(j == other, parts[other], part)
        whole[:, p * width : (p + 1) * width] = part.astype(jnp.float32)
    full = whole[...].astype(jnp.bfloat16)
    sent = jnp.dot(place_ref[...], full, preferred_element_type=jnp.float32)
    sent = sent.astype(jnp.bfloat16)
    at = 0
    for out in out_refs:
        out[...] = sent[at : at + out.shape[0]]
        at += out.shape[0]


def experts_kernel(exp_dev, blocks, gu_hbm, dn_hbm, gu0, dn0, *refs):
    x_refs, y_refs = refs[:blocks], refs[blocks : 2 * blocks]
    x, hidden, *held, sems = refs[2 * blocks :]
    gus, dns = [gu0, *held[0::2]], [dn0, *held[1::2]]
    copies = [
        fetches(e, gu_hbm, dn_hbm, gus[e], dns[e], sems.at[pl.ds(2 * e, 2)])
        for e in range(1, exp_dev)
    ]
    for pair in copies:
        for c in pair:
            c.start()
    hid, width = dn0.shape
    for e in range(exp_dev):
        gu, dn, rows = gus[e], dns[e], slice(e * CAP, (e + 1) * CAP)
        for b in range(blocks):
            x[b * CAP : (b + 1) * CAP] = x_refs[b][rows]
        if e:
            copies[e - 1][0].wait()
        for at, size in chunks_of(hid, 256):
            gate, up = [
                lax.dot_general(
                    x[...],
                    gu[g, at : at + size],
                    NT,
                    preferred_element_type=jnp.float32,
                )
                for g in range(2)
            ]
            act = (up + 1.0) * gate * jax.nn.sigmoid(1.702 * gate)
            hidden[:, at : at + size] = act.astype(jnp.bfloat16)
        if e:
            copies[e - 1][1].wait()
        for at, size in chunks_of(width, 768):
            part = jnp.dot(
                hidden[...], dn[:, at : at + size], preferred_element_type=jnp.float32
            ).astype(jnp.bfloat16)
            for b in range(blocks):
                y_refs[b][rows, at : at + size] = part[b * CAP : (b + 1) * CAP]


def combine_kernel(cols, pieces, high_ref, low_ref, *refs):
    ins, refs = refs[:pieces], refs[pieces:]
    own_ref, out_refs, flat, mixed = refs[0], refs[1:cols], refs[-2], refs[-1]
    col = lax.axis_index("col")
    at = 0
    for piece in ins:
        flat[at : at + piece.shape[0]] = piece[...]
        at += piece.shape[0]
    y = flat[...]
    total = lax.dot_general(high_ref[...], y, TN, preferred_element_type=jnp.float32)
    total += lax.dot_general(low_ref[...], y, TN, preferred_element_type=jnp.float32)
    width = own_ref.shape[1]
    for p in range(cols):
        mixed[p] = total[:, p * width : (p + 1) * width]
    own_ref[...] = mixed[col]
    for j in range(1, cols):
        out_refs[j - 1][...] = mixed[dest(col, j, cols)].astype(jnp.bfloat16)


def params(mib):
    return pltpu.CompilerParams(vmem_limit_bytes=mib << 20)


def layer(tokens, route_ids, route_weights, expert_gate_up, expert_down):
    rows, cols = lax.axis_size("row"), lax.axis_size("col")
    pair = 2 if rows % 2 == 0 else 1
    chips = rows // pair
    toks, part_width = tokens.shape
    exp_dev, width, _, hid = expert_gate_up.shape
    slots = exp_dev * rows * CAP
    block = exp_dev * CAP
    bf16, f32 = jnp.bfloat16, jnp.float32
    shape = jax.ShapeDtypeStruct

    def over_col(x, j):
        return lax.ppermute(x, "col", [(i, dest(i, j, cols)) for i in range(cols)])

    def over_chips(x, j, back=False):
        to = source if back else dest
        perm = [
            (c * pair + k, to(c, j, chips) * pair + k)
            for c in range(chips)
            for k in range(pair)
        ]
        return lax.ppermute(x, "row", perm)

    def over_cores(x):
        return lax.ppermute(x, "row", [(i, i ^ 1) for i in range(rows)])

    def hold(x):
        return pltpu.with_memory_space_constraint(x, pltpu.HBM)

    far = range(cols - 1, 0, -1)
    arrived = {j: over_col(tokens, j) for j in far}
    parts = [tokens] + [arrived[j] for j in range(1, cols)]

    gate_up = hold(jnp.transpose(expert_gate_up, (0, 2, 3, 1)))
    expert_down = hold(expert_down)
    held = [((2, hid, width), bf16), ((hid, width), bf16)]
    place, high, low, gu, dn = pl.pallas_call(
        functools.partial(route_kernel, rows, exp_dev),
        out_shape=[shape((slots, toks), bf16)] * 3 + [pltpu.VMEM(*h) for h in held],
        in_specs=[HBM] * 4,
        out_specs=[VMEM] * 5,
        scratch_shapes=[
            pltpu.VMEM(route_ids.shape[::-1], route_ids.dtype),
            pltpu.VMEM(route_weights.shape[::-1], f32),
            pltpu.SemaphoreType.DMA((4,)),
        ],
        compiler_params=params(4),
        name="route",
    )(hold(route_ids.T), hold(route_weights.T), gate_up, expert_down)

    outs = chips + (pair - 1)
    dispatched = pl.pallas_call(
        functools.partial(dispatch_kernel, cols, outs),
        out_shape=[shape((block, width), bf16)] * chips
        + [shape((chips * block, width), bf16)] * (pair - 1),
        in_specs=[VMEM] * (1 + cols),
        out_specs=[VMEM] * outs,
        scratch_shapes=[pltpu.VMEM((toks, width), f32)],
        compiler_params=params(8),
        name="dispatch",
    )(place, *parts)

    keep, give = dispatched[:chips], dispatched[chips:]
    others = range(1, chips)
    inputs = [keep[0]] + [over_chips(keep[j], j) for j in others]
    if pair == 2:
        got = over_cores(give[0])
        got = [got[j * block : (j + 1) * block] for j in range(chips)]
        inputs += [got[0]] + [over_chips(got[j], j) for j in others]

    n = len(inputs)
    ys = pl.pallas_call(
        functools.partial(experts_kernel, exp_dev, n),
        out_shape=[shape((block, width), bf16)] * n,
        in_specs=[HBM] * 2 + [VMEM] * (2 + n),
        out_specs=[VMEM] * n,
        scratch_shapes=[
            pltpu.VMEM((n * CAP, width), bf16),
            pltpu.VMEM((n * CAP, hid), bf16),
        ]
        + [pltpu.VMEM(*h) for h in held] * (exp_dev - 1)
        + [pltpu.SemaphoreType.DMA((2 * exp_dev,))],
        compiler_params=params(24),
        cost_estimate=pl.CostEstimate(
            flops=6 * exp_dev * n * CAP * width * hid,
            bytes_accessed=6 * exp_dev * width * hid,
            transcendentals=exp_dev * n * CAP * hid,
        ),
        name="experts",
    )(gate_up, expert_down, gu, dn, *inputs)

    terms = []
    if pair == 2:
        back = [over_chips(ys[chips + j], j, True) for j in others]
        passed = jnp.concatenate([ys[chips], *back], axis=0)
        terms = [over_cores(passed)]
    near = [over_chips(ys[j], j, True) for j in others]
    terms = [ys[0], *near, *terms]

    own, *leaving = pl.pallas_call(
        functools.partial(combine_kernel, cols, len(terms)),
        out_shape=[shape((toks, part_width), f32)]
        + [shape((toks, part_width), bf16)] * (cols - 1),
        in_specs=[VMEM] * (2 + len(terms)),
        out_specs=[VMEM] * cols,
        scratch_shapes=[
            pltpu.VMEM((slots, width), bf16),
            pltpu.VMEM((cols, toks, part_width), f32),
        ],
        compiler_params=params(16),
        name="combine",
    )(high, low, *terms)
    total = own
    for j in far:
        total = total + over_col(leaving[j - 1], j).astype(f32)
    return total.astype(bf16)


def solution(mesh):
    return jax.shard_map(
        layer,
        mesh=mesh,
        in_specs=(
            P("row", "col"),
            P("row", None),
            P("row", None),
            P("row", None, None, "col"),
            P("row", "col", None),
        ),
        out_specs=P("row", "col"),
        check_vma=False,
    )
```

time: 53.7 us -> 59.2 us (1.10)
  waiting for transfers between devices: 11.4 us -> 18.5 us
  local copies, waits for them, and re-layouts: 1.46 us -> 0.03 us
  Pallas kernels: 13.9 us -> 15.3 us
  starting transfers between devices: 25.7 us -> 24.5 us
    ppermute x12, waiting for transfers between devices: 4.74 us -> 14 us  [over_chips(): return lax.ppermute(x, 'row', perm)]
    ppermute x4 -> x2, waiting for transfers between devices: 2.3 us -> 0.01 us  [over_cores(): return lax.ppermute(x, 'row', [(i, i ^ 1) for i in range(rows)])]
    pallas_call x5 -> x4, Pallas kernels: 13.9 us -> 15.3 us  [the longest x1 9.63 us: layer(): pl.pallas_call(functools.partial(experts_kernel, exp_dev, n), out_shape=[...]
    unnamed x6 -> x2, local copies, waits for them, and re-layouts: 1.37 us -> 0.01 us
    ppermute x12, starting transfers between devices: 14.9 us -> 14.2 us  [over_chips(): return lax.ppermute(x, 'row', perm)]
  transfers between devices with their start and end apart: 22 -> 20, of which waited for: 8 -> 10; matrix products, arithmetic and copies ran while one was open for 0% -> 0% of each run, Pallas kernels for 24% -> 8%
where the time goes in v3:
time: 59.2 us; the launch traced here: 59 us
  starting transfers between devices  24.5 us (41%)
  waiting for transfers between devices  18.5 us (31%)
  Pallas kernels  15.3 us (26%)
  other arithmetic  0.67 us (1%)
    ppermute x12, starting transfers between devices, over_chips(): return lax.ppermute(x, 'row', perm)  14.2 us
    ppermute x12, waiting for transfers between devices, over_chips(): return lax.ppermute(x, 'row', perm)  14 us
    ppermute x6, starting transfers between devices, over_col(): return lax.ppermute(x, 'col', [(i, dest(i, j, cols)) for i in range(cols)])  10.1 us
    pallas_call x1, Pallas kernels, layer(): pl.pallas_call(functools.partial(experts_kernel, exp_dev, n), out_shape=[...  9.63 us
    pallas_call x1, Pallas kernels, layer(): pl.pallas_call(functools.partial(route_kernel, rows, exp_dev), out_shape=...  4.76 us
    ppermute x6, waiting for transfers between devices, over_col(): return lax.ppermute(x, 'col', [(i, dest(i, j, cols)) for i in range(cols)])  4.47 us
  transfers between devices with their start and end apart: 20, of which 10 were waited for; matrix products, arithmetic and copies ran while one was open for 0% of the time, Pallas kernels for 8%

profile of v3, /device:TPU:0, one launch (start us, length us, event | category | flops | bytes accessed | tf_op | source)
XLA Modules:
  0.0 59.0 jit_solution(3539754765621870753)
XLA Ops:
  0.0 4.1 %collective-permute-start.1 = (bf16[32,720]{1,0:T(8,128)(2,1)}, bf16[32,720]{1,0:T(8,128)(2,1)S(1)}, u32[]{:S(2)}, u32[]{:S(2)}) collective-permute-start(bf16[32,720]{1,0:T(8,128)(2,1)} %refs_0_.1), channel_id=1, source_target_pairs={{0,2},{1,3},{2,0},{3,1},{4,6},{5,7},{6,4},{7,5},{8,10},{9,11},{10,... | collective-permute-start | bytes 138248 | tf_op jit(solution)/shard_map/ppermute | solution.py:181
  4.1 1.6 %collective-permute-start = (bf16[32,720]{1,0:T(8,128)(2,1)}, bf16[32,720]{1,0:T(8,128)(2,1)S(1)}, u32[]{:S(2)}, u32[]{:S(2)}) collective-permute-start(bf16[32,720]{1,0:T(8,128)(2,1)} %refs_0_.1), channel_id=1, source_target_pairs={{0,1},{1,0},{2,3},{3,2},{4,5},{5,4},{6,7},{7,6},{8,9},{9,8},{10,11... | collective-permute-start | bytes 138248 | tf_op jit(solution)/shard_map/ppermute | solution.py:181
  5.6 4.8 %route.1 = (bf16[128,32]{1,0:T(8,128)(2,1)S(1)}, bf16[128,32]{1,0:T(8,128)(2,1)S(1)}, bf16[128,32]{1,0:T(8,128)(2,1)S(1)}, bf16[2,720,2880]{2,1,0:T(8,128)(2,1)S(1)}, bf16[720,2880]{1,0:T(8,128)(2,1)S(1)}) custom-call(s32[4,32]{1,0:T(4,128)} %bitcast.5, f32[4,32]{1,0:T(4,128)} %bitcast.6, bf16[2,2,720,2880]{3,2,1,0:T(8,128)(2,1)} %bitcast.3, ...), custom_call_target="tpu_custom_call" | custom-call | tf_op jit(solution)/shard_map/route/pallas_call | solution.py:205
  10.4 1.3 %collective-permute-done.2.refs_3_ = bf16[32,720]{1,0:T(8,128)(2,1)S(1)} collective-permute-done((bf16[32,720]{1,0:T(8,128)(2,1)}, bf16[32,720]{1,0:T(8,128)(2,1)S(1)}, u32[]{:S(2)}, u32[]{:S(2)}) %collective-permute-start.2) | collective-permute-done | bytes 46112 | tf_op jit(solution)/shard_map/ppermute | solution.py:181
  12.2 1.6 %collective-permute-start.3 = (bf16[16,2880]{1,0:T(8,128)(2,1)S(1)}, bf16[16,2880]{1,0:T(8,128)(2,1)S(1)}, u32[]{:S(2)}, u32[]{:S(2)}) collective-permute-start(bf16[16,2880]{1,0:T(8,128)(2,1)S(1)} %get-tuple-element.33), channel_id=1, source_target_pairs={{0,8},{4,12},{8,0},{12,4},{16,24},{20,28},{24,16},{28,20},{1,9},{5... | collective-permute-start | bytes 276488 | tf_op jit(solution)/shard_map/ppermute | solution.py:190
  13.8 1.5 %collective-permute-start.4 = (bf16[16,2880]{1,0:T(8,128)(2,1)S(1)}, bf16[16,2880]{1,0:T(8,128)(2,1)S(1)}, u32[]{:S(2)}, u32[]{:S(2)}) collective-permute-start(bf16[16,2880]{1,0:T(8,128)(2,1)S(1)} %get-tuple-element.34), channel_id=1, source_target_pairs={{0,16},{4,20},{8,24},{12,28},{16,0},{20,4},{24,8},{28,12},{1,17},{... | collective-permute-start | bytes 276488 | tf_op jit(solution)/shard_map/ppermute | solution.py:190
  15.8 2.5 %collective-permute-start.9 = (bf16[16,2880]{1,0:T(8,128)(2,1)S(1)}, bf16[16,2880]{1,0:T(8,128)(2,1)S(1)}, u32[]{:S(2)}, u32[]{:S(2)}) collective-permute-start(bf16[16,2880]{1,0:T(8,128)(2,1)S(1)} %get-tuple-element.49), channel_id=1, source_target_pairs={{0,24},{4,28},{8,16},{12,20},{16,8},{20,12},{24,0},{28,4},{1,25},{... | collective-permute-start | bytes 276488 | tf_op jit(solution)/shard_map/ppermute | solution.py:190
  19.4 3.0 %collective-permute-done.4.refs_2_ = bf16[16,2880]{1,0:T(8,128)(2,1)S(1)} collective-permute-done((bf16[16,2880]{1,0:T(8,128)(2,1)S(1)}, bf16[16,2880]{1,0:T(8,128)(2,1)S(1)}, u32[]{:S(2)}, u32[]{:S(2)}) %collective-permute-start.4) | collective-permute-done | bytes 92192 | tf_op jit(solution)/shard_map/ppermute | solution.py:190
  22.4 1.3 %collective-permute-done.9.refs_7_ = bf16[16,2880]{1,0:T(8,128)(2,1)S(1)} collective-permute-done((bf16[16,2880]{1,0:T(8,128)(2,1)S(1)}, bf16[16,2880]{1,0:T(8,128)(2,1)S(1)}, u32[]{:S(2)}, u32[]{:S(2)}) %collective-permute-start.9) | collective-permute-done | bytes 92192 | tf_op jit(solution)/shard_map/ppermute | solution.py:190
  23.7 1.0 %collective-permute-done.8.refs_6_ = bf16[16,2880]{1,0:T(8,128)(2,1)S(1)} collective-permute-done((bf16[16,2880]{1,0:T(8,128)(2,1)S(1)}, bf16[16,2880]{1,0:T(8,128)(2,1)S(1)}, u32[]{:S(2)}, u32[]{:S(2)}) %collective-permute-start.8) | collective-permute-done | bytes 92192 | tf_op jit(solution)/shard_map/ppermute | solution.py:190
  24.7 9.6 %experts.1 = (bf16[16,2880]{1,0:T(8,128)(2,1)S(1)}, bf16[16,2880]{1,0:T(8,128)(2,1)S(1)}, bf16[16,2880]{1,0:T(8,128)(2,1)S(1)}, bf16[16,2880]{1,0:T(8,128)(2,1)S...) custom-call(bf16[2,2,720,2880]{3,2,1,0:T(8,128)(2,1)} %bitcast.4, ...), custom_call_target="tpu_custom_call" | custom-call | flops 1592524800 | bytes 24883200 | tf_op jit(solution)/shard_map/experts/pallas_call | solution.py:240
  34.3 1.2 %collective-permute-start.13 = (bf16[16,2880]{1,0:T(8,128)(2,1)S(1)}, bf16[16,2880]{1,0:T(8,128)(2,1)S(1)}, u32[]{:S(2)}, u32[]{:S(2)}) collective-permute-start(bf16[16,2880]{1,0:T(8,128)(2,1)S(1)} %get-tuple-element.42), channel_id=1, source_target_pairs={{0,8},{4,12},{8,0},{12,4},{16,24},{20,28},{24,16},{28,20},{1,9},{5... | collective-permute-start | bytes 276488 | tf_op jit(solution)/shard_map/ppermute | solution.py:190
  36.3 1.6 %collective-permute-start.15 = (bf16[16,2880]{1,0:T(8,128)(2,1)S(1)}, bf16[16,2880]{1,0:T(8,128)(2,1)S(1)}, u32[]{:S(2)}, u32[]{:S(2)}) collective-permute-start(bf16[16,2880]{1,0:T(8,128)(2,1)S(1)} %get-tuple-element.44), channel_id=1, source_target_pairs={{0,24},{4,28},{8,16},{12,20},{16,8},{20,12},{24,0},{28,4},{1,25},{... | collective-permute-start | bytes 276488 | tf_op jit(solution)/shard_map/ppermute | solution.py:190
  37.9 1.1 %collective-permute-done.13 = bf16[16,2880]{1,0:T(8,128)(2,1)S(1)} collective-permute-done((bf16[16,2880]{1,0:T(8,128)(2,1)S(1)}, bf16[16,2880]{1,0:T(8,128)(2,1)S(1)}, u32[]{:S(2)}, u32[]{:S(2)}) %collective-permute-start.13) | collective-permute-done | bytes 92192 | tf_op jit(solution)/shard_map/ppermute | solution.py:190
  39.0 3.1 %collective-permute-done.14 = bf16[16,2880]{1,0:T(8,128)(2,1)S(1)} collective-permute-done((bf16[16,2880]{1,0:T(8,128)(2,1)S(1)}, bf16[16,2880]{1,0:T(8,128)(2,1)S(1)}, u32[]{:S(2)}, u32[]{:S(2)}) %collective-permute-start.14) | collective-permute-done | bytes 92192 | tf_op jit(solution)/shard_map/ppermute | solution.py:190
  42.2 1.2 %collective-permute-start.10 = (bf16[16,2880]{1,0:T(8,128)(2,1)S(1)}, bf16[16,2880]{1,0:T(8,128)(2,1)S(1)}, u32[]{:S(2)}, u32[]{:S(2)}) collective-permute-start(bf16[16,2880]{1,0:T(8,128)(2,1)S(1)} %get-tuple-element.38), channel_id=1, source_target_pairs={{0,8},{4,12},{8,0},{12,4},{16,24},{20,28},{24,16},{28,20},{1,9},{5... | collective-permute-start | bytes 276488 | tf_op jit(solution)/shard_map/ppermute | solution.py:190
  43.5 1.1 %collective-permute-start.11 = (bf16[16,2880]{1,0:T(8,128)(2,1)S(1)}, bf16[16,2880]{1,0:T(8,128)(2,1)S(1)}, u32[]{:S(2)}, u32[]{:S(2)}) collective-permute-start(bf16[16,2880]{1,0:T(8,128)(2,1)S(1)} %get-tuple-element.39), channel_id=1, source_target_pairs={{0,16},{4,20},{8,24},{12,28},{16,0},{20,4},{24,8},{28,12},{1,17},{... | collective-permute-start | bytes 276488 | tf_op jit(solution)/shard_map/ppermute | solution.py:190
  44.6 1.2 %collective-permute-start.12 = (bf16[16,2880]{1,0:T(8,128)(2,1)S(1)}, bf16[16,2880]{1,0:T(8,128)(2,1)S(1)}, u32[]{:S(2)}, u32[]{:S(2)}) collective-permute-start(bf16[16,2880]{1,0:T(8,128)(2,1)S(1)} %get-tuple-element.40), channel_id=1, source_target_pairs={{0,24},{4,28},{8,16},{12,20},{16,8},{20,12},{24,0},{28,4},{1,25},{... | collective-permute-start | bytes 276488 | tf_op jit(solution)/shard_map/ppermute | solution.py:190
  45.8 1.6 %collective-permute-done.10.refs_1_ = bf16[16,2880]{1,0:T(8,128)(2,1)S(1)} collective-permute-done((bf16[16,2880]{1,0:T(8,128)(2,1)S(1)}, bf16[16,2880]{1,0:T(8,128)(2,1)S(1)}, u32[]{:S(2)}, u32[]{:S(2)}) %collective-permute-start.10) | collective-permute-done | bytes 92192 | tf_op jit(solution)/shard_map/ppermute | solution.py:190
  47.3 2.9 %collective-permute-done.11.refs_2_ = bf16[16,2880]{1,0:T(8,128)(2,1)S(1)} collective-permute-done((bf16[16,2880]{1,0:T(8,128)(2,1)S(1)}, bf16[16,2880]{1,0:T(8,128)(2,1)S(1)}, u32[]{:S(2)}, u32[]{:S(2)}) %collective-permute-start.11) | collective-permute-done | bytes 92192 | tf_op jit(solution)/shard_map/ppermute | solution.py:190
  50.8 2.6 %collective-permute-start.17 = (bf16[32,720]{1,0:T(8,128)(2,1)S(1)}, bf16[32,720]{1,0:T(8,128)(2,1)S(1)}, u32[]{:S(2)}, u32[]{:S(2)}) collective-permute-start(bf16[32,720]{1,0:T(8,128)(2,1)S(1)} %get-tuple-element.46), channel_id=1, source_target_pairs={{0,3},{1,2},{2,1},{3,0},{4,7},{5,6},{6,5},{7,4},{8,11},{9,10},{10,... | collective-permute-start | bytes 138248 | tf_op jit(solution)/shard_map/ppermute | solution.py:181
  53.4 1.8 %collective-permute-start.19 = (bf16[32,720]{1,0:T(8,128)(2,1)S(1)}, bf16[32,720]{1,0:T(8,128)(2,1)S(1)}, u32[]{:S(2)}, u32[]{:S(2)}) collective-permute-start(bf16[32,720]{1,0:T(8,128)(2,1)S(1)} %get-tuple-element.48), channel_id=1, source_target_pairs={{0,1},{1,0},{2,3},{3,2},{4,5},{5,4},{6,7},{7,6},{8,9},{9,8},{10,11... | collective-permute-start | bytes 138248 | tf_op jit(solution)/shard_map/ppermute | solution.py:181
  55.2 1.8 %collective-permute-done.17 = bf16[32,720]{1,0:T(8,128)(2,1)S(1)} collective-permute-done((bf16[32,720]{1,0:T(8,128)(2,1)S(1)}, bf16[32,720]{1,0:T(8,128)(2,1)S(1)}, u32[]{:S(2)}, u32[]{:S(2)}) %collective-permute-start.17) | collective-permute-done | bytes 46112 | tf_op jit(solution)/shard_map/ppermute | solution.py:181
  57.0 1.3 %collective-permute-done.18 = bf16[32,720]{1,0:T(8,128)(2,1)S(1)} collective-permute-done((bf16[32,720]{1,0:T(8,128)(2,1)S(1)}, bf16[32,720]{1,0:T(8,128)(2,1)S(1)}, u32[]{:S(2)}, u32[]{:S(2)}) %collective-permute-start.18) | collective-permute-done | bytes 46112 | tf_op jit(solution)/shard_map/ppermute | solution.py:181
  (25 shorter events, 4.1 us)
Async XLA Ops:
  0.0 10.4 %collective-permute-start.1 = (bf16[32,720]{1,0:T(8,128)(2,1)}, bf16[32,720]{1,0:T(8,128)(2,1)S(1)}, u32[]{:S(2)}, u32[]{:S(2)}) collective-permute-start(bf16[32,720]{1,0:T(8,128)(2,1)} %refs_0_.1), channel_id=1, source_target_pairs={{0,2},{1,3},{2,0},{3,1},{4,6},{5,7},{6,4},{7,5},{8,10},{9,11},{10,... | collective-permute-start | bytes 138248 | tf_op jit(solution)/shard_map/ppermute | solution.py:181
  4.1 6.4 %collective-permute-start = (bf16[32,720]{1,0:T(8,128)(2,1)}, bf16[32,720]{1,0:T(8,128)(2,1)S(1)}, u32[]{:S(2)}, u32[]{:S(2)}) collective-permute-start(bf16[32,720]{1,0:T(8,128)(2,1)} %refs_0_.1), channel_id=1, source_target_pairs={{0,1},{1,0},{2,3},{3,2},{4,5},{5,4},{6,7},{7,6},{8,9},{9,8},{10,11... | collective-permute-start | bytes 138248 | tf_op jit(solution)/shard_map/ppermute | solution.py:181
  5.6 6.1 %collective-permute-start.2 = (bf16[32,720]{1,0:T(8,128)(2,1)}, bf16[32,720]{1,0:T(8,128)(2,1)S(1)}, u32[]{:S(2)}, u32[]{:S(2)}) collective-permute-start(bf16[32,720]{1,0:T(8,128)(2,1)} %refs_0_.1), channel_id=1, source_target_pairs={{0,3},{1,2},{2,1},{3,0},{4,7},{5,6},{6,5},{7,4},{8,11},{9,10},{10,... | collective-permute-start | bytes 138248 | tf_op jit(solution)/shard_map/ppermute | solution.py:181
  5.6 6.1 %copy-start = (bf16[32,720]{1,0:T(8,128)(2,1)S(1)}, bf16[32,720]{1,0:T(8,128)(2,1)}, u32[]{:S(2)}) copy-start(bf16[32,720]{1,0:T(8,128)(2,1)} %refs_0_.1) | copy-start | bytes 138244
  12.1 3.6 %collective-permute-start.6 = (bf16[64,2880]{1,0:T(8,128)(2,1)S(1)}, bf16[64,2880]{1,0:T(8,128)(2,1)S(1)}, u32[]{:S(2)}, u32[]{:S(2)}) collective-permute-start(bf16[64,2880]{1,0:T(8,128)(2,1)S(1)} %get-tuple-element.36), channel_id=1, source_target_pairs={{0,4},{4,0},{8,12},{12,8},{16,20},{20,16},{24,28},{28,24},{1,5},{5... | collective-permute-start | bytes 1105928 | tf_op jit(solution)/shard_map/ppermute | solution.py:193
  12.2 6.6 %collective-permute-start.3 = (bf16[16,2880]{1,0:T(8,128)(2,1)S(1)}, bf16[16,2880]{1,0:T(8,128)(2,1)S(1)}, u32[]{:S(2)}, u32[]{:S(2)}) collective-permute-start(bf16[16,2880]{1,0:T(8,128)(2,1)S(1)} %get-tuple-element.33), channel_id=1, source_target_pairs={{0,8},{4,12},{8,0},{12,4},{16,24},{20,28},{24,16},{28,20},{1,9},{5... | collective-permute-start | bytes 276488 | tf_op jit(solution)/shard_map/ppermute | solution.py:190
  13.8 8.6 %collective-permute-start.4 = (bf16[16,2880]{1,0:T(8,128)(2,1)S(1)}, bf16[16,2880]{1,0:T(8,128)(2,1)S(1)}, u32[]{:S(2)}, u32[]{:S(2)}) collective-permute-start(bf16[16,2880]{1,0:T(8,128)(2,1)S(1)} %get-tuple-element.34), channel_id=1, source_target_pairs={{0,16},{4,20},{8,24},{12,28},{16,0},{20,4},{24,8},{28,12},{1,17},{... | collective-permute-start | bytes 276488 | tf_op jit(solution)/shard_map/ppermute | solution.py:190
  15.3 7.1 %collective-permute-start.5 = (bf16[16,2880]{1,0:T(8,128)(2,1)S(1)}, bf16[16,2880]{1,0:T(8,128)(2,1)S(1)}, u32[]{:S(2)}, u32[]{:S(2)}) collective-permute-start(bf16[16,2880]{1,0:T(8,128)(2,1)S(1)} %get-tuple-element.35), channel_id=1, source_target_pairs={{0,24},{4,28},{8,16},{12,20},{16,8},{20,12},{24,0},{28,4},{1,25},{... | collective-permute-start | bytes 276488 | tf_op jit(solution)/shard_map/ppermute | solution.py:190
  15.8 7.9 %collective-permute-start.9 = (bf16[16,2880]{1,0:T(8,128)(2,1)S(1)}, bf16[16,2880]{1,0:T(8,128)(2,1)S(1)}, u32[]{:S(2)}, u32[]{:S(2)}) collective-permute-start(bf16[16,2880]{1,0:T(8,128)(2,1)S(1)} %get-tuple-element.49), channel_id=1, source_target_pairs={{0,24},{4,28},{8,16},{12,20},{16,8},{20,12},{24,0},{28,4},{1,25},{... | collective-permute-start | bytes 276488 | tf_op jit(solution)/shard_map/ppermute | solution.py:190
  18.3 6.4 %collective-permute-start.8 = (bf16[16,2880]{1,0:T(8,128)(2,1)S(1)}, bf16[16,2880]{1,0:T(8,128)(2,1)S(1)}, u32[]{:S(2)}, u32[]{:S(2)}) collective-permute-start(bf16[16,2880]{1,0:T(8,128)(2,1)S(1)} %get-tuple-element.50), channel_id=1, source_target_pairs={{0,16},{4,20},{8,24},{12,28},{16,0},{20,4},{24,8},{28,12},{1,17},{... | collective-permute-start | bytes 276488 | tf_op jit(solution)/shard_map/ppermute | solution.py:190
  18.8 5.9 %collective-permute-start.7 = (bf16[16,2880]{1,0:T(8,128)(2,1)S(1)}, bf16[16,2880]{1,0:T(8,128)(2,1)S(1)}, u32[]{:S(2)}, u32[]{:S(2)}) collective-permute-start(bf16[16,2880]{1,0:T(8,128)(2,1)S(1)} %get-tuple-element.51), channel_id=1, source_target_pairs={{0,8},{4,12},{8,0},{12,4},{16,24},{20,28},{24,16},{28,20},{1,9},{5... | collective-permute-start | bytes 276488 | tf_op jit(solution)/shard_map/ppermute | solution.py:190
  34.3 4.6 %collective-permute-start.13 = (bf16[16,2880]{1,0:T(8,128)(2,1)S(1)}, bf16[16,2880]{1,0:T(8,128)(2,1)S(1)}, u32[]{:S(2)}, u32[]{:S(2)}) collective-permute-start(bf16[16,2880]{1,0:T(8,128)(2,1)S(1)} %get-tuple-element.42), channel_id=1, source_target_pairs={{0,8},{4,12},{8,0},{12,4},{16,24},{20,28},{24,16},{28,20},{1,9},{5... | collective-permute-start | bytes 276488 | tf_op jit(solution)/shard_map/ppermute | solution.py:190
  35.5 6.6 %collective-permute-start.14 = (bf16[16,2880]{1,0:T(8,128)(2,1)S(1)}, bf16[16,2880]{1,0:T(8,128)(2,1)S(1)}, u32[]{:S(2)}, u32[]{:S(2)}) collective-permute-start(bf16[16,2880]{1,0:T(8,128)(2,1)S(1)} %get-tuple-element.43), channel_id=1, source_target_pairs={{0,16},{4,20},{8,24},{12,28},{16,0},{20,4},{24,8},{28,12},{1,17},{... | collective-permute-start | bytes 276488 | tf_op jit(solution)/shard_map/ppermute | solution.py:190
  36.3 5.8 %collective-permute-start.15 = (bf16[16,2880]{1,0:T(8,128)(2,1)S(1)}, bf16[16,2880]{1,0:T(8,128)(2,1)S(1)}, u32[]{:S(2)}, u32[]{:S(2)}) collective-permute-start(bf16[16,2880]{1,0:T(8,128)(2,1)S(1)} %get-tuple-element.44), channel_id=1, source_target_pairs={{0,24},{4,28},{8,16},{12,20},{16,8},{20,12},{24,0},{28,4},{1,25},{... | collective-permute-start | bytes 276488 | tf_op jit(solution)/shard_map/ppermute | solution.py:190
  42.2 8.1 %collective-permute-start.16 = (bf16[64,2880]{1,0:T(8,128)(2,1)S(1)}, bf16[64,2880]{1,0:T(8,128)(2,1)S(1)}, u32[]{:S(2)}, u32[]{:S(2)}) collective-permute-start(bf16[64,2880]{1,0:T(8,128)(2,1)S(1)} %pad_maximum_fusion), channel_id=1, source_target_pairs={{0,4},{4,0},{8,12},{12,8},{16,20},{20,16},{24,28},{28,24},{1,5},{5... | collective-permute-start | bytes 1105928 | tf_op jit(solution)/shard_map/ppermute | solution.py:193
  42.2 5.1 %collective-permute-start.10 = (bf16[16,2880]{1,0:T(8,128)(2,1)S(1)}, bf16[16,2880]{1,0:T(8,128)(2,1)S(1)}, u32[]{:S(2)}, u32[]{:S(2)}) collective-permute-start(bf16[16,2880]{1,0:T(8,128)(2,1)S(1)} %get-tuple-element.38), channel_id=1, source_target_pairs={{0,8},{4,12},{8,0},{12,4},{16,24},{20,28},{24,16},{28,20},{1,9},{5... | collective-permute-start | bytes 276488 | tf_op jit(solution)/shard_map/ppermute | solution.py:190
  43.5 6.8 %collective-permute-start.11 = (bf16[16,2880]{1,0:T(8,128)(2,1)S(1)}, bf16[16,2880]{1,0:T(8,128)(2,1)S(1)}, u32[]{:S(2)}, u32[]{:S(2)}) collective-permute-start(bf16[16,2880]{1,0:T(8,128)(2,1)S(1)} %get-tuple-element.39), channel_id=1, source_target_pairs={{0,16},{4,20},{8,24},{12,28},{16,0},{20,4},{24,8},{28,12},{1,17},{... | collective-permute-start | bytes 276488 | tf_op jit(solution)/shard_map/ppermute | solution.py:190
  44.6 5.7 %collective-permute-start.12 = (bf16[16,2880]{1,0:T(8,128)(2,1)S(1)}, bf16[16,2880]{1,0:T(8,128)(2,1)S(1)}, u32[]{:S(2)}, u32[]{:S(2)}) collective-permute-start(bf16[16,2880]{1,0:T(8,128)(2,1)S(1)} %get-tuple-element.40), channel_id=1, source_target_pairs={{0,24},{4,28},{8,16},{12,20},{16,8},{20,12},{24,0},{28,4},{1,25},{... | collective-permute-start | bytes 276488 | tf_op jit(solution)/shard_map/ppermute | solution.py:190
  50.8 6.3 %collective-permute-start.17 = (bf16[32,720]{1,0:T(8,128)(2,1)S(1)}, bf16[32,720]{1,0:T(8,128)(2,1)S(1)}, u32[]{:S(2)}, u32[]{:S(2)}) collective-permute-start(bf16[32,720]{1,0:T(8,128)(2,1)S(1)} %get-tuple-element.46), channel_id=1, source_target_pairs={{0,3},{1,2},{2,1},{3,0},{4,7},{5,6},{6,5},{7,4},{8,11},{9,10},{10,... | collective-permute-start | bytes 138248 | tf_op jit(solution)/shard_map/ppermute | solution.py:181
  53.4 5.0 %collective-permute-start.18 = (bf16[32,720]{1,0:T(8,128)(2,1)S(1)}, bf16[32,720]{1,0:T(8,128)(2,1)S(1)}, u32[]{:S(2)}, u32[]{:S(2)}) collective-permute-start(bf16[32,720]{1,0:T(8,128)(2,1)S(1)} %get-tuple-element.47), channel_id=1, source_target_pairs={{0,2},{1,3},{2,0},{3,1},{4,6},{5,7},{6,4},{7,5},{8,10},{9,11},{10,... | collective-permute-start | bytes 138248 | tf_op jit(solution)/shard_map/ppermute | solution.py:181
  53.4 5.0 %collective-permute-start.19 = (bf16[32,720]{1,0:T(8,128)(2,1)S(1)}, bf16[32,720]{1,0:T(8,128)(2,1)S(1)}, u32[]{:S(2)}, u32[]{:S(2)}) collective-permute-start(bf16[32,720]{1,0:T(8,128)(2,1)S(1)} %get-tuple-element.48), channel_id=1, source_target_pairs={{0,1},{1,0},{2,3},{3,2},{4,5},{5,4},{6,7},{7,6},{8,9},{9,8},{10,11... | collective-permute-start | bytes 138248 | tf_op jit(solution)/shard_map/ppermute | solution.py:181

commit v4 on v2

--- a/solution.py
+++ b/solution.py
@@ -7,6 +7,7 @@
 from jax.experimental.pallas import tpu as pltpu
 from jax.sharding import PartitionSpec as P
 
+
 CAP = 8
 NT = (((1,), (1,)), ((), ()))
 TN = (((0,), (0,)), ((), ()))
@@ -33,10 +34,14 @@
     ]
 
 
-def route_kernel(rows, exp_dev, ids_ref, w_ref, gu_hbm, dn_hbm, *refs):
-    place_ref, high_ref, low_ref, gu, dn, *_, sems = refs
+def route_kernel(rows, exp_dev, ids_hbm, w_hbm, gu_hbm, dn_hbm, *refs):
+    place_ref, high_ref, low_ref, gu, dn, *_, ids_ref, w_ref, sems = refs
+    small = [
+        pltpu.make_async_copy(ids_hbm, ids_ref, sems.at[2]),
+        pltpu.make_async_copy(w_hbm, w_ref, sems.at[3]),
+    ]
     copies = fetches(0, gu_hbm, dn_hbm, gu, dn, sems)
-    for c in copies:
+    for c in small + copies:
         c.start()
     pair = 2 if rows % 2 == 0 else 1
     chips = rows // pair
@@ -50,6 +55,8 @@
     expert = (chip * pair + core) * exp_dev + e
     hit = jnp.zeros((experts, toks), jnp.float32)
     weight = jnp.zeros((experts, toks), jnp.float32)
+    for c in small:
+        c.wait()
     for k in range(top):
         same = (ids_ref[k : k + 1, :] == expert).astype(jnp.float32)
         hit += same
@@ -96,8 +103,7 @@
 
 
 def expert_kernel(e, blocks, more, *refs):
-    gu, dn = refs[:2]
-    refs = refs[2:]
+    gu, dn, refs = refs[0], refs[1], refs[2:]
     copies = []
     if more:
         copies = fetches(e + 1, *refs[:2], *refs[-5:-3], refs[-1])
@@ -153,15 +159,11 @@
         out_refs[j - 1][...] = mixed[dest(col, j, cols)].astype(jnp.bfloat16)
 
 
-def room(held_bytes):
-    return pltpu.CompilerParams(vmem_limit_bytes=(58 << 20) - held_bytes)
-
-
 def params(mib):
     return pltpu.CompilerParams(vmem_limit_bytes=mib << 20)
 
 
-def on_device(tokens, route_ids, route_weights, expert_gate_up, expert_down):
+def layer(tokens, route_ids, route_weights, expert_gate_up, expert_down):
     rows, cols = lax.axis_size("row"), lax.axis_size("col")
     pair = 2 if rows % 2 == 0 else 1
     chips = rows // pair
@@ -186,25 +188,30 @@
     def over_cores(x):
         return lax.ppermute(x, "row", [(i, i ^ 1) for i in range(rows)])
 
-    far = list(range(cols - 1, 0, -1))
+    def hold(x):
+        return pltpu.with_memory_space_constraint(x, pltpu.HBM)
+
+    far = range(cols - 1, 0, -1)
+    others = range(1, chips)
     arrived = {j: over_col(tokens, j) for j in far}
     parts = [tokens] + [arrived[j] for j in range(1, cols)]
 
-    gate_up = pltpu.with_memory_space_constraint(
-        jnp.transpose(expert_gate_up, (0, 2, 3, 1)), pltpu.HBM
-    )
-    expert_down = pltpu.with_memory_space_constraint(expert_down, pltpu.HBM)
+    gate_up = hold(jnp.transpose(expert_gate_up, (0, 2, 3, 1)))
+    expert_down = hold(expert_down)
     held = [pltpu.VMEM((2, hid, width), bf16), pltpu.VMEM((hid, width), bf16)]
-    held_bytes = 6 * hid * width
     place, high, low, *weights = pl.pallas_call(
         functools.partial(route_kernel, rows, exp_dev),
         out_shape=[shape((slots, toks), bf16)] * 3 + held * exp_dev,
-        in_specs=[VMEM] * 2 + [HBM] * 2,
+        in_specs=[HBM] * 4,
         out_specs=[VMEM] * (3 + 2 * exp_dev),
-        scratch_shapes=[pltpu.SemaphoreType.DMA((2,))],
-        compiler_params=params(16),
+        scratch_shapes=[
+            pltpu.VMEM(route_ids.shape[::-1], route_ids.dtype),
+            pltpu.VMEM(route_weights.shape[::-1], f32),
+            pltpu.SemaphoreType.DMA((4,)),
+        ],
+        compiler_params=params(4),
         name="route",
-    )(route_ids.T, route_weights.T, gate_up, expert_down)
+    )(hold(route_ids.T), hold(route_weights.T), gate_up, expert_down)
 
     outs = exp_dev * pair
     sent = pl.pallas_call(
@@ -222,14 +229,12 @@
     for e in range(exp_dev):
         halves = [sent[e * pair].reshape(chips, CAP, width)]
         if pair == 2:
-            halves.append(over_cores(sent[e * pair + 1]).reshape(chips, CAP, width))
+            swapped = over_cores(sent[e * pair + 1])
+            halves.append(swapped.reshape(chips, CAP, width))
         blocks = [
             jnp.concatenate([h[j] for h in halves], axis=0) for j in range(chips)
         ]
-        inputs.append(
-            {0: blocks[0]}
-            | {j: over_chips(blocks[j], j) for j in range(chips - 1, 0, -1)}
-        )
+        inputs.append([blocks[0]] + [over_chips(blocks[j], j) for j in others])
     terms = []
     for e in range(exp_dev):
         more = e + 1 < exp_dev
@@ -243,24 +248,16 @@
                 pltpu.VMEM((chips * block, hid), bf16),
             ]
             + [pltpu.SemaphoreType.DMA((2,))] * more,
-            compiler_params=params(16),
+            compiler_params=params(12),
             cost_estimate=pl.CostEstimate(
                 flops=6 * chips * block * width * hid,
                 bytes_accessed=6 * width * hid,
                 transcendentals=chips * block * hid,
             ),
             input_output_aliases={4: chips, 5: chips + 1} if more else {},
-            name=f"expert{e}",
-        )(
-            *weights[:2],
-            *[gate_up, expert_down, *weights[2:4]] * more,
-            *[inputs[e][j] for j in range(chips)],
-        )
+        )(*weights[:2], *[gate_up, expert_down, *weights[2:4]] * more, *inputs[e])
         weights = [*ys[chips:], *weights[4:]]
-        back = {0: ys[0]} | {
-            j: over_chips(ys[j], j, True) for j in range(chips - 1, 0, -1)
-        }
-        got = [back[j] for j in range(chips)]
+        got = [ys[0]] + [over_chips(ys[j], j, True) for j in others]
         terms += got
         if pair == 2:
             give = jnp.concatenate([g[CAP:] for g in got], axis=0)
@@ -287,7 +284,7 @@
 
 def solution(mesh):
     return jax.shard_map(
-        on_device,
+        layer,
         mesh=mesh,
         in_specs=(
             P("row", "col"),

time: 53.7 us -> 52.4 us (0.976)
  local copies, waits for them, and re-layouts: 1.46 us -> 0.09 us
    unnamed x6 -> x2, local copies, waits for them, and re-layouts: 1.37 us -> 0.01 us
  transfers between devices with their start and end apart: 22 -> 22, of which waited for: 8 -> 9; matrix products, arithmetic and copies ran while one was open for 0% -> 0% of each run, Pallas kernels for 24% -> 25%
where the time goes in v4:
time: 52.4 us; the launch traced here: 52.3 us
  starting transfers between devices  25.5 us (49%)
  Pallas kernels  13.9 us (27%)
  waiting for transfers between devices  11.8 us (23%)
  other arithmetic  0.78 us (1%)
    ppermute x12, starting transfers between devices, over_chips(): return lax.ppermute(x, 'row', perm)  14.7 us
    ppermute x6, starting transfers between devices, over_col(): return lax.ppermute(x, 'col', [(i, dest(i, j, cols)) for i in range(cols)])  10.1 us
    pallas_call x2, Pallas kernels, layer(): pl.pallas_call(functools.partial(expert_kernel, e, chips, more), out_shap...  8.22 us
    ppermute x12, waiting for transfers between devices, over_chips(): return lax.ppermute(x, 'row', perm)  4.92 us
    pallas_call x1, Pallas kernels, layer(): pl.pallas_call(functools.partial(route_kernel, rows, exp_dev), out_shape=...  4.76 us
    ppermute x6, waiting for transfers between devices, over_col(): return lax.ppermute(x, 'col', [(i, dest(i, j, cols)) for i in range(cols)])  4.61 us
    ppermute x4, waiting for transfers between devices, over_cores(): return lax.ppermute(x, 'row', [(i, i ^ 1) for i in range(rows)])  2.3 us
  transfers between devices with their start and end apart: 22, of which 9 were waited for; matrix products, arithmetic and copies ran while one was open for 0% of the time, Pallas kernels for 25%

profile of v4, /device:TPU:0, one launch (start us, length us, event | category | flops | bytes accessed | tf_op | source)
XLA Modules:
  0.0 52.3 jit_solution(17790977520116045740)
XLA Ops:
  0.0 4.1 %collective-permute-start.1 = (bf16[32,720]{1,0:T(8,128)(2,1)}, bf16[32,720]{1,0:T(8,128)(2,1)S(1)}, u32[]{:S(2)}, u32[]{:S(2)}) collective-permute-start(bf16[32,720]{1,0:T(8,128)(2,1)} %refs_0_.1), channel_id=1, source_target_pairs={{0,2},{1,3},{2,0},{3,1},{4,6},{5,7},{6,4},{7,5},{8,10},{9,11},{10,... | collective-permute-start | bytes 138248 | tf_op jit(solution)/shard_map/ppermute | solution.py:177
  4.1 1.6 %collective-permute-start = (bf16[32,720]{1,0:T(8,128)(2,1)}, bf16[32,720]{1,0:T(8,128)(2,1)S(1)}, u32[]{:S(2)}, u32[]{:S(2)}) collective-permute-start(bf16[32,720]{1,0:T(8,128)(2,1)} %refs_0_.1), channel_id=1, source_target_pairs={{0,1},{1,0},{2,3},{3,2},{4,5},{5,4},{6,7},{7,6},{8,9},{9,8},{10,11... | collective-permute-start | bytes 138248 | tf_op jit(solution)/shard_map/ppermute | solution.py:177
  5.6 4.8 %route.1 = (bf16[128,32]{1,0:T(8,128)(2,1)S(1)}, bf16[128,32]{1,0:T(8,128)(2,1)S(1)}, bf16[128,32]{1,0:T(8,128)(2,1)S(1)}, bf16[2,720,2880]{2,1,0:T(8,128)(2,1)S...) custom-call(s32[4,32]{1,0:T(4,128)} %bitcast.5, ...), custom_call_target="tpu_custom_call" | custom-call | tf_op jit(solution)/shard_map/route/pallas_call | solution.py:202
  10.4 1.3 %collective-permute-done.2.refs_3_ = bf16[32,720]{1,0:T(8,128)(2,1)S(1)} collective-permute-done((bf16[32,720]{1,0:T(8,128)(2,1)}, bf16[32,720]{1,0:T(8,128)(2,1)S(1)}, u32[]{:S(2)}, u32[]{:S(2)}) %collective-permute-start.2) | collective-permute-done | bytes 46112 | tf_op jit(solution)/shard_map/ppermute | solution.py:177
  12.7 0.9 %collective-permute-done.3 = bf16[32,2880]{1,0:T(8,128)(2,1)S(1)} collective-permute-done((bf16[32,2880]{1,0:T(8,128)(2,1)S(1)}, bf16[32,2880]{1,0:T(8,128)(2,1)S(1)}, u32[]{:S(2)}, u32[]{:S(2)}) %collective-permute-start.3) | collective-permute-done | bytes 184352 | tf_op jit(solution)/shard_map/ppermute | solution.py:189
  13.7 1.6 %collective-permute-start.4 = (bf16[16,2880]{1,0:T(8,128)(2,1)S(1)}, bf16[16,2880]{1,0:T(8,128)(2,1)S(1)}, u32[]{:S(2)}, u32[]{:S(2)}) collective-permute-start(bf16[16,2880]{1,0:T(8,128)(2,1)S(1)} %pad_maximum_fusion.3), channel_id=1, source_target_pairs={{0,8},{4,12},{8,0},{12,4},{16,24},{20,28},{24,16},{28,20},{1,9},{5... | collective-permute-start | bytes 276488 | tf_op jit(solution)/shard_map/ppermute | solution.py:186
  15.2 1.6 %collective-permute-start.5 = (bf16[16,2880]{1,0:T(8,128)(2,1)S(1)}, bf16[16,2880]{1,0:T(8,128)(2,1)S(1)}, u32[]{:S(2)}, u32[]{:S(2)}) collective-permute-start(bf16[16,2880]{1,0:T(8,128)(2,1)S(1)} %pad_maximum_fusion.4), channel_id=1, source_target_pairs={{0,16},{4,20},{8,24},{12,28},{16,0},{20,4},{24,8},{28,12},{1,17},{... | collective-permute-start | bytes 276488 | tf_op jit(solution)/shard_map/ppermute | solution.py:186
  17.4 1.6 %collective-permute-start.12 = (bf16[16,2880]{1,0:T(8,128)(2,1)S(1)}, bf16[16,2880]{1,0:T(8,128)(2,1)S(1)}, u32[]{:S(2)}, u32[]{:S(2)}) collective-permute-start(bf16[16,2880]{1,0:T(8,128)(2,1)S(1)} %pad_maximum_fusion.7), channel_id=1, source_target_pairs={{0,8},{4,12},{8,0},{12,4},{16,24},{20,28},{24,16},{28,20},{1,9},{5... | collective-permute-start | bytes 276488 | tf_op jit(solution)/shard_map/ppermute | solution.py:186
  19.0 1.6 %collective-permute-start.13 = (bf16[16,2880]{1,0:T(8,128)(2,1)S(1)}, bf16[16,2880]{1,0:T(8,128)(2,1)S(1)}, u32[]{:S(2)}, u32[]{:S(2)}) collective-permute-start(bf16[16,2880]{1,0:T(8,128)(2,1)S(1)} %pad_maximum_fusion.8), channel_id=1, source_target_pairs={{0,16},{4,20},{8,24},{12,28},{16,0},{20,4},{24,8},{28,12},{1,17},{... | collective-permute-start | bytes 276488 | tf_op jit(solution)/shard_map/ppermute | solution.py:186
  21.4 1.7 %collective-permute-done.6.refs_9_ = bf16[16,2880]{1,0:T(8,128)(2,1)S(1)} collective-permute-done((bf16[16,2880]{1,0:T(8,128)(2,1)S(1)}, bf16[16,2880]{1,0:T(8,128)(2,1)S(1)}, u32[]{:S(2)}, u32[]{:S(2)}) %collective-permute-start.6) | collective-permute-done | bytes 92192 | tf_op jit(solution)/shard_map/ppermute | solution.py:186
  23.1 4.6 %shard_map.55 = (bf16[16,2880]{1,0:T(8,128)(2,1)S(1)}, bf16[16,2880]{1,0:T(8,128)(2,1)S(1)}, bf16[16,2880]{1,0:T(8,128)(2,1)S(1)}, bf16[16,2880]{1,0:T(8,128)(2,...) custom-call(bf16[2,720,2880]{2,1,0:T(8,128)(2,1)S(1)} %get-tuple-ele, ...), custom_call_target="tpu_custom_call", output_to_operand_aliasing={{4}: (4, {}), {5}: (5, {})} | custom-call | flops 796262400 | bytes 12441600 | tf_op jit(solution)/shard_map/pallas_call | solution.py:241
  27.7 0.9 %collective-permute-start.7 = (bf16[16,2880]{1,0:T(8,128)(2,1)S(1)}, bf16[16,2880]{1,0:T(8,128)(2,1)S(1)}, u32[]{:S(2)}, u32[]{:S(2)}) collective-permute-start(bf16[16,2880]{1,0:T(8,128)(2,1)S(1)} %get-tuple-element.40), channel_id=1, source_target_pairs={{0,8},{4,12},{8,0},{12,4},{16,24},{20,28},{24,16},{28,20},{1,9},{5... | collective-permute-start | bytes 276488 | tf_op jit(solution)/shard_map/ppermute | solution.py:186
  29.1 2.1 %collective-permute-start.9 = (bf16[16,2880]{1,0:T(8,128)(2,1)S(1)}, bf16[16,2880]{1,0:T(8,128)(2,1)S(1)}, u32[]{:S(2)}, u32[]{:S(2)}) collective-permute-start(bf16[16,2880]{1,0:T(8,128)(2,1)S(1)} %get-tuple-element.42), channel_id=1, source_target_pairs={{0,24},{4,28},{8,16},{12,20},{16,8},{20,12},{24,0},{28,4},{1,25},{... | collective-permute-start | bytes 276488 | tf_op jit(solution)/shard_map/ppermute | solution.py:186
  31.3 3.6 %shard_map.56 = (bf16[16,2880]{1,0:T(8,128)(2,1)S(1)}, bf16[16,2880]{1,0:T(8,128)(2,1)S(1)}, bf16[16,2880]{1,0:T(8,128)(2,1)S(1)}, bf16[16,2880]{1,0:T(8,128)(2,1)S(1)}) custom-call(bf16[2,720,2880]{2,1,0:T(8,128)(2,1)S(1)} %get-tuple-element.43.refs_0_, bf16[720,2880]{1,0:T(8,128)(2,1)S(1)} %get-tuple-element.44.refs_1_, ...), custom_call_target="tpu_custom_call" | custom-call | flops 796262400 | bytes 12441600 | tf_op jit(solution)/shard_map/pallas_call | solution.py:241
  34.9 0.9 %collective-permute-start.15 = (bf16[16,2880]{1,0:T(8,128)(2,1)S(1)}, bf16[16,2880]{1,0:T(8,128)(2,1)S(1)}, u32[]{:S(2)}, u32[]{:S(2)}) collective-permute-start(bf16[16,2880]{1,0:T(8,128)(2,1)S(1)} %get-tuple-element.48), channel_id=1, source_target_pairs={{0,8},{4,12},{8,0},{12,4},{16,24},{20,28},{24,16},{28,20},{1,9},{5... | collective-permute-start | bytes 276488 | tf_op jit(solution)/shard_map/ppermute | solution.py:186
  36.3 2.1 %collective-permute-start.17 = (bf16[16,2880]{1,0:T(8,128)(2,1)S(1)}, bf16[16,2880]{1,0:T(8,128)(2,1)S(1)}, u32[]{:S(2)}, u32[]{:S(2)}) collective-permute-start(bf16[16,2880]{1,0:T(8,128)(2,1)S(1)} %get-tuple-element.50), channel_id=1, source_target_pairs={{0,24},{4,28},{8,16},{12,20},{16,8},{20,12},{24,0},{28,4},{1,25},{... | collective-permute-start | bytes 276488 | tf_op jit(solution)/shard_map/ppermute | solution.py:186
  38.6 0.9 %collective-permute-done.15.refs_6_ = bf16[16,2880]{1,0:T(8,128)(2,1)S(1)} collective-permute-done((bf16[16,2880]{1,0:T(8,128)(2,1)S(1)}, bf16[16,2880]{1,0:T(8,128)(2,1)S(1)}, u32[]{:S(2)}, u32[]{:S(2)}) %collective-permute-start.15) | collective-permute-done | bytes 92192 | tf_op jit(solution)/shard_map/ppermute | solution.py:186
  39.6 0.8 %collective-permute-done.16.refs_7_ = bf16[16,2880]{1,0:T(8,128)(2,1)S(1)} collective-permute-done((bf16[16,2880]{1,0:T(8,128)(2,1)S(1)}, bf16[16,2880]{1,0:T(8,128)(2,1)S(1)}, u32[]{:S(2)}, u32[]{:S(2)}) %collective-permute-start.16) | collective-permute-done | bytes 92192 | tf_op jit(solution)/shard_map/ppermute | solution.py:186
  40.4 1.4 %collective-permute-done.17.refs_8_ = bf16[16,2880]{1,0:T(8,128)(2,1)S(1)} collective-permute-done((bf16[16,2880]{1,0:T(8,128)(2,1)S(1)}, bf16[16,2880]{1,0:T(8,128)(2,1)S(1)}, u32[]{:S(2)}, u32[]{:S(2)}) %collective-permute-start.17) | collective-permute-done | bytes 92192 | tf_op jit(solution)/shard_map/ppermute | solution.py:186
  41.9 1.4 %collective-permute-done.18.refs_9_ = bf16[32,2880]{1,0:T(8,128)(2,1)S(1)} collective-permute-done((bf16[32,2880]{1,0:T(8,128)(2,1)S(1)}, bf16[32,2880]{1,0:T(8,128)(2,1)S(1)}, u32[]{:S(2)}, u32[]{:S(2)}) %collective-permute-start.18) | collective-permute-done | bytes 184352 | tf_op jit(solution)/shard_map/ppermute | solution.py:189
  43.8 2.6 %collective-permute-start.19 = (bf16[32,720]{1,0:T(8,128)(2,1)S(1)}, bf16[32,720]{1,0:T(8,128)(2,1)S(1)}, u32[]{:S(2)}, u32[]{:S(2)}) collective-permute-start(bf16[32,720]{1,0:T(8,128)(2,1)S(1)} %get-tuple-element.52), channel_id=1, source_target_pairs={{0,3},{1,2},{2,1},{3,0},{4,7},{5,6},{6,5},{7,4},{8,11},{9,10},{10,... | collective-permute-start | bytes 138248 | tf_op jit(solution)/shard_map/ppermute | solution.py:177
  46.5 1.8 %collective-permute-start.21 = (bf16[32,720]{1,0:T(8,128)(2,1)S(1)}, bf16[32,720]{1,0:T(8,128)(2,1)S(1)}, u32[]{:S(2)}, u32[]{:S(2)}) collective-permute-start(bf16[32,720]{1,0:T(8,128)(2,1)S(1)} %get-tuple-element.54), channel_id=1, source_target_pairs={{0,1},{1,0},{2,3},{3,2},{4,5},{5,4},{6,7},{7,6},{8,9},{9,8},{10,11... | collective-permute-start | bytes 138248 | tf_op jit(solution)/shard_map/ppermute | solution.py:177
  48.3 1.7 %collective-permute-done.19 = bf16[32,720]{1,0:T(8,128)(2,1)S(1)} collective-permute-done((bf16[32,720]{1,0:T(8,128)(2,1)S(1)}, bf16[32,720]{1,0:T(8,128)(2,1)S(1)}, u32[]{:S(2)}, u32[]{:S(2)}) %collective-permute-start.19) | collective-permute-done | bytes 46112 | tf_op jit(solution)/shard_map/ppermute | solution.py:177
  50.0 1.6 %collective-permute-done.20 = bf16[32,720]{1,0:T(8,128)(2,1)S(1)} collective-permute-done((bf16[32,720]{1,0:T(8,128)(2,1)S(1)}, bf16[32,720]{1,0:T(8,128)(2,1)S(1)}, u32[]{:S(2)}, u32[]{:S(2)}) %collective-permute-start.20) | collective-permute-done | bytes 46112 | tf_op jit(solution)/shard_map/ppermute | solution.py:177
  (49 shorter events, 4.8 us)
Async XLA Ops:
  0.0 10.4 %collective-permute-start.1 = (bf16[32,720]{1,0:T(8,128)(2,1)}, bf16[32,720]{1,0:T(8,128)(2,1)S(1)}, u32[]{:S(2)}, u32[]{:S(2)}) collective-permute-start(bf16[32,720]{1,0:T(8,128)(2,1)} %refs_0_.1), channel_id=1, source_target_pairs={{0,2},{1,3},{2,0},{3,1},{4,6},{5,7},{6,4},{7,5},{8,10},{9,11},{10,... | collective-permute-start | bytes 138248 | tf_op jit(solution)/shard_map/ppermute | solution.py:177
  4.1 6.4 %collective-permute-start = (bf16[32,720]{1,0:T(8,128)(2,1)}, bf16[32,720]{1,0:T(8,128)(2,1)S(1)}, u32[]{:S(2)}, u32[]{:S(2)}) collective-permute-start(bf16[32,720]{1,0:T(8,128)(2,1)} %refs_0_.1), channel_id=1, source_target_pairs={{0,1},{1,0},{2,3},{3,2},{4,5},{5,4},{6,7},{7,6},{8,9},{9,8},{10,11... | collective-permute-start | bytes 138248 | tf_op jit(solution)/shard_map/ppermute | solution.py:177
  5.6 6.1 %collective-permute-start.2 = (bf16[32,720]{1,0:T(8,128)(2,1)}, bf16[32,720]{1,0:T(8,128)(2,1)S(1)}, u32[]{:S(2)}, u32[]{:S(2)}) collective-permute-start(bf16[32,720]{1,0:T(8,128)(2,1)} %refs_0_.1), channel_id=1, source_target_pairs={{0,3},{1,2},{2,1},{3,0},{4,7},{5,6},{6,5},{7,4},{8,11},{9,10},{10,... | collective-permute-start | bytes 138248 | tf_op jit(solution)/shard_map/ppermute | solution.py:177
  5.6 6.1 %copy-start = (bf16[32,720]{1,0:T(8,128)(2,1)S(1)}, bf16[32,720]{1,0:T(8,128)(2,1)}, u32[]{:S(2)}) copy-start(bf16[32,720]{1,0:T(8,128)(2,1)} %refs_0_.1) | copy-start | bytes 138244
  12.1 1.5 %collective-permute-start.3 = (bf16[32,2880]{1,0:T(8,128)(2,1)S(1)}, bf16[32,2880]{1,0:T(8,128)(2,1)S(1)}, u32[]{:S(2)}, u32[]{:S(2)}) collective-permute-start(bf16[32,2880]{1,0:T(8,128)(2,1)S(1)} %get-tuple-element.38), channel_id=1, source_target_pairs={{0,4},{4,0},{8,12},{12,8},{16,20},{20,16},{24,28},{28,24},{1,5},{5... | collective-permute-start | bytes 552968 | tf_op jit(solution)/shard_map/ppermute | solution.py:189
  12.2 5.2 %collective-permute-start.11 = (bf16[32,2880]{1,0:T(8,128)(2,1)S(1)}, bf16[32,2880]{1,0:T(8,128)(2,1)S(1)}, u32[]{:S(2)}, u32[]{:S(2)}) collective-permute-start(bf16[32,2880]{1,0:T(8,128)(2,1)S(1)} %get-tuple-element.46), channel_id=1, source_target_pairs={{0,4},{4,0},{8,12},{12,8},{16,20},{20,16},{24,28},{28,24},{1,5},{5... | collective-permute-start | bytes 552968 | tf_op jit(solution)/shard_map/ppermute | solution.py:189
  13.7 6.9 %collective-permute-start.4 = (bf16[16,2880]{1,0:T(8,128)(2,1)S(1)}, bf16[16,2880]{1,0:T(8,128)(2,1)S(1)}, u32[]{:S(2)}, u32[]{:S(2)}) collective-permute-start(bf16[16,2880]{1,0:T(8,128)(2,1)S(1)} %pad_maximum_fusion.3), channel_id=1, source_target_pairs={{0,8},{4,12},{8,0},{12,4},{16,24},{20,28},{24,16},{28,20},{1,9},{5... | collective-permute-start | bytes 276488 | tf_op jit(solution)/shard_map/ppermute | solution.py:186
  15.2 6.1 %collective-permute-start.5 = (bf16[16,2880]{1,0:T(8,128)(2,1)S(1)}, bf16[16,2880]{1,0:T(8,128)(2,1)S(1)}, u32[]{:S(2)}, u32[]{:S(2)}) collective-permute-start(bf16[16,2880]{1,0:T(8,128)(2,1)S(1)} %pad_maximum_fusion.4), channel_id=1, source_target_pairs={{0,16},{4,20},{8,24},{12,28},{16,0},{20,4},{24,8},{28,12},{1,17},{... | collective-permute-start | bytes 276488 | tf_op jit(solution)/shard_map/ppermute | solution.py:186
  16.8 6.2 %collective-permute-start.6 = (bf16[16,2880]{1,0:T(8,128)(2,1)S(1)}, bf16[16,2880]{1,0:T(8,128)(2,1)S(1)}, u32[]{:S(2)}, u32[]{:S(2)}) collective-permute-start(bf16[16,2880]{1,0:T(8,128)(2,1)S(1)} %pad_maximum_fusion.5), channel_id=1, source_target_pairs={{0,24},{4,28},{8,16},{12,20},{16,8},{20,12},{24,0},{28,4},{1,25},{... | collective-permute-start | bytes 276488 | tf_op jit(solution)/shard_map/ppermute | solution.py:186
  17.4 11.7 %collective-permute-start.12 = (bf16[16,2880]{1,0:T(8,128)(2,1)S(1)}, bf16[16,2880]{1,0:T(8,128)(2,1)S(1)}, u32[]{:S(2)}, u32[]{:S(2)}) collective-permute-start(bf16[16,2880]{1,0:T(8,128)(2,1)S(1)} %pad_maximum_fusion.7), channel_id=1, source_target_pairs={{0,8},{4,12},{8,0},{12,4},{16,24},{20,28},{24,16},{28,20},{1,9},{5... | collective-permute-start | bytes 276488 | tf_op jit(solution)/shard_map/ppermute | solution.py:186
  19.0 12.3 %collective-permute-start.13 = (bf16[16,2880]{1,0:T(8,128)(2,1)S(1)}, bf16[16,2880]{1,0:T(8,128)(2,1)S(1)}, u32[]{:S(2)}, u32[]{:S(2)}) collective-permute-start(bf16[16,2880]{1,0:T(8,128)(2,1)S(1)} %pad_maximum_fusion.8), channel_id=1, source_target_pairs={{0,16},{4,20},{8,24},{12,28},{16,0},{20,4},{24,8},{28,12},{1,17},{... | collective-permute-start | bytes 276488 | tf_op jit(solution)/shard_map/ppermute | solution.py:186
  20.6 10.7 %collective-permute-start.14 = (bf16[16,2880]{1,0:T(8,128)(2,1)S(1)}, bf16[16,2880]{1,0:T(8,128)(2,1)S(1)}, u32[]{:S(2)}, u32[]{:S(2)}) collective-permute-start(bf16[16,2880]{1,0:T(8,128)(2,1)S(1)} %pad_maximum_fusion.9), channel_id=1, source_target_pairs={{0,24},{4,28},{8,16},{12,20},{16,8},{20,12},{24,0},{28,4},{1,25},{... | collective-permute-start | bytes 276488 | tf_op jit(solution)/shard_map/ppermute | solution.py:186
  27.7 8.6 %collective-permute-start.7 = (bf16[16,2880]{1,0:T(8,128)(2,1)S(1)}, bf16[16,2880]{1,0:T(8,128)(2,1)S(1)}, u32[]{:S(2)}, u32[]{:S(2)}) collective-permute-start(bf16[16,2880]{1,0:T(8,128)(2,1)S(1)} %get-tuple-element.40), channel_id=1, source_target_pairs={{0,8},{4,12},{8,0},{12,4},{16,24},{20,28},{24,16},{28,20},{1,9},{5... | collective-permute-start | bytes 276488 | tf_op jit(solution)/shard_map/ppermute | solution.py:186
  28.6 9.9 %collective-permute-start.8 = (bf16[16,2880]{1,0:T(8,128)(2,1)S(1)}, bf16[16,2880]{1,0:T(8,128)(2,1)S(1)}, u32[]{:S(2)}, u32[]{:S(2)}) collective-permute-start(bf16[16,2880]{1,0:T(8,128)(2,1)S(1)} %get-tuple-element.41), channel_id=1, source_target_pairs={{0,16},{4,20},{8,24},{12,28},{16,0},{20,4},{24,8},{28,12},{1,17},{... | collective-permute-start | bytes 276488 | tf_op jit(solution)/shard_map/ppermute | solution.py:186
  29.1 9.4 %collective-permute-start.9 = (bf16[16,2880]{1,0:T(8,128)(2,1)S(1)}, bf16[16,2880]{1,0:T(8,128)(2,1)S(1)}, u32[]{:S(2)}, u32[]{:S(2)}) collective-permute-start(bf16[16,2880]{1,0:T(8,128)(2,1)S(1)} %get-tuple-element.42), channel_id=1, source_target_pairs={{0,24},{4,28},{8,16},{12,20},{16,8},{20,12},{24,0},{28,4},{1,25},{... | collective-permute-start | bytes 276488 | tf_op jit(solution)/shard_map/ppermute | solution.py:186
  34.9 4.6 %collective-permute-start.15 = (bf16[16,2880]{1,0:T(8,128)(2,1)S(1)}, bf16[16,2880]{1,0:T(8,128)(2,1)S(1)}, u32[]{:S(2)}, u32[]{:S(2)}) collective-permute-start(bf16[16,2880]{1,0:T(8,128)(2,1)S(1)} %get-tuple-element.48), channel_id=1, source_target_pairs={{0,8},{4,12},{8,0},{12,4},{16,24},{20,28},{24,16},{28,20},{1,9},{5... | collective-permute-start | bytes 276488 | tf_op jit(solution)/shard_map/ppermute | solution.py:186
  35.8 4.6 %collective-permute-start.16 = (bf16[16,2880]{1,0:T(8,128)(2,1)S(1)}, bf16[16,2880]{1,0:T(8,128)(2,1)S(1)}, u32[]{:S(2)}, u32[]{:S(2)}) collective-permute-start(bf16[16,2880]{1,0:T(8,128)(2,1)S(1)} %get-tuple-element.49), channel_id=1, source_target_pairs={{0,16},{4,20},{8,24},{12,28},{16,0},{20,4},{24,8},{28,12},{1,17},{... | collective-permute-start | bytes 276488 | tf_op jit(solution)/shard_map/ppermute | solution.py:186
  36.3 5.5 %collective-permute-start.17 = (bf16[16,2880]{1,0:T(8,128)(2,1)S(1)}, bf16[16,2880]{1,0:T(8,128)(2,1)S(1)}, u32[]{:S(2)}, u32[]{:S(2)}) collective-permute-start(bf16[16,2880]{1,0:T(8,128)(2,1)S(1)} %get-tuple-element.50), channel_id=1, source_target_pairs={{0,24},{4,28},{8,16},{12,20},{16,8},{20,12},{24,0},{28,4},{1,25},{... | collective-permute-start | bytes 276488 | tf_op jit(solution)/shard_map/ppermute | solution.py:186
  38.6 3.4 %collective-permute-start.10 = (bf16[32,2880]{1,0:T(8,128)(2,1)S(1)}, bf16[32,2880]{1,0:T(8,128)(2,1)S(1)}, u32[]{:S(2)}, u32[]{:S(2)}) collective-permute-start(bf16[32,2880]{1,0:T(8,128)(2,1)S(1)} %pad_maximum_fusion), channel_id=1, source_target_pairs={{0,4},{4,0},{8,12},{12,8},{16,20},{20,16},{24,28},{28,24},{1,5},{5... | collective-permute-start | bytes 552968 | tf_op jit(solution)/shard_map/ppermute | solution.py:189
  41.8 1.5 %collective-permute-start.18 = (bf16[32,2880]{1,0:T(8,128)(2,1)S(1)}, bf16[32,2880]{1,0:T(8,128)(2,1)S(1)}, u32[]{:S(2)}, u32[]{:S(2)}) collective-permute-start(bf16[32,2880]{1,0:T(8,128)(2,1)S(1)} %pad_maximum_fusion.1), channel_id=1, source_target_pairs={{0,4},{4,0},{8,12},{12,8},{16,20},{20,16},{24,28},{28,24},{1,5},{5... | collective-permute-start | bytes 552968 | tf_op jit(solution)/shard_map/ppermute | solution.py:189
  43.8 6.2 %collective-permute-start.19 = (bf16[32,720]{1,0:T(8,128)(2,1)S(1)}, bf16[32,720]{1,0:T(8,128)(2,1)S(1)}, u32[]{:S(2)}, u32[]{:S(2)}) collective-permute-start(bf16[32,720]{1,0:T(8,128)(2,1)S(1)} %get-tuple-element.52), channel_id=1, source_target_pairs={{0,3},{1,2},{2,1},{3,0},{4,7},{5,6},{6,5},{7,4},{8,11},{9,10},{10,... | collective-permute-start | bytes 138248 | tf_op jit(solution)/shard_map/ppermute | solution.py:177
  46.5 5.1 %collective-permute-start.20 = (bf16[32,720]{1,0:T(8,128)(2,1)S(1)}, bf16[32,720]{1,0:T(8,128)(2,1)S(1)}, u32[]{:S(2)}, u32[]{:S(2)}) collective-permute-start(bf16[32,720]{1,0:T(8,128)(2,1)S(1)} %get-tuple-element.53), channel_id=1, source_target_pairs={{0,2},{1,3},{2,0},{3,1},{4,6},{5,7},{6,4},{7,5},{8,10},{9,11},{10,... | collective-permute-start | bytes 138248 | tf_op jit(solution)/shard_map/ppermute | solution.py:177
  46.5 5.1 %collective-permute-start.21 = (bf16[32,720]{1,0:T(8,128)(2,1)S(1)}, bf16[32,720]{1,0:T(8,128)(2,1)S(1)}, u32[]{:S(2)}, u32[]{:S(2)}) collective-permute-start(bf16[32,720]{1,0:T(8,128)(2,1)S(1)} %get-tuple-element.54), channel_id=1, source_target_pairs={{0,1},{1,0},{2,3},{3,2},{4,5},{5,4},{6,7},{7,6},{8,9},{9,8},{10,11... | collective-permute-start | bytes 138248 | tf_op jit(solution)/shard_map/ppermute | solution.py:177

commit v5 on v4

--- a/solution.py
+++ b/solution.py
@@ -136,18 +136,16 @@
 
 
 def combine_kernel(exp_dev, chips, pair, cols, high_ref, low_ref, *refs):
-    per = chips + (pair - 1)
-    ins, refs = refs[: exp_dev * per], refs[exp_dev * per :]
+    ins, refs = refs[: chips + pair - 1], refs[chips + pair - 1 :]
     own_ref, out_refs, flat, mixed = refs[0], refs[1:cols], refs[-2], refs[-1]
     col = lax.axis_index("col")
-    at = 0
     for e in range(exp_dev):
-        for j in range(chips):
-            flat[at : at + CAP] = ins[e * per + j][:CAP]
-            at += CAP
-        if pair == 2:
-            flat[at : at + CAP * chips] = ins[e * per + chips][...]
-            at += CAP * chips
+        for q in range(pair):
+            for j in range(chips):
+                piece = ins[chips] if q else ins[j]
+                at = ((q * j) * exp_dev + e) * CAP
+                to = ((e * pair + q) * chips + j) * CAP
+                flat[to : to + CAP] = piece[at : at + CAP]
     y = flat[...]
     total = lax.dot_general(high_ref[...], y, TN, preferred_element_type=jnp.float32)
     total += lax.dot_general(low_ref[...], y, TN, preferred_element_type=jnp.float32)
@@ -235,7 +233,7 @@
             jnp.concatenate([h[j] for h in halves], axis=0) for j in range(chips)
         ]
         inputs.append([blocks[0]] + [over_chips(blocks[j], j) for j in others])
-    terms = []
+    made = []
     for e in range(exp_dev):
         more = e + 1 < exp_dev
         ys = pl.pallas_call(
@@ -257,11 +255,18 @@
             input_output_aliases={4: chips, 5: chips + 1} if more else {},
         )(*weights[:2], *[gate_up, expert_down, *weights[2:4]] * more, *inputs[e])
         weights = [*ys[chips:], *weights[4:]]
-        got = [ys[0]] + [over_chips(ys[j], j, True) for j in others]
-        terms += got
-        if pair == 2:
-            give = jnp.concatenate([g[CAP:] for g in got], axis=0)
-            terms.append(over_cores(give))
+        made.append(ys[:chips])
+
+    def of_core(j, q):
+        rows = [made[e][j][q * CAP : (q + 1) * CAP] for e in range(exp_dev)]
+        return jnp.concatenate(rows, axis=0)
+
+    terms = []
+    if pair == 2:
+        passed = [of_core(0, 1)] + [over_chips(of_core(j, 1), j, True) for j in others]
+        terms = [over_cores(jnp.concatenate(passed, axis=0))]
+    near = [of_core(0, 0)] + [over_chips(of_core(j, 0), j, True) for j in others]
+    terms = [*near, *terms]
 
     own, *leaving = pl.pallas_call(
         functools.partial(combine_kernel, exp_dev, chips, pair, cols),

time: 52.4 us -> 55.7 us (1.063)
  waiting for transfers between devices: 11.8 us -> 14.6 us
    ppermute x12, waiting for transfers between devices: 4.92 us -> 9.15 us  [over_chips(): return lax.ppermute(x, 'row', perm)]
    ppermute x4 -> x3, waiting for transfers between devices: 2.3 us -> 0.89 us  [over_cores(): return lax.ppermute(x, 'row', [(i, i ^ 1) for i in range(rows)])]
  transfers between devices with their start and end apart: 22 -> 21, of which waited for: 9 -> 8; matrix products, arithmetic and copies ran while one was open for 0% -> 1% of each run, Pallas kernels for 25% -> 17%
where the time goes in v5:
time: 55.7 us; the launch traced here: 55.5 us
  starting transfers between devices  25.8 us (46%)
  waiting for transfers between devices  14.6 us (26%)
  Pallas kernels  13.9 us (25%)
  other arithmetic  0.84 us (2%)
    ppermute x12, starting transfers between devices, over_chips(): return lax.ppermute(x, 'row', perm)  15.1 us
    ppermute x6, starting transfers between devices, over_col(): return lax.ppermute(x, 'col', [(i, dest(i, j, cols)) for i in range(cols)])  10.1 us
    ppermute x12, waiting for transfers between devices, over_chips(): return lax.ppermute(x, 'row', perm)  9.15 us
    pallas_call x2, Pallas kernels, layer(): pl.pallas_call(functools.partial(expert_kernel, e, chips, more), out_shap...  8.22 us
    pallas_call x1, Pallas kernels, layer(): pl.pallas_call(functools.partial(route_kernel, rows, exp_dev), out_shape=...  4.76 us
    ppermute x6, waiting for transfers between devices, over_col(): return lax.ppermute(x, 'col', [(i, dest(i, j, cols)) for i in range(cols)])  4.55 us
  transfers between devices with their start and end apart: 21, of which 8 were waited for; matrix products, arithmetic and copies ran while one was open for 1% of the time, Pallas kernels for 17%

profile of v5, /device:TPU:0, one launch (start us, length us, event | category | flops | bytes accessed | tf_op | source)
XLA Modules:
  0.0 55.5 jit_solution(9156044354261891953)
XLA Ops:
  0.0 4.1 %collective-permute-start.1 = (bf16[32,720]{1,0:T(8,128)(2,1)}, bf16[32,720]{1,0:T(8,128)(2,1)S(1)}, u32[]{:S(2)}, u32[]{:S(2)}) collective-permute-start(bf16[32,720]{1,0:T(8,128)(2,1)} %refs_0_.1), channel_id=1, source_target_pairs={{0,2},{1,3},{2,0},{3,1},{4,6},{5,7},{6,4},{7,5},{8,10},{9,11},{10,... | collective-permute-start | bytes 138248 | tf_op jit(solution)/shard_map/ppermute | solution.py:175
  4.1 1.6 %collective-permute-start = (bf16[32,720]{1,0:T(8,128)(2,1)}, bf16[32,720]{1,0:T(8,128)(2,1)S(1)}, u32[]{:S(2)}, u32[]{:S(2)}) collective-permute-start(bf16[32,720]{1,0:T(8,128)(2,1)} %refs_0_.1), channel_id=1, source_target_pairs={{0,1},{1,0},{2,3},{3,2},{4,5},{5,4},{6,7},{7,6},{8,9},{9,8},{10,11... | collective-permute-start | bytes 138248 | tf_op jit(solution)/shard_map/ppermute | solution.py:175
  5.6 4.8 %route.1 = (bf16[128,32]{1,0:T(8,128)(2,1)S(1)}, bf16[128,32]{1,0:T(8,128)(2,1)S(1)}, bf16[128,32]{1,0:T(8,128)(2,1)S(1)}, bf16[2,720,2880]{2,1,0:T(8,128)(2,1)S...) custom-call(s32[4,32]{1,0:T(4,128)} %bitcast.5, ...), custom_call_target="tpu_custom_call" | custom-call | tf_op jit(solution)/shard_map/route/pallas_call | solution.py:200
  10.4 1.3 %collective-permute-done.2.refs_3_ = bf16[32,720]{1,0:T(8,128)(2,1)S(1)} collective-permute-done((bf16[32,720]{1,0:T(8,128)(2,1)}, bf16[32,720]{1,0:T(8,128)(2,1)S(1)}, u32[]{:S(2)}, u32[]{:S(2)}) %collective-permute-start.2) | collective-permute-done | bytes 46112 | tf_op jit(solution)/shard_map/ppermute | solution.py:175
  12.7 0.9 %collective-permute-done.3 = bf16[32,2880]{1,0:T(8,128)(2,1)S(1)} collective-permute-done((bf16[32,2880]{1,0:T(8,128)(2,1)S(1)}, bf16[32,2880]{1,0:T(8,128)(2,1)S(1)}, u32[]{:S(2)}, u32[]{:S(2)}) %collective-permute-start.3) | collective-permute-done | bytes 184352 | tf_op jit(solution)/shard_map/ppermute | solution.py:187
  13.7 1.6 %collective-permute-start.4 = (bf16[16,2880]{1,0:T(8,128)(2,1)S(1)}, bf16[16,2880]{1,0:T(8,128)(2,1)S(1)}, u32[]{:S(2)}, u32[]{:S(2)}) collective-permute-start(bf16[16,2880]{1,0:T(8,128)(2,1)S(1)} %pad_maximum_fusion.1), channel_id=1, source_target_pairs={{0,8},{4,12},{8,0},{12,4},{16,24},{20,28},{24,16},{28,20},{1,9},{5... | collective-permute-start | bytes 276488 | tf_op jit(solution)/shard_map/ppermute | solution.py:184
  15.2 1.6 %collective-permute-start.5 = (bf16[16,2880]{1,0:T(8,128)(2,1)S(1)}, bf16[16,2880]{1,0:T(8,128)(2,1)S(1)}, u32[]{:S(2)}, u32[]{:S(2)}) collective-permute-start(bf16[16,2880]{1,0:T(8,128)(2,1)S(1)} %pad_maximum_fusion.2), channel_id=1, source_target_pairs={{0,16},{4,20},{8,24},{12,28},{16,0},{20,4},{24,8},{28,12},{1,17},{... | collective-permute-start | bytes 276488 | tf_op jit(solution)/shard_map/ppermute | solution.py:184
  17.4 1.6 %collective-permute-start.8 = (bf16[16,2880]{1,0:T(8,128)(2,1)S(1)}, bf16[16,2880]{1,0:T(8,128)(2,1)S(1)}, u32[]{:S(2)}, u32[]{:S(2)}) collective-permute-start(bf16[16,2880]{1,0:T(8,128)(2,1)S(1)} %pad_maximum_fusion.5), channel_id=1, source_target_pairs={{0,8},{4,12},{8,0},{12,4},{16,24},{20,28},{24,16},{28,20},{1,9},{5... | collective-permute-start | bytes 276488 | tf_op jit(solution)/shard_map/ppermute | solution.py:184
  19.0 1.6 %collective-permute-start.9 = (bf16[16,2880]{1,0:T(8,128)(2,1)S(1)}, bf16[16,2880]{1,0:T(8,128)(2,1)S(1)}, u32[]{:S(2)}, u32[]{:S(2)}) collective-permute-start(bf16[16,2880]{1,0:T(8,128)(2,1)S(1)} %pad_maximum_fusion.6), channel_id=1, source_target_pairs={{0,16},{4,20},{8,24},{12,28},{16,0},{20,4},{24,8},{28,12},{1,17},{... | collective-permute-start | bytes 276488 | tf_op jit(solution)/shard_map/ppermute | solution.py:184
  21.4 1.7 %collective-permute-done.6.refs_9_ = bf16[16,2880]{1,0:T(8,128)(2,1)S(1)} collective-permute-done((bf16[16,2880]{1,0:T(8,128)(2,1)S(1)}, bf16[16,2880]{1,0:T(8,128)(2,1)S(1)}, u32[]{:S(2)}, u32[]{:S(2)}) %collective-permute-start.6) | collective-permute-done | bytes 92192 | tf_op jit(solution)/shard_map/ppermute | solution.py:184
  23.1 4.6 %shard_map.55 = (bf16[16,2880]{1,0:T(8,128)(2,1)S(1)}, bf16[16,2880]{1,0:T(8,128)(2,1)S(1)}, bf16[16,2880]{1,0:T(8,128)(2,1)S(1)}, bf16[16,2880]{1,0:T(8,128)(2,...) custom-call(bf16[2,720,2880]{2,1,0:T(8,128)(2,1)S(1)} %get-tuple-ele, ...), custom_call_target="tpu_custom_call", output_to_operand_aliasing={{4}: (4, {}), {5}: (5, {})} | custom-call | flops 796262400 | bytes 12441600 | tf_op jit(solution)/shard_map/pallas_call | solution.py:239
  27.8 3.6 %shard_map.56 = (bf16[16,2880]{1,0:T(8,128)(2,1)S(1)}, bf16[16,2880]{1,0:T(8,128)(2,1)S(1)}, bf16[16,2880]{1,0:T(8,128)(2,1)S(1)}, bf16[16,2880]{1,0:T(8,128)(2,1)S(1)}) custom-call(bf16[2,720,2880]{2,1,0:T(8,128)(2,1)S(1)} %get-tuple-element.40.refs_0_, bf16[720,2880]{1,0:T(8,128)(2,1)S(1)} %get-tuple-element.41.refs_1_, ...), custom_call_target="tpu_custom_call" | custom-call | flops 796262400 | bytes 12441600 | tf_op jit(solution)/shard_map/pallas_call | solution.py:239
  31.5 0.9 %collective-permute-start.13 = (bf16[16,2880]{1,0:T(8,128)(2,1)S(1)}, bf16[16,2880]{1,0:T(8,128)(2,1)S(1)}, u32[]{:S(2)}, u32[]{:S(2)}) collective-permute-start(bf16[16,2880]{1,0:T(8,128)(2,1)S(1)} %pad_maximum_fusion.11), channel_id=1, source_target_pairs={{0,24},{4,28},{8,16},{12,20},{16,8},{20,12},{24,0},{28,4},{1,25},{... | collective-permute-start | bytes 276488 | tf_op jit(solution)/shard_map/ppermute | solution.py:184
  32.3 2.2 %collective-permute-start.16 = (bf16[16,2880]{1,0:T(8,128)(2,1)S(1)}, bf16[16,2880]{1,0:T(8,128)(2,1)S(1)}, u32[]{:S(2)}, u32[]{:S(2)}) collective-permute-start(bf16[16,2880]{1,0:T(8,128)(2,1)S(1)} %pad_maximum_fusion.14), channel_id=1, source_target_pairs={{0,24},{4,28},{8,16},{12,20},{16,8},{20,12},{24,0},{28,4},{1,25},{... | collective-permute-start | bytes 276488 | tf_op jit(solution)/shard_map/ppermute | solution.py:184
  34.5 1.1 %collective-permute-start.12 = (bf16[16,2880]{1,0:T(8,128)(2,1)S(1)}, bf16[16,2880]{1,0:T(8,128)(2,1)S(1)}, u32[]{:S(2)}, u32[]{:S(2)}) collective-permute-start(bf16[16,2880]{1,0:T(8,128)(2,1)S(1)} %pad_maximum_fusion.10), channel_id=1, source_target_pairs={{0,16},{4,20},{8,24},{12,28},{16,0},{20,4},{24,8},{28,12},{1,17},{... | collective-permute-start | bytes 276488 | tf_op jit(solution)/shard_map/ppermute | solution.py:184
  35.7 1.0 %collective-permute-start.15 = (bf16[16,2880]{1,0:T(8,128)(2,1)S(1)}, bf16[16,2880]{1,0:T(8,128)(2,1)S(1)}, u32[]{:S(2)}, u32[]{:S(2)}) collective-permute-start(bf16[16,2880]{1,0:T(8,128)(2,1)S(1)} %pad_maximum_fusion.13), channel_id=1, source_target_pairs={{0,16},{4,20},{8,24},{12,28},{16,0},{20,4},{24,8},{28,12},{1,17},{... | collective-permute-start | bytes 276488 | tf_op jit(solution)/shard_map/ppermute | solution.py:184
  36.7 0.9 %collective-permute-start.14 = (bf16[16,2880]{1,0:T(8,128)(2,1)S(1)}, bf16[16,2880]{1,0:T(8,128)(2,1)S(1)}, u32[]{:S(2)}, u32[]{:S(2)}) collective-permute-start(bf16[16,2880]{1,0:T(8,128)(2,1)S(1)} %pad_maximum_fusion.12), channel_id=1, source_target_pairs={{0,8},{4,12},{8,0},{12,4},{16,24},{20,28},{24,16},{28,20},{1,9},{5... | collective-permute-start | bytes 276488 | tf_op jit(solution)/shard_map/ppermute | solution.py:184
  37.7 3.7 %collective-permute-done.14 = bf16[16,2880]{1,0:T(8,128)(2,1)S(1)} collective-permute-done((bf16[16,2880]{1,0:T(8,128)(2,1)S(1)}, bf16[16,2880]{1,0:T(8,128)(2,1)S(1)}, u32[]{:S(2)}, u32[]{:S(2)}) %collective-permute-start.14) | collective-permute-done | bytes 92192 | tf_op jit(solution)/shard_map/ppermute | solution.py:184
  41.5 1.4 %collective-permute-start.11 = (bf16[16,2880]{1,0:T(8,128)(2,1)S(1)}, bf16[16,2880]{1,0:T(8,128)(2,1)S(1)}, u32[]{:S(2)}, u32[]{:S(2)}) collective-permute-start(bf16[16,2880]{1,0:T(8,128)(2,1)S(1)} %pad_maximum_fusion.9), channel_id=1, source_target_pairs={{0,8},{4,12},{8,0},{12,4},{16,24},{20,28},{24,16},{28,20},{1,9},{5... | collective-permute-start | bytes 276488 | tf_op jit(solution)/shard_map/ppermute | solution.py:184
  43.0 3.7 %collective-permute-done.11.refs_1_ = bf16[16,2880]{1,0:T(8,128)(2,1)S(1)} collective-permute-done((bf16[16,2880]{1,0:T(8,128)(2,1)S(1)}, bf16[16,2880]{1,0:T(8,128)(2,1)S(1)}, u32[]{:S(2)}, u32[]{:S(2)}) %collective-permute-start.11) | collective-permute-done | bytes 92192 | tf_op jit(solution)/shard_map/ppermute | solution.py:184
  47.2 2.6 %collective-permute-start.18 = (bf16[32,720]{1,0:T(8,128)(2,1)S(1)}, bf16[32,720]{1,0:T(8,128)(2,1)S(1)}, u32[]{:S(2)}, u32[]{:S(2)}) collective-permute-start(bf16[32,720]{1,0:T(8,128)(2,1)S(1)} %get-tuple-element.52), channel_id=1, source_target_pairs={{0,3},{1,2},{2,1},{3,0},{4,7},{5,6},{6,5},{7,4},{8,11},{9,10},{10,... | collective-permute-start | bytes 138248 | tf_op jit(solution)/shard_map/ppermute | solution.py:175
  49.8 1.8 %collective-permute-start.20 = (bf16[32,720]{1,0:T(8,128)(2,1)S(1)}, bf16[32,720]{1,0:T(8,128)(2,1)S(1)}, u32[]{:S(2)}, u32[]{:S(2)}) collective-permute-start(bf16[32,720]{1,0:T(8,128)(2,1)S(1)} %get-tuple-element.54), channel_id=1, source_target_pairs={{0,1},{1,0},{2,3},{3,2},{4,5},{5,4},{6,7},{7,6},{8,9},{9,8},{10,11... | collective-permute-start | bytes 138248 | tf_op jit(solution)/shard_map/ppermute | solution.py:175
  51.7 1.5 %collective-permute-done.18 = bf16[32,720]{1,0:T(8,128)(2,1)S(1)} collective-permute-done((bf16[32,720]{1,0:T(8,128)(2,1)S(1)}, bf16[32,720]{1,0:T(8,128)(2,1)S(1)}, u32[]{:S(2)}, u32[]{:S(2)}) %collective-permute-start.18) | collective-permute-done | bytes 46112 | tf_op jit(solution)/shard_map/ppermute | solution.py:175
  53.2 1.6 %collective-permute-done.19 = bf16[32,720]{1,0:T(8,128)(2,1)S(1)} collective-permute-done((bf16[32,720]{1,0:T(8,128)(2,1)S(1)}, bf16[32,720]{1,0:T(8,128)(2,1)S(1)}, u32[]{:S(2)}, u32[]{:S(2)}) %collective-permute-start.19) | collective-permute-done | bytes 46112 | tf_op jit(solution)/shard_map/ppermute | solution.py:175
  (55 shorter events, 3.9 us)
Async XLA Ops:
  0.0 10.4 %collective-permute-start.1 = (bf16[32,720]{1,0:T(8,128)(2,1)}, bf16[32,720]{1,0:T(8,128)(2,1)S(1)}, u32[]{:S(2)}, u32[]{:S(2)}) collective-permute-start(bf16[32,720]{1,0:T(8,128)(2,1)} %refs_0_.1), channel_id=1, source_target_pairs={{0,2},{1,3},{2,0},{3,1},{4,6},{5,7},{6,4},{7,5},{8,10},{9,11},{10,... | collective-permute-start | bytes 138248 | tf_op jit(solution)/shard_map/ppermute | solution.py:175
  4.1 6.4 %collective-permute-start = (bf16[32,720]{1,0:T(8,128)(2,1)}, bf16[32,720]{1,0:T(8,128)(2,1)S(1)}, u32[]{:S(2)}, u32[]{:S(2)}) collective-permute-start(bf16[32,720]{1,0:T(8,128)(2,1)} %refs_0_.1), channel_id=1, source_target_pairs={{0,1},{1,0},{2,3},{3,2},{4,5},{5,4},{6,7},{7,6},{8,9},{9,8},{10,11... | collective-permute-start | bytes 138248 | tf_op jit(solution)/shard_map/ppermute | solution.py:175
  5.6 6.1 %collective-permute-start.2 = (bf16[32,720]{1,0:T(8,128)(2,1)}, bf16[32,720]{1,0:T(8,128)(2,1)S(1)}, u32[]{:S(2)}, u32[]{:S(2)}) collective-permute-start(bf16[32,720]{1,0:T(8,128)(2,1)} %refs_0_.1), channel_id=1, source_target_pairs={{0,3},{1,2},{2,1},{3,0},{4,7},{5,6},{6,5},{7,4},{8,11},{9,10},{10,... | collective-permute-start | bytes 138248 | tf_op jit(solution)/shard_map/ppermute | solution.py:175
  5.6 6.1 %copy-start = (bf16[32,720]{1,0:T(8,128)(2,1)S(1)}, bf16[32,720]{1,0:T(8,128)(2,1)}, u32[]{:S(2)}) copy-start(bf16[32,720]{1,0:T(8,128)(2,1)} %refs_0_.1) | copy-start | bytes 138244
  12.1 1.5 %collective-permute-start.3 = (bf16[32,2880]{1,0:T(8,128)(2,1)S(1)}, bf16[32,2880]{1,0:T(8,128)(2,1)S(1)}, u32[]{:S(2)}, u32[]{:S(2)}) collective-permute-start(bf16[32,2880]{1,0:T(8,128)(2,1)S(1)} %get-tuple-element.38), channel_id=1, source_target_pairs={{0,4},{4,0},{8,12},{12,8},{16,20},{20,16},{24,28},{28,24},{1,5},{5... | collective-permute-start | bytes 552968 | tf_op jit(solution)/shard_map/ppermute | solution.py:187
  12.2 5.2 %collective-permute-start.7 = (bf16[32,2880]{1,0:T(8,128)(2,1)S(1)}, bf16[32,2880]{1,0:T(8,128)(2,1)S(1)}, u32[]{:S(2)}, u32[]{:S(2)}) collective-permute-start(bf16[32,2880]{1,0:T(8,128)(2,1)S(1)} %get-tuple-element.43), channel_id=1, source_target_pairs={{0,4},{4,0},{8,12},{12,8},{16,20},{20,16},{24,28},{28,24},{1,5},{5... | collective-permute-start | bytes 552968 | tf_op jit(solution)/shard_map/ppermute | solution.py:187
  13.7 7.0 %collective-permute-start.4 = (bf16[16,2880]{1,0:T(8,128)(2,1)S(1)}, bf16[16,2880]{1,0:T(8,128)(2,1)S(1)}, u32[]{:S(2)}, u32[]{:S(2)}) collective-permute-start(bf16[16,2880]{1,0:T(8,128)(2,1)S(1)} %pad_maximum_fusion.1), channel_id=1, source_target_pairs={{0,8},{4,12},{8,0},{12,4},{16,24},{20,28},{24,16},{28,20},{1,9},{5... | collective-permute-start | bytes 276488 | tf_op jit(solution)/shard_map/ppermute | solution.py:184
  15.2 6.1 %collective-permute-start.5 = (bf16[16,2880]{1,0:T(8,128)(2,1)S(1)}, bf16[16,2880]{1,0:T(8,128)(2,1)S(1)}, u32[]{:S(2)}, u32[]{:S(2)}) collective-permute-start(bf16[16,2880]{1,0:T(8,128)(2,1)S(1)} %pad_maximum_fusion.2), channel_id=1, source_target_pairs={{0,16},{4,20},{8,24},{12,28},{16,0},{20,4},{24,8},{28,12},{1,17},{... | collective-permute-start | bytes 276488 | tf_op jit(solution)/shard_map/ppermute | solution.py:184
  16.8 6.2 %collective-permute-start.6 = (bf16[16,2880]{1,0:T(8,128)(2,1)S(1)}, bf16[16,2880]{1,0:T(8,128)(2,1)S(1)}, u32[]{:S(2)}, u32[]{:S(2)}) collective-permute-start(bf16[16,2880]{1,0:T(8,128)(2,1)S(1)} %pad_maximum_fusion.3), channel_id=1, source_target_pairs={{0,24},{4,28},{8,16},{12,20},{16,8},{20,12},{24,0},{28,4},{1,25},{... | collective-permute-start | bytes 276488 | tf_op jit(solution)/shard_map/ppermute | solution.py:184
  17.4 10.4 %collective-permute-start.8 = (bf16[16,2880]{1,0:T(8,128)(2,1)S(1)}, bf16[16,2880]{1,0:T(8,128)(2,1)S(1)}, u32[]{:S(2)}, u32[]{:S(2)}) collective-permute-start(bf16[16,2880]{1,0:T(8,128)(2,1)S(1)} %pad_maximum_fusion.5), channel_id=1, source_target_pairs={{0,8},{4,12},{8,0},{12,4},{16,24},{20,28},{24,16},{28,20},{1,9},{5... | collective-permute-start | bytes 276488 | tf_op jit(solution)/shard_map/ppermute | solution.py:184
  19.0 8.8 %collective-permute-start.9 = (bf16[16,2880]{1,0:T(8,128)(2,1)S(1)}, bf16[16,2880]{1,0:T(8,128)(2,1)S(1)}, u32[]{:S(2)}, u32[]{:S(2)}) collective-permute-start(bf16[16,2880]{1,0:T(8,128)(2,1)S(1)} %pad_maximum_fusion.6), channel_id=1, source_target_pairs={{0,16},{4,20},{8,24},{12,28},{16,0},{20,4},{24,8},{28,12},{1,17},{... | collective-permute-start | bytes 276488 | tf_op jit(solution)/shard_map/ppermute | solution.py:184
  20.6 7.2 %collective-permute-start.10 = (bf16[16,2880]{1,0:T(8,128)(2,1)S(1)}, bf16[16,2880]{1,0:T(8,128)(2,1)S(1)}, u32[]{:S(2)}, u32[]{:S(2)}) collective-permute-start(bf16[16,2880]{1,0:T(8,128)(2,1)S(1)} %pad_maximum_fusion.7), channel_id=1, source_target_pairs={{0,24},{4,28},{8,16},{12,20},{16,8},{20,12},{24,0},{28,4},{1,25},{... | collective-permute-start | bytes 276488 | tf_op jit(solution)/shard_map/ppermute | solution.py:184
  31.5 11.5 %collective-permute-start.13 = (bf16[16,2880]{1,0:T(8,128)(2,1)S(1)}, bf16[16,2880]{1,0:T(8,128)(2,1)S(1)}, u32[]{:S(2)}, u32[]{:S(2)}) collective-permute-start(bf16[16,2880]{1,0:T(8,128)(2,1)S(1)} %pad_maximum_fusion.11), channel_id=1, source_target_pairs={{0,24},{4,28},{8,16},{12,20},{16,8},{20,12},{24,0},{28,4},{1,25},{... | collective-permute-start | bytes 276488 | tf_op jit(solution)/shard_map/ppermute | solution.py:184
  32.3 9.1 %collective-permute-start.16 = (bf16[16,2880]{1,0:T(8,128)(2,1)S(1)}, bf16[16,2880]{1,0:T(8,128)(2,1)S(1)}, u32[]{:S(2)}, u32[]{:S(2)}) collective-permute-start(bf16[16,2880]{1,0:T(8,128)(2,1)S(1)} %pad_maximum_fusion.14), channel_id=1, source_target_pairs={{0,24},{4,28},{8,16},{12,20},{16,8},{20,12},{24,0},{28,4},{1,25},{... | collective-permute-start | bytes 276488 | tf_op jit(solution)/shard_map/ppermute | solution.py:184
  34.5 8.4 %collective-permute-start.12 = (bf16[16,2880]{1,0:T(8,128)(2,1)S(1)}, bf16[16,2880]{1,0:T(8,128)(2,1)S(1)}, u32[]{:S(2)}, u32[]{:S(2)}) collective-permute-start(bf16[16,2880]{1,0:T(8,128)(2,1)S(1)} %pad_maximum_fusion.10), channel_id=1, source_target_pairs={{0,16},{4,20},{8,24},{12,28},{16,0},{20,4},{24,8},{28,12},{1,17},{... | collective-permute-start | bytes 276488 | tf_op jit(solution)/shard_map/ppermute | solution.py:184
  35.7 5.7 %collective-permute-start.15 = (bf16[16,2880]{1,0:T(8,128)(2,1)S(1)}, bf16[16,2880]{1,0:T(8,128)(2,1)S(1)}, u32[]{:S(2)}, u32[]{:S(2)}) collective-permute-start(bf16[16,2880]{1,0:T(8,128)(2,1)S(1)} %pad_maximum_fusion.13), channel_id=1, source_target_pairs={{0,16},{4,20},{8,24},{12,28},{16,0},{20,4},{24,8},{28,12},{1,17},{... | collective-permute-start | bytes 276488 | tf_op jit(solution)/shard_map/ppermute | solution.py:184
  36.7 4.6 %collective-permute-start.14 = (bf16[16,2880]{1,0:T(8,128)(2,1)S(1)}, bf16[16,2880]{1,0:T(8,128)(2,1)S(1)}, u32[]{:S(2)}, u32[]{:S(2)}) collective-permute-start(bf16[16,2880]{1,0:T(8,128)(2,1)S(1)} %pad_maximum_fusion.12), channel_id=1, source_target_pairs={{0,8},{4,12},{8,0},{12,4},{16,24},{20,28},{24,16},{28,20},{1,9},{5... | collective-permute-start | bytes 276488 | tf_op jit(solution)/shard_map/ppermute | solution.py:184
  41.4 5.3 %collective-permute-start.17 = (bf16[64,2880]{1,0:T(8,128)(2,1)S(1)}, bf16[64,2880]{1,0:T(8,128)(2,1)S(1)}, u32[]{:S(2)}, u32[]{:S(2)}) collective-permute-start(bf16[64,2880]{1,0:T(8,128)(2,1)S(1)} %constant_dynamic-update-slice_fusion), channel_id=1, source_target_pairs={{0,4},{4,0},{8,12},{12,8},{16,20},{20,16},{24,28},{28,24},{1,5},{5... | collective-permute-start | bytes 1105928 | tf_op jit(solution)/shard_map/ppermute | solution.py:187
  41.5 5.2 %collective-permute-start.11 = (bf16[16,2880]{1,0:T(8,128)(2,1)S(1)}, bf16[16,2880]{1,0:T(8,128)(2,1)S(1)}, u32[]{:S(2)}, u32[]{:S(2)}) collective-permute-start(bf16[16,2880]{1,0:T(8,128)(2,1)S(1)} %pad_maximum_fusion.9), channel_id=1, source_target_pairs={{0,8},{4,12},{8,0},{12,4},{16,24},{20,28},{24,16},{28,20},{1,9},{5... | collective-permute-start | bytes 276488 | tf_op jit(solution)/shard_map/ppermute | solution.py:184
  47.2 6.0 %collective-permute-start.18 = (bf16[32,720]{1,0:T(8,128)(2,1)S(1)}, bf16[32,720]{1,0:T(8,128)(2,1)S(1)}, u32[]{:S(2)}, u32[]{:S(2)}) collective-permute-start(bf16[32,720]{1,0:T(8,128)(2,1)S(1)} %get-tuple-element.52), channel_id=1, source_target_pairs={{0,3},{1,2},{2,1},{3,0},{4,7},{5,6},{6,5},{7,4},{8,11},{9,10},{10,... | collective-permute-start | bytes 138248 | tf_op jit(solution)/shard_map/ppermute | solution.py:175
  49.8 5.0 %collective-permute-start.19 = (bf16[32,720]{1,0:T(8,128)(2,1)S(1)}, bf16[32,720]{1,0:T(8,128)(2,1)S(1)}, u32[]{:S(2)}, u32[]{:S(2)}) collective-permute-start(bf16[32,720]{1,0:T(8,128)(2,1)S(1)} %get-tuple-element.53), channel_id=1, source_target_pairs={{0,2},{1,3},{2,0},{3,1},{4,6},{5,7},{6,4},{7,5},{8,10},{9,11},{10,... | collective-permute-start | bytes 138248 | tf_op jit(solution)/shard_map/ppermute | solution.py:175
  49.8 5.1 %collective-permute-start.20 = (bf16[32,720]{1,0:T(8,128)(2,1)S(1)}, bf16[32,720]{1,0:T(8,128)(2,1)S(1)}, u32[]{:S(2)}, u32[]{:S(2)}) collective-permute-start(bf16[32,720]{1,0:T(8,128)(2,1)S(1)} %get-tuple-element.54), channel_id=1, source_target_pairs={{0,1},{1,0},{2,3},{3,2},{4,5},{5,4},{6,7},{7,6},{8,9},{9,8},{10,11... | collective-permute-start | bytes 138248 | tf_op jit(solution)/shard_map/ppermute | solution.py:175

commit v6 on v5

--- a/solution.py
+++ b/solution.py
@@ -102,16 +102,19 @@
         out_refs[i][...] = sent[i * each : (i + 1) * each]
 
 
-def expert_kernel(e, blocks, more, *refs):
-    gu, dn, refs = refs[0], refs[1], refs[2:]
-    copies = []
+def expert_kernel(e, blocks, more, gu_hbm, dn_hbm, gu, dn, *refs):
+    refs = refs[more:]
+    x_refs, y_refs, refs = refs[:blocks], refs[blocks : 2 * blocks], refs[2 * blocks :]
+    x, hidden, sems = refs[-3:]
+    down, ahead = [], []
+    if e > 0:
+        dn = refs[0]
+        down = [pltpu.make_async_copy(dn_hbm.at[e], dn, sems.at[0])]
     if more:
-        copies = fetches(e + 1, *refs[:2], *refs[-5:-3], refs[-1])
-        refs = refs[4:-1]
-    for c in copies:
+        next_gu = refs[-4]
+        ahead = [pltpu.make_async_copy(gu_hbm.at[e + 1], next_gu, sems.at[1])]
+    for c in down + ahead:
         c.start()
-    x_refs, y_refs = refs[:blocks], refs[blocks : 2 * blocks]
-    x, hidden = refs[-2:]
     hid, width = dn.shape
     rows = x_refs[0].shape[0]
     for b in range(blocks):
@@ -125,13 +128,15 @@
         ]
         act = (up + 1.0) * gate * jax.nn.sigmoid(1.702 * gate)
         hidden[:, at : at + size] = act.astype(jnp.bfloat16)
+    for c in down:
+        c.wait()
     for at, size in chunks_of(width, 768):
         part = jnp.dot(
             hidden[...], dn[:, at : at + size], preferred_element_type=jnp.float32
         ).astype(jnp.bfloat16)
         for b in range(blocks):
             y_refs[b][:, at : at + size] = part[b * rows : (b + 1) * rows]
-    for c in copies:
+    for c in ahead:
         c.wait()
 
 
@@ -236,25 +241,29 @@
     made = []
     for e in range(exp_dev):
         more = e + 1 < exp_dev
+        gu, dn = weights[2 * e : 2 * e + 2]
+        filled = [held[1]] * (e > 0) + [held[0]] * more
         ys = pl.pallas_call(
             functools.partial(expert_kernel, e, chips, more),
-            out_shape=[shape((block, width), bf16)] * chips + held * more,
-            in_specs=[VMEM] * 2 + [HBM, HBM, VMEM, VMEM] * more + [VMEM] * chips,
-            out_specs=[VMEM] * (chips + 2 * more),
+            out_shape=[shape((block, width), bf16)] * chips + filled,
+            in_specs=[HBM] * 2 + [VMEM] * (2 + more + chips),
+            out_specs=[VMEM] * (chips + len(filled)),
             scratch_shapes=[
                 pltpu.VMEM((chips * block, width), bf16),
                 pltpu.VMEM((chips * block, hid), bf16),
-            ]
-            + [pltpu.SemaphoreType.DMA((2,))] * more,
+                pltpu.SemaphoreType.DMA((2,)),
+            ],
             compiler_params=params(12),
             cost_estimate=pl.CostEstimate(
                 flops=6 * chips * block * width * hid,
                 bytes_accessed=6 * width * hid,
                 transcendentals=chips * block * hid,
             ),
-            input_output_aliases={4: chips, 5: chips + 1} if more else {},
-        )(*weights[:2], *[gate_up, expert_down, *weights[2:4]] * more, *inputs[e])
-        weights = [*ys[chips:], *weights[4:]]
+            input_output_aliases=({3: chips} if e > 0 else {})
+            | ({4: chips + (e > 0)} if more else {}),
+        )(gate_up, expert_down, gu, dn, *weights[2 * e + 2 : 2 * e + 2 + more], *inputs[e])
+        if more:
+            weights = [*weights[: 2 * e + 2], ys[-1], *weights[2 * e + 3 :]]
         made.append(ys[:chips])
 
     def of_core(j, q):

time: 55.7 us -> 55.5 us (level)
  transfers between devices with their start and end apart: 21 -> 21, of which waited for: 8 -> 8; matrix products, arithmetic and copies ran while one was open for 1% -> 1% of each run, Pallas kernels for 17% -> 16%
where the time goes in v6:
time: 55.5 us; the launch traced here: 55.3 us
  starting transfers between devices  25.8 us (46%)
  waiting for transfers between devices  14.6 us (26%)
  Pallas kernels  13.6 us (25%)
  other arithmetic  0.83 us (1%)
    ppermute x12, starting transfers between devices, over_chips(): return lax.ppermute(x, 'row', perm)  15.1 us
    ppermute x6, starting transfers between devices, over_col(): return lax.ppermute(x, 'col', [(i, dest(i, j, cols)) for i in range(cols)])  10.1 us
    ppermute x12, waiting for transfers between devices, over_chips(): return lax.ppermute(x, 'row', perm)  9.14 us
    pallas_call x2, Pallas kernels, layer(): pl.pallas_call(functools.partial(expert_kernel, e, chips, more), out_shap...  7.96 us
    pallas_call x1, Pallas kernels, layer(): pl.pallas_call(functools.partial(route_kernel, rows, exp_dev), out_shape=...  4.76 us
    ppermute x6, waiting for transfers between devices, over_col(): return lax.ppermute(x, 'col', [(i, dest(i, j, cols)) for i in range(cols)])  4.55 us
  transfers between devices with their start and end apart: 21, of which 8 were waited for; matrix products, arithmetic and copies ran while one was open for 1% of the time, Pallas kernels for 16%

profile of v6, /device:TPU:0, one launch (start us, length us, event | category | flops | bytes accessed | tf_op | source)
XLA Modules:
  0.0 55.3 jit_solution(5643709294121553695)
XLA Ops:
  0.0 4.1 %collective-permute-start.1 = (bf16[32,720]{1,0:T(8,128)(2,1)}, bf16[32,720]{1,0:T(8,128)(2,1)S(1)}, u32[]{:S(2)}, u32[]{:S(2)}) collective-permute-start(bf16[32,720]{1,0:T(8,128)(2,1)} %refs_0_.1), channel_id=1, source_target_pairs={{0,2},{1,3},{2,0},{3,1},{4,6},{5,7},{6,4},{7,5},{8,10},{9,11},{10,... | collective-permute-start | bytes 138248 | tf_op jit(solution)/shard_map/ppermute | solution.py:180
  4.1 1.6 %collective-permute-start = (bf16[32,720]{1,0:T(8,128)(2,1)}, bf16[32,720]{1,0:T(8,128)(2,1)S(1)}, u32[]{:S(2)}, u32[]{:S(2)}) collective-permute-start(bf16[32,720]{1,0:T(8,128)(2,1)} %refs_0_.1), channel_id=1, source_target_pairs={{0,1},{1,0},{2,3},{3,2},{4,5},{5,4},{6,7},{7,6},{8,9},{9,8},{10,11... | collective-permute-start | bytes 138248 | tf_op jit(solution)/shard_map/ppermute | solution.py:180
  5.6 4.8 %route.1 = (bf16[128,32]{1,0:T(8,128)(2,1)S(1)}, bf16[128,32]{1,0:T(8,128)(2,1)S(1)}, bf16[128,32]{1,0:T(8,128)(2,1)S(1)}, bf16[2,720,2880]{2,1,0:T(8,128)(2,1)S...) custom-call(s32[4,32]{1,0:T(4,128)} %bitcast.6, ...), custom_call_target="tpu_custom_call" | custom-call | tf_op jit(solution)/shard_map/route/pallas_call | solution.py:205
  10.4 1.3 %collective-permute-done.2.refs_3_ = bf16[32,720]{1,0:T(8,128)(2,1)S(1)} collective-permute-done((bf16[32,720]{1,0:T(8,128)(2,1)}, bf16[32,720]{1,0:T(8,128)(2,1)S(1)}, u32[]{:S(2)}, u32[]{:S(2)}) %collective-permute-start.2) | collective-permute-done | bytes 46112 | tf_op jit(solution)/shard_map/ppermute | solution.py:180
  12.7 0.9 %collective-permute-done.3 = bf16[32,2880]{1,0:T(8,128)(2,1)S(1)} collective-permute-done((bf16[32,2880]{1,0:T(8,128)(2,1)S(1)}, bf16[32,2880]{1,0:T(8,128)(2,1)S(1)}, u32[]{:S(2)}, u32[]{:S(2)}) %collective-permute-start.3) | collective-permute-done | bytes 184352 | tf_op jit(solution)/shard_map/ppermute | solution.py:192
  13.7 1.6 %collective-permute-start.4 = (bf16[16,2880]{1,0:T(8,128)(2,1)S(1)}, bf16[16,2880]{1,0:T(8,128)(2,1)S(1)}, u32[]{:S(2)}, u32[]{:S(2)}) collective-permute-start(bf16[16,2880]{1,0:T(8,128)(2,1)S(1)} %pad_maximum_fusion.1), channel_id=1, source_target_pairs={{0,8},{4,12},{8,0},{12,4},{16,24},{20,28},{24,16},{28,20},{1,9},{5... | collective-permute-start | bytes 276488 | tf_op jit(solution)/shard_map/ppermute | solution.py:189
  15.2 1.6 %collective-permute-start.5 = (bf16[16,2880]{1,0:T(8,128)(2,1)S(1)}, bf16[16,2880]{1,0:T(8,128)(2,1)S(1)}, u32[]{:S(2)}, u32[]{:S(2)}) collective-permute-start(bf16[16,2880]{1,0:T(8,128)(2,1)S(1)} %pad_maximum_fusion.2), channel_id=1, source_target_pairs={{0,16},{4,20},{8,24},{12,28},{16,0},{20,4},{24,8},{28,12},{1,17},{... | collective-permute-start | bytes 276488 | tf_op jit(solution)/shard_map/ppermute | solution.py:189
  17.4 1.6 %collective-permute-start.8 = (bf16[16,2880]{1,0:T(8,128)(2,1)S(1)}, bf16[16,2880]{1,0:T(8,128)(2,1)S(1)}, u32[]{:S(2)}, u32[]{:S(2)}) collective-permute-start(bf16[16,2880]{1,0:T(8,128)(2,1)S(1)} %pad_maximum_fusion.5), channel_id=1, source_target_pairs={{0,8},{4,12},{8,0},{12,4},{16,24},{20,28},{24,16},{28,20},{1,9},{5... | collective-permute-start | bytes 276488 | tf_op jit(solution)/shard_map/ppermute | solution.py:189
  19.0 1.6 %collective-permute-start.9 = (bf16[16,2880]{1,0:T(8,128)(2,1)S(1)}, bf16[16,2880]{1,0:T(8,128)(2,1)S(1)}, u32[]{:S(2)}, u32[]{:S(2)}) collective-permute-start(bf16[16,2880]{1,0:T(8,128)(2,1)S(1)} %pad_maximum_fusion.6), channel_id=1, source_target_pairs={{0,16},{4,20},{8,24},{12,28},{16,0},{20,4},{24,8},{28,12},{1,17},{... | collective-permute-start | bytes 276488 | tf_op jit(solution)/shard_map/ppermute | solution.py:189
  21.4 1.7 %collective-permute-done.6.refs_4_ = bf16[16,2880]{1,0:T(8,128)(2,1)S(1)} collective-permute-done((bf16[16,2880]{1,0:T(8,128)(2,1)S(1)}, bf16[16,2880]{1,0:T(8,128)(2,1)S(1)}, u32[]{:S(2)}, u32[]{:S(2)}) %collective-permute-start.6) | collective-permute-done | bytes 92192 | tf_op jit(solution)/shard_map/ppermute | solution.py:189
  23.1 4.2 %shard_map.55 = (bf16[16,2880]{1,0:T(8,128)(2,1)S(1)}, bf16[16,2880]{1,0:T(8,128)(2,1)S(1)}, bf16[16,2880]{1,0:T(8,128)(2,1)S(1)}, bf16[16,2880]{1,0:T(8,128)(2,1)S(1)}, bf16[2,720,2880]{2,1,0:T(8,128)(2,1)S(1)}) custom-call(bf16[2,2,720,2880]{3,2,1,0:T(8,128)(2,1)} %bitcast.4, bf16[2,720,2880]{2,1,0:T(8,128)(2,1)} %dn_hbm.5, ...), custom_call_target="tpu_custom_call", output_to_operand_aliasing={{4}: (4, {})} | custom-call | flops 796262400 | bytes 12441600 | tf_op jit(solution)/shard_map/pallas_call | solution.py:246
  27.3 3.8 %shard_map.56 = (bf16[16,2880]{1,0:T(8,128)(2,1)S(1)}, bf16[16,2880]{1,0:T(8,128)(2,1)S(1)}, bf16[16,2880]{1,0:T(8,128)(2,1)S(1)}, bf16[16,2880]{1,0:T(8,128)(2,1)S(1)}, bf16[720,2880]{1,0:T(8,128)(2,1)S(1)}) custom-call(bf16[2,2,720,2880]{3,2,1,0:T(8,128)(2,1)} %bitcast.5, bf16[2,720,2880]{2,1,0:T(8,128)(2,1)} %dn_hbm.5, ...), custom_call_target="tpu_custom_call", output_to_operand_aliasing={{4}: (3, {})} | custom-call | flops 796262400 | bytes 12441600 | tf_op jit(solution)/shard_map/pallas_call | solution.py:246
  31.2 0.9 %collective-permute-start.13 = (bf16[16,2880]{1,0:T(8,128)(2,1)S(1)}, bf16[16,2880]{1,0:T(8,128)(2,1)S(1)}, u32[]{:S(2)}, u32[]{:S(2)}) collective-permute-start(bf16[16,2880]{1,0:T(8,128)(2,1)S(1)} %pad_maximum_fusion.11), channel_id=1, source_target_pairs={{0,24},{4,28},{8,16},{12,20},{16,8},{20,12},{24,0},{28,4},{1,25},{... | collective-permute-start | bytes 276488 | tf_op jit(solution)/shard_map/ppermute | solution.py:189
  32.1 2.2 %collective-permute-start.16 = (bf16[16,2880]{1,0:T(8,128)(2,1)S(1)}, bf16[16,2880]{1,0:T(8,128)(2,1)S(1)}, u32[]{:S(2)}, u32[]{:S(2)}) collective-permute-start(bf16[16,2880]{1,0:T(8,128)(2,1)S(1)} %pad_maximum_fusion.14), channel_id=1, source_target_pairs={{0,24},{4,28},{8,16},{12,20},{16,8},{20,12},{24,0},{28,4},{1,25},{... | collective-permute-start | bytes 276488 | tf_op jit(solution)/shard_map/ppermute | solution.py:189
  34.3 1.1 %collective-permute-start.12 = (bf16[16,2880]{1,0:T(8,128)(2,1)S(1)}, bf16[16,2880]{1,0:T(8,128)(2,1)S(1)}, u32[]{:S(2)}, u32[]{:S(2)}) collective-permute-start(bf16[16,2880]{1,0:T(8,128)(2,1)S(1)} %pad_maximum_fusion.10), channel_id=1, source_target_pairs={{0,16},{4,20},{8,24},{12,28},{16,0},{20,4},{24,8},{28,12},{1,17},{... | collective-permute-start | bytes 276488 | tf_op jit(solution)/shard_map/ppermute | solution.py:189
  35.4 1.0 %collective-permute-start.15 = (bf16[16,2880]{1,0:T(8,128)(2,1)S(1)}, bf16[16,2880]{1,0:T(8,128)(2,1)S(1)}, u32[]{:S(2)}, u32[]{:S(2)}) collective-permute-start(bf16[16,2880]{1,0:T(8,128)(2,1)S(1)} %pad_maximum_fusion.13), channel_id=1, source_target_pairs={{0,16},{4,20},{8,24},{12,28},{16,0},{20,4},{24,8},{28,12},{1,17},{... | collective-permute-start | bytes 276488 | tf_op jit(solution)/shard_map/ppermute | solution.py:189
  36.5 0.9 %collective-permute-start.14 = (bf16[16,2880]{1,0:T(8,128)(2,1)S(1)}, bf16[16,2880]{1,0:T(8,128)(2,1)S(1)}, u32[]{:S(2)}, u32[]{:S(2)}) collective-permute-start(bf16[16,2880]{1,0:T(8,128)(2,1)S(1)} %pad_maximum_fusion.12), channel_id=1, source_target_pairs={{0,8},{4,12},{8,0},{12,4},{16,24},{20,28},{24,16},{28,20},{1,9},{5... | collective-permute-start | bytes 276488 | tf_op jit(solution)/shard_map/ppermute | solution.py:189
  37.4 3.7 %collective-permute-done.14 = bf16[16,2880]{1,0:T(8,128)(2,1)S(1)} collective-permute-done((bf16[16,2880]{1,0:T(8,128)(2,1)S(1)}, bf16[16,2880]{1,0:T(8,128)(2,1)S(1)}, u32[]{:S(2)}, u32[]{:S(2)}) %collective-permute-start.14) | collective-permute-done | bytes 92192 | tf_op jit(solution)/shard_map/ppermute | solution.py:189
  41.3 1.4 %collective-permute-start.11 = (bf16[16,2880]{1,0:T(8,128)(2,1)S(1)}, bf16[16,2880]{1,0:T(8,128)(2,1)S(1)}, u32[]{:S(2)}, u32[]{:S(2)}) collective-permute-start(bf16[16,2880]{1,0:T(8,128)(2,1)S(1)} %pad_maximum_fusion.9), channel_id=1, source_target_pairs={{0,8},{4,12},{8,0},{12,4},{16,24},{20,28},{24,16},{28,20},{1,9},{5... | collective-permute-start | bytes 276488 | tf_op jit(solution)/shard_map/ppermute | solution.py:189
  42.7 3.7 %collective-permute-done.11.refs_1_ = bf16[16,2880]{1,0:T(8,128)(2,1)S(1)} collective-permute-done((bf16[16,2880]{1,0:T(8,128)(2,1)S(1)}, bf16[16,2880]{1,0:T(8,128)(2,1)S(1)}, u32[]{:S(2)}, u32[]{:S(2)}) %collective-permute-start.11) | collective-permute-done | bytes 92192 | tf_op jit(solution)/shard_map/ppermute | solution.py:189
  46.9 2.6 %collective-permute-start.18 = (bf16[32,720]{1,0:T(8,128)(2,1)S(1)}, bf16[32,720]{1,0:T(8,128)(2,1)S(1)}, u32[]{:S(2)}, u32[]{:S(2)}) collective-permute-start(bf16[32,720]{1,0:T(8,128)(2,1)S(1)} %get-tuple-element.50), channel_id=1, source_target_pairs={{0,3},{1,2},{2,1},{3,0},{4,7},{5,6},{6,5},{7,4},{8,11},{9,10},{10,... | collective-permute-start | bytes 138248 | tf_op jit(solution)/shard_map/ppermute | solution.py:180
  49.6 1.8 %collective-permute-start.20 = (bf16[32,720]{1,0:T(8,128)(2,1)S(1)}, bf16[32,720]{1,0:T(8,128)(2,1)S(1)}, u32[]{:S(2)}, u32[]{:S(2)}) collective-permute-start(bf16[32,720]{1,0:T(8,128)(2,1)S(1)} %get-tuple-element.52), channel_id=1, source_target_pairs={{0,1},{1,0},{2,3},{3,2},{4,5},{5,4},{6,7},{7,6},{8,9},{9,8},{10,11... | collective-permute-start | bytes 138248 | tf_op jit(solution)/shard_map/ppermute | solution.py:180
  51.4 1.5 %collective-permute-done.18 = bf16[32,720]{1,0:T(8,128)(2,1)S(1)} collective-permute-done((bf16[32,720]{1,0:T(8,128)(2,1)S(1)}, bf16[32,720]{1,0:T(8,128)(2,1)S(1)}, u32[]{:S(2)}, u32[]{:S(2)}) %collective-permute-start.18) | collective-permute-done | bytes 46112 | tf_op jit(solution)/shard_map/ppermute | solution.py:180
  52.9 1.6 %collective-permute-done.19 = bf16[32,720]{1,0:T(8,128)(2,1)S(1)} collective-permute-done((bf16[32,720]{1,0:T(8,128)(2,1)S(1)}, bf16[32,720]{1,0:T(8,128)(2,1)S(1)}, u32[]{:S(2)}, u32[]{:S(2)}) %collective-permute-start.19) | collective-permute-done | bytes 46112 | tf_op jit(solution)/shard_map/ppermute | solution.py:180
  (55 shorter events, 3.9 us)
Async XLA Ops:
  0.0 10.4 %collective-permute-start.1 = (bf16[32,720]{1,0:T(8,128)(2,1)}, bf16[32,720]{1,0:T(8,128)(2,1)S(1)}, u32[]{:S(2)}, u32[]{:S(2)}) collective-permute-start(bf16[32,720]{1,0:T(8,128)(2,1)} %refs_0_.1), channel_id=1, source_target_pairs={{0,2},{1,3},{2,0},{3,1},{4,6},{5,7},{6,4},{7,5},{8,10},{9,11},{10,... | collective-permute-start | bytes 138248 | tf_op jit(solution)/shard_map/ppermute | solution.py:180
  4.1 6.4 %collective-permute-start = (bf16[32,720]{1,0:T(8,128)(2,1)}, bf16[32,720]{1,0:T(8,128)(2,1)S(1)}, u32[]{:S(2)}, u32[]{:S(2)}) collective-permute-start(bf16[32,720]{1,0:T(8,128)(2,1)} %refs_0_.1), channel_id=1, source_target_pairs={{0,1},{1,0},{2,3},{3,2},{4,5},{5,4},{6,7},{7,6},{8,9},{9,8},{10,11... | collective-permute-start | bytes 138248 | tf_op jit(solution)/shard_map/ppermute | solution.py:180
  5.6 6.1 %collective-permute-start.2 = (bf16[32,720]{1,0:T(8,128)(2,1)}, bf16[32,720]{1,0:T(8,128)(2,1)S(1)}, u32[]{:S(2)}, u32[]{:S(2)}) collective-permute-start(bf16[32,720]{1,0:T(8,128)(2,1)} %refs_0_.1), channel_id=1, source_target_pairs={{0,3},{1,2},{2,1},{3,0},{4,7},{5,6},{6,5},{7,4},{8,11},{9,10},{10,... | collective-permute-start | bytes 138248 | tf_op jit(solution)/shard_map/ppermute | solution.py:180
  5.6 6.1 %copy-start = (bf16[32,720]{1,0:T(8,128)(2,1)S(1)}, bf16[32,720]{1,0:T(8,128)(2,1)}, u32[]{:S(2)}) copy-start(bf16[32,720]{1,0:T(8,128)(2,1)} %refs_0_.1) | copy-start | bytes 138244
  12.1 1.5 %collective-permute-start.3 = (bf16[32,2880]{1,0:T(8,128)(2,1)S(1)}, bf16[32,2880]{1,0:T(8,128)(2,1)S(1)}, u32[]{:S(2)}, u32[]{:S(2)}) collective-permute-start(bf16[32,2880]{1,0:T(8,128)(2,1)S(1)} %get-tuple-element.36), channel_id=1, source_target_pairs={{0,4},{4,0},{8,12},{12,8},{16,20},{20,16},{24,28},{28,24},{1,5},{5... | collective-permute-start | bytes 552968 | tf_op jit(solution)/shard_map/ppermute | solution.py:192
  12.2 5.2 %collective-permute-start.7 = (bf16[32,2880]{1,0:T(8,128)(2,1)S(1)}, bf16[32,2880]{1,0:T(8,128)(2,1)S(1)}, u32[]{:S(2)}, u32[]{:S(2)}) collective-permute-start(bf16[32,2880]{1,0:T(8,128)(2,1)S(1)} %get-tuple-element.41), channel_id=1, source_target_pairs={{0,4},{4,0},{8,12},{12,8},{16,20},{20,16},{24,28},{28,24},{1,5},{5... | collective-permute-start | bytes 552968 | tf_op jit(solution)/shard_map/ppermute | solution.py:192
  13.7 7.0 %collective-permute-start.4 = (bf16[16,2880]{1,0:T(8,128)(2,1)S(1)}, bf16[16,2880]{1,0:T(8,128)(2,1)S(1)}, u32[]{:S(2)}, u32[]{:S(2)}) collective-permute-start(bf16[16,2880]{1,0:T(8,128)(2,1)S(1)} %pad_maximum_fusion.1), channel_id=1, source_target_pairs={{0,8},{4,12},{8,0},{12,4},{16,24},{20,28},{24,16},{28,20},{1,9},{5... | collective-permute-start | bytes 276488 | tf_op jit(solution)/shard_map/ppermute | solution.py:189
  15.2 6.1 %collective-permute-start.5 = (bf16[16,2880]{1,0:T(8,128)(2,1)S(1)}, bf16[16,2880]{1,0:T(8,128)(2,1)S(1)}, u32[]{:S(2)}, u32[]{:S(2)}) collective-permute-start(bf16[16,2880]{1,0:T(8,128)(2,1)S(1)} %pad_maximum_fusion.2), channel_id=1, source_target_pairs={{0,16},{4,20},{8,24},{12,28},{16,0},{20,4},{24,8},{28,12},{1,17},{... | collective-permute-start | bytes 276488 | tf_op jit(solution)/shard_map/ppermute | solution.py:189
  16.8 6.2 %collective-permute-start.6 = (bf16[16,2880]{1,0:T(8,128)(2,1)S(1)}, bf16[16,2880]{1,0:T(8,128)(2,1)S(1)}, u32[]{:S(2)}, u32[]{:S(2)}) collective-permute-start(bf16[16,2880]{1,0:T(8,128)(2,1)S(1)} %pad_maximum_fusion.3), channel_id=1, source_target_pairs={{0,24},{4,28},{8,16},{12,20},{16,8},{20,12},{24,0},{28,4},{1,25},{... | collective-permute-start | bytes 276488 | tf_op jit(solution)/shard_map/ppermute | solution.py:189
  17.4 9.9 %collective-permute-start.8 = (bf16[16,2880]{1,0:T(8,128)(2,1)S(1)}, bf16[16,2880]{1,0:T(8,128)(2,1)S(1)}, u32[]{:S(2)}, u32[]{:S(2)}) collective-permute-start(bf16[16,2880]{1,0:T(8,128)(2,1)S(1)} %pad_maximum_fusion.5), channel_id=1, source_target_pairs={{0,8},{4,12},{8,0},{12,4},{16,24},{20,28},{24,16},{28,20},{1,9},{5... | collective-permute-start | bytes 276488 | tf_op jit(solution)/shard_map/ppermute | solution.py:189
  19.0 8.3 %collective-permute-start.9 = (bf16[16,2880]{1,0:T(8,128)(2,1)S(1)}, bf16[16,2880]{1,0:T(8,128)(2,1)S(1)}, u32[]{:S(2)}, u32[]{:S(2)}) collective-permute-start(bf16[16,2880]{1,0:T(8,128)(2,1)S(1)} %pad_maximum_fusion.6), channel_id=1, source_target_pairs={{0,16},{4,20},{8,24},{12,28},{16,0},{20,4},{24,8},{28,12},{1,17},{... | collective-permute-start | bytes 276488 | tf_op jit(solution)/shard_map/ppermute | solution.py:189
  20.6 6.7 %collective-permute-start.10 = (bf16[16,2880]{1,0:T(8,128)(2,1)S(1)}, bf16[16,2880]{1,0:T(8,128)(2,1)S(1)}, u32[]{:S(2)}, u32[]{:S(2)}) collective-permute-start(bf16[16,2880]{1,0:T(8,128)(2,1)S(1)} %pad_maximum_fusion.7), channel_id=1, source_target_pairs={{0,24},{4,28},{8,16},{12,20},{16,8},{20,12},{24,0},{28,4},{1,25},{... | collective-permute-start | bytes 276488 | tf_op jit(solution)/shard_map/ppermute | solution.py:189
  31.2 11.5 %collective-permute-start.13 = (bf16[16,2880]{1,0:T(8,128)(2,1)S(1)}, bf16[16,2880]{1,0:T(8,128)(2,1)S(1)}, u32[]{:S(2)}, u32[]{:S(2)}) collective-permute-start(bf16[16,2880]{1,0:T(8,128)(2,1)S(1)} %pad_maximum_fusion.11), channel_id=1, source_target_pairs={{0,24},{4,28},{8,16},{12,20},{16,8},{20,12},{24,0},{28,4},{1,25},{... | collective-permute-start | bytes 276488 | tf_op jit(solution)/shard_map/ppermute | solution.py:189
  32.1 9.1 %collective-permute-start.16 = (bf16[16,2880]{1,0:T(8,128)(2,1)S(1)}, bf16[16,2880]{1,0:T(8,128)(2,1)S(1)}, u32[]{:S(2)}, u32[]{:S(2)}) collective-permute-start(bf16[16,2880]{1,0:T(8,128)(2,1)S(1)} %pad_maximum_fusion.14), channel_id=1, source_target_pairs={{0,24},{4,28},{8,16},{12,20},{16,8},{20,12},{24,0},{28,4},{1,25},{... | collective-permute-start | bytes 276488 | tf_op jit(solution)/shard_map/ppermute | solution.py:189
  34.3 8.4 %collective-permute-start.12 = (bf16[16,2880]{1,0:T(8,128)(2,1)S(1)}, bf16[16,2880]{1,0:T(8,128)(2,1)S(1)}, u32[]{:S(2)}, u32[]{:S(2)}) collective-permute-start(bf16[16,2880]{1,0:T(8,128)(2,1)S(1)} %pad_maximum_fusion.10), channel_id=1, source_target_pairs={{0,16},{4,20},{8,24},{12,28},{16,0},{20,4},{24,8},{28,12},{1,17},{... | collective-permute-start | bytes 276488 | tf_op jit(solution)/shard_map/ppermute | solution.py:189
  35.4 5.7 %collective-permute-start.15 = (bf16[16,2880]{1,0:T(8,128)(2,1)S(1)}, bf16[16,2880]{1,0:T(8,128)(2,1)S(1)}, u32[]{:S(2)}, u32[]{:S(2)}) collective-permute-start(bf16[16,2880]{1,0:T(8,128)(2,1)S(1)} %pad_maximum_fusion.13), channel_id=1, source_target_pairs={{0,16},{4,20},{8,24},{12,28},{16,0},{20,4},{24,8},{28,12},{1,17},{... | collective-permute-start | bytes 276488 | tf_op jit(solution)/shard_map/ppermute | solution.py:189
  36.5 4.6 %collective-permute-start.14 = (bf16[16,2880]{1,0:T(8,128)(2,1)S(1)}, bf16[16,2880]{1,0:T(8,128)(2,1)S(1)}, u32[]{:S(2)}, u32[]{:S(2)}) collective-permute-start(bf16[16,2880]{1,0:T(8,128)(2,1)S(1)} %pad_maximum_fusion.12), channel_id=1, source_target_pairs={{0,8},{4,12},{8,0},{12,4},{16,24},{20,28},{24,16},{28,20},{1,9},{5... | collective-permute-start | bytes 276488 | tf_op jit(solution)/shard_map/ppermute | solution.py:189
  41.2 5.3 %collective-permute-start.17 = (bf16[64,2880]{1,0:T(8,128)(2,1)S(1)}, bf16[64,2880]{1,0:T(8,128)(2,1)S(1)}, u32[]{:S(2)}, u32[]{:S(2)}) collective-permute-start(bf16[64,2880]{1,0:T(8,128)(2,1)S(1)} %constant_dynamic-update-slice_fusion), channel_id=1, source_target_pairs={{0,4},{4,0},{8,12},{12,8},{16,20},{20,16},{24,28},{28,24},{1,5},{5... | collective-permute-start | bytes 1105928 | tf_op jit(solution)/shard_map/ppermute | solution.py:192
  41.3 5.2 %collective-permute-start.11 = (bf16[16,2880]{1,0:T(8,128)(2,1)S(1)}, bf16[16,2880]{1,0:T(8,128)(2,1)S(1)}, u32[]{:S(2)}, u32[]{:S(2)}) collective-permute-start(bf16[16,2880]{1,0:T(8,128)(2,1)S(1)} %pad_maximum_fusion.9), channel_id=1, source_target_pairs={{0,8},{4,12},{8,0},{12,4},{16,24},{20,28},{24,16},{28,20},{1,9},{5... | collective-permute-start | bytes 276488 | tf_op jit(solution)/shard_map/ppermute | solution.py:189
  46.9 6.0 %collective-permute-start.18 = (bf16[32,720]{1,0:T(8,128)(2,1)S(1)}, bf16[32,720]{1,0:T(8,128)(2,1)S(1)}, u32[]{:S(2)}, u32[]{:S(2)}) collective-permute-start(bf16[32,720]{1,0:T(8,128)(2,1)S(1)} %get-tuple-element.50), channel_id=1, source_target_pairs={{0,3},{1,2},{2,1},{3,0},{4,7},{5,6},{6,5},{7,4},{8,11},{9,10},{10,... | collective-permute-start | bytes 138248 | tf_op jit(solution)/shard_map/ppermute | solution.py:180
  49.6 5.0 %collective-permute-start.19 = (bf16[32,720]{1,0:T(8,128)(2,1)S(1)}, bf16[32,720]{1,0:T(8,128)(2,1)S(1)}, u32[]{:S(2)}, u32[]{:S(2)}) collective-permute-start(bf16[32,720]{1,0:T(8,128)(2,1)S(1)} %get-tuple-element.51), channel_id=1, source_target_pairs={{0,2},{1,3},{2,0},{3,1},{4,6},{5,7},{6,4},{7,5},{8,10},{9,11},{10,... | collective-permute-start | bytes 138248 | tf_op jit(solution)/shard_map/ppermute | solution.py:180
  49.6 5.1 %collective-permute-start.20 = (bf16[32,720]{1,0:T(8,128)(2,1)S(1)}, bf16[32,720]{1,0:T(8,128)(2,1)S(1)}, u32[]{:S(2)}, u32[]{:S(2)}) collective-permute-start(bf16[32,720]{1,0:T(8,128)(2,1)S(1)} %get-tuple-element.52), channel_id=1, source_target_pairs={{0,1},{1,0},{2,3},{3,2},{4,5},{5,4},{6,7},{7,6},{8,9},{9,8},{10,11... | collective-permute-start | bytes 138248 | tf_op jit(solution)/shard_map/ppermute | solution.py:180
